TPU v7x, 512 devices: a whole 4x4x16 slice. The times are simulated.
512 devices in a mesh: ctx: 32 (over z, core), tp: 16 (over x, y).
Axes of the slice: x: 4, y: 4, z: 16, core: 2. Of those that a mesh axis runs over, the one named last changes fastest.
Arguments:
- queries: bfloat16 [8192, 8192], P('ctx', 'tp'), may hold values from -6 to 6
- keys: bfloat16 [8192, 8192], P('ctx', 'tp'), may hold values from -0.0625 to 0.0625
- values: bfloat16 [8192, 8192], P('ctx', 'tp'), may hold values from -6 to 6
- log_keep: float32 [64, 8192], P('tp', 'ctx'), may hold values from -1 to 0, as said below
- state_in: float32 [64, 128, 128], P('tp'), may hold values from -6 to 6
- norm_gain: float32 [8192], P('tp'), may hold values from 0.1 to 1.9
- out_weight: bfloat16 [8192, 6144], P('tp', 'ctx'), may hold values from -0.125 to 0.125
Outputs:
- normed: bfloat16 [8192, 8192], P('ctx', 'tp')
- state_out: float32 [64, 128, 128], P('tp', 'ctx')
- layer_out: bfloat16 [8192, 6144], P('ctx', 'tp')
Inputs may be any that keep to these rules, and one draw needn't show every extreme that they name: `log_keep`: every entry is a logarithm of a keep factor, so at most 0.
All inputs are finite; a program needn't handle non-finite values.
Results may differ from a plain program's by a relative error of at most 0.014.
Values may be sent and summed in bfloat16 or wider, within the bound.
No kernel may reach another device: no remote copies, remote signals or barrier semaphores. Data moves between devices by JAX's collectives and lax.ppermute only.
A program may use at most 64 MiB of HBM per device.

v0:
```python
import jax
import jax.numpy as jnp
from jax import lax
from jax.sharding import PartitionSpec as P

H = 64
DH = 128
SPAN = 256


HIGH = lax.Precision.HIGHEST
EPSILON = 1e-06


def shifted(x, axis, by):
    peers = lax.axis_size(axis)
    pairs = [(i, i + by) for i in range(peers) if 0 <= i + by < peers]
    return lax.ppermute(x, axis, pairs)


def broadcast(x, axis, root):
    mine = lax.axis_index(axis) == root
    return lax.psum(jnp.where(mine, x, jnp.zeros_like(x)), axis)


def join_states(earlier, later):
    log_early, state_early = earlier
    log_late, state_late = later
    return (log_early + log_late, jnp.exp(log_late)[:, None, None] * state_early + state_late)


def close_chain(prev_log, prev_state, own_log, own_state, state_in):
    last_log, last_state = join_states((prev_log, prev_state), (own_log, own_state))
    return jnp.exp(last_log)[:, None, None] * state_in + last_state


def per_device(queries, keys, values, log_keep, state_in, norm_gain, out_weight):
    tokens_here = queries.shape[0]
    heads = log_keep.shape[0]
    width = state_in.shape[1]
    blocks = tokens_here // SPAN
    q_blocks = queries.reshape(blocks, SPAN, heads, width)
    k_blocks = keys.reshape(blocks, SPAN, heads, width)
    v_blocks = values.reshape(blocks, SPAN, heads, width)
    within = jnp.cumsum(log_keep.reshape(heads, blocks, SPAN), axis=2)
    causal = jnp.tril(jnp.ones((SPAN, SPAN), dtype=bool))
    spread = within[:, :, :, None] - within[:, :, None, :]
    decay = jnp.where(causal, jnp.exp(jnp.minimum(spread, 0.0)), 0.0)
    scores = jnp.einsum("cshd,cthd->hcst", q_blocks, k_blocks, preferred_element_type=jnp.float32)
    weights = (scores * decay).astype(jnp.bfloat16)
    intra = jnp.einsum("hcst,cthd->cshd", weights, v_blocks, preferred_element_type=jnp.float32)
    block_log = within[:, :, -1]
    key_factor = jnp.exp(block_log[:, :, None] - within).transpose(1, 2, 0)
    keys_decayed = (k_blocks * key_factor[:, :, :, None]).astype(jnp.bfloat16)
    increments = jnp.einsum(
        "cshd,cshe->chde", keys_decayed, v_blocks, preferred_element_type=jnp.float32
    )
    running = jnp.cumsum(block_log, axis=1)
    preceding_blocks = running - block_log
    order = jnp.arange(blocks)
    earlier_mask = order[None, :] < order[:, None]
    relative = preceding_blocks[:, :, None] - running[:, None, :]
    mixing = jnp.where(earlier_mask[None], jnp.exp(jnp.minimum(relative, 0.0)), 0.0)
    local_prefix = jnp.einsum("hcx,xhde->chde", mixing, increments, precision=HIGH)
    own_log = running[:, -1]
    own_state = jnp.einsum(
        "hc,chde->hde", jnp.exp(own_log[:, None] - running), increments, precision=HIGH
    )
    sequence_parts = lax.axis_size("ctx")
    zero_log = jnp.zeros_like(own_log)
    zero_state = jnp.zeros_like(own_state)

    def cycle_step(turn, carry):
        passed = join_states(carry, (own_log, own_state))
        return shifted((passed[0], passed[1]), "ctx", 1)

    prev_log, prev_state = lax.fori_loop(0, sequence_parts - 1, cycle_step, (zero_log, zero_state))
    closing = close_chain(prev_log, prev_state, own_log, own_state, state_in)
    shared_final = broadcast(closing, "ctx", sequence_parts - 1)
    share_rows = width // sequence_parts
    row_start = lax.axis_index("ctx") * share_rows
    final_share = lax.dynamic_slice_in_dim(shared_final, row_start, share_rows, 1)
    incoming_state = jnp.exp(prev_log)[:, None, None] * state_in + prev_state
    starts = jnp.exp(preceding_blocks).T[:, :, None, None] * incoming_state[None] + local_prefix
    starts_low = starts.astype(jnp.bfloat16)
    inter = jnp.einsum("cshd,chde->cshe", q_blocks, starts_low, preferred_element_type=jnp.float32)
    inter = inter * jnp.exp(within).transpose(1, 2, 0)[:, :, :, None]
    attended = (intra + inter).reshape(tokens_here, heads * width)
    squares = lax.psum(jnp.sum(attended * attended, axis=1), "tp")
    scale = lax.rsqrt(squares / (H * DH) + EPSILON)
    normed = (attended * scale[:, None] * norm_gain).astype(jnp.bfloat16)
    partials = jnp.dot(
        normed,
        lax.all_gather(out_weight, "ctx", axis=1, tiled=True),
        preferred_element_type=jnp.float32,
    )
    layer_out = lax.psum_scatter(
        partials.astype(jnp.bfloat16), "tp", scatter_dimension=1, tiled=True
    )
    return (normed, final_share, layer_out)


def solution(mesh):
    return jax.shard_map(
        per_device,
        mesh=mesh,
        in_specs=(
            P("ctx", "tp"),
            P("ctx", "tp"),
            P("ctx", "tp"),
            P("tp", "ctx"),
            P("tp", None, None),
            P("tp"),
            P("tp", "ctx"),
        ),
        out_specs=(P("ctx", "tp"), P("tp", "ctx", None), P("ctx", "tp")),
        check_vma=False,
    )
```

profile of v0, /device:TPU:1, one launch (start us, length us, event | category | flops | bytes accessed | tf_op | source)
XLA Modules:
  0.0 631.3 jit_solution(6297971191016926080)
XLA Ops:
  12.8 289.4 %while.13 = (s32[]{:T(128)}, f32[4]{0:T(128)S(1)}, f32[4,128,128]{2,1,0:T(8,128)S(1)}, f32[4]{0:T(128)S(1)}, f32[4,1,1]{0,2,1:T(1,128)S(1)}, /*index=5*/f32[4,128,128]{2,1,0:T(8,128)S(1)}, s32[]{:T(128)}) while((s32[]{:T(128)}, f32[4]{0:T(128)S(1)}, f32[4,128,128]{2,1,0:T(8,128)S(1)}, f32[4]{0:T(128)S(1)}, f32[4,1,1]{0,2,1:T(1,128)S(1)}, ...), condition=%wide.region_3.4_spmd, body=%wide.region_2.3_spmd.sunk | while | flops 131078 | bytes 1835293 | solution.py:77
  12.9 4.9 collective-permute-start.1
  19.8 3.2 collective-permute-done
  23.1 2.6 collective-permute-start.1
  29.1 4.4 collective-permute-start.1
  37.4 4.4 collective-permute-start.1
  41.8 2.9 collective-permute-start
  44.7 5.2 collective-permute-done
  50.1 4.5 collective-permute-start.1
  56.5 5.9 collective-permute-done
  62.4 4.4 collective-permute-start.1
  68.8 6.1 collective-permute-done
  74.9 4.4 collective-permute-start.1
  81.3 3.2 collective-permute-done
  84.6 4.4 collective-permute-start.1
  92.9 4.4 collective-permute-start.1
  97.3 3.8 collective-permute-start
  102.0 5.9 collective-permute-start.1
  111.4 5.7 collective-permute-start.1
  120.4 5.7 collective-permute-start.1
  129.5 5.7 collective-permute-start.1
  135.2 2.5 collective-permute-start
  138.6 5.7 collective-permute-start.1
  144.3 2.5 collective-permute-start
  147.7 5.7 collective-permute-start.1
  153.4 2.5 collective-permute-start
  156.8 5.7 collective-permute-start.1
  162.5 2.5 collective-permute-start
  165.9 5.7 collective-permute-start.1
  175.0 5.7 collective-permute-start.1
  184.1 5.7 collective-permute-start.1
  193.2 5.7 collective-permute-start.1
  202.3 5.7 collective-permute-start.1
  211.4 5.7 collective-permute-start.1
  220.5 5.7 collective-permute-start.1
  229.5 5.7 collective-permute-start.1
  238.6 5.7 collective-permute-start.1
  247.7 5.7 collective-permute-start.1
  256.8 5.7 collective-permute-start.1
  265.9 5.7 collective-permute-start.1
  275.0 5.7 collective-permute-start.1
  284.1 5.7 collective-permute-start.1
  293.2 5.7 collective-permute-start.1
  304.5 36.2 %psum.14 = f32[256]{0:T(256)S(1)} all-reduce(f32[256]{0:T(256)S(1)} %get-tuple-element.79), channel_id=1, replica_groups=mesh['ctx'=32,'tp'=16] {'tp'}, use_global_device_ids=true, to_apply=%region_5.6 | all-reduce | flops 256 | bytes 2048 | tf_op jit(solution)/shard_map/psum | solution.py:89
  341.5 4.7 convolution_convert_fusion
  346.3 2.8 copy.38
  349.1 179.5 %all-reduce.2.cloned.1.call-done = f32[4,128,128]{2,1,0:T(8,128)} async-done(((f32[4,128,128]{2,1,0:T(8,128)}), f32[4,128,128]{2,1,0:T(8,128)}) %all-reduce.2.cloned.1.call-update) | async-done | bytes 262160 | tf_op jit(solution)/shard_map/psum | solution.py:23
  529.9 93.1 %reduce-scatter.4.cloned.1.call-done = bf16[384,256]{1,0:T(8,128)(2,1)} async-done(((bf16[6144,256]{1,0:T(8,128)(2,1)}), bf16[384,256]{1,0:T(8,128)(2,1)}) %reduce-scatter.4.cloned.1.call-update) | async-done | bytes 196624
  (189 shorter events, 96.6 us)
Async XLA Ops:
  7.2 334.3 %all-gather.2.cloned.1.call-start = ((), (), s32[]{:S(2)}) async-start(), calls=%async_computation.2 | async-start | bytes 6488064 | tf_op jit(solution)/shard_map/all_gather | solution.py:94
  7.9 520.6 %all-reduce.2.cloned.1.call-start = ((), (), s32[]{:S(2)}) async-start(), calls=%async_computation.1 | async-start | bytes 524288 | tf_op jit(solution)/shard_map/psum | solution.py:23
  12.9 10.1 %collective-permute-start.1 = (f32[4,128,128]{2,1,0:T(8,128)S(1)}, f32[4,128,128]{2,1,0:T(8,128)S(1)}, u32[]{:S(2)}, u32[]{:S(2)}) collective-permute-start(f32[4,128,128]{2,1,0:T(8,128)S(1)} %multiply_add_fusion.2), channel_id=1, source_target_pairs={{0,16},{16,32},{32,48},{48,64},{64,80},{80,96},{96,112},{112,128},... | collective-permute-start | bytes 786440 | tf_op jit(solution)/shard_map/while/body/eval_jaxpr/ppermute | solution.py:18
  17.8 5.2 collective-permute-start
  23.1 6.0 collective-permute-start.1
  25.7 3.3 collective-permute-start
  29.1 8.1 %collective-permute-start.1 = (f32[4,128,128]{2,1,0:T(8,128)S(1)}, f32[4,128,128]{2,1,0:T(8,128)S(1)}, u32[]{:S(2)}, u32[]{:S(2)}) collective-permute-start(f32[4,128,128]{2,1,0:T(8,128)S(1)} %multiply_add_fusion.2), channel_id=1, source_target_pairs={{0,16},{16,32},{32,48},{48,64},{64,80},{80,96},{96,112},{112,128},... | collective-permute-start | bytes 786440 | tf_op jit(solution)/shard_map/while/body/eval_jaxpr/ppermute | solution.py:18
  33.6 3.7 collective-permute-start
  37.4 12.6 %collective-permute-start.1 = (f32[4,128,128]{2,1,0:T(8,128)S(1)}, f32[4,128,128]{2,1,0:T(8,128)S(1)}, u32[]{:S(2)}, u32[]{:S(2)}) collective-permute-start(f32[4,128,128]{2,1,0:T(8,128)S(1)} %multiply_add_fusion.2), channel_id=1, source_target_pairs={{0,16},{16,32},{32,48},{48,64},{64,80},{80,96},{96,112},{112,128},... | collective-permute-start | bytes 786440 | tf_op jit(solution)/shard_map/while/body/eval_jaxpr/ppermute | solution.py:18
  41.8 8.1 %collective-permute-start = (f32[4]{0:T(128)S(1)}, f32[4]{0:T(128)S(1)}, u32[]{:S(2)}, u32[]{:S(2)}) collective-permute-start(f32[4]{0:T(128)S(1)} %add.76), channel_id=1, source_target_pairs={{0,16},{16,32},{32,48},{48,64},{64,80},{80,96},{96,112},{112,128},... | collective-permute-start | bytes 56 | tf_op jit(solution)/shard_map/while/body/eval_jaxpr/ppermute | solution.py:18
  50.1 12.3 %collective-permute-start.1 = (f32[4,128,128]{2,1,0:T(8,128)S(1)}, f32[4,128,128]{2,1,0:T(8,128)S(1)}, u32[]{:S(2)}, u32[]{:S(2)}) collective-permute-start(f32[4,128,128]{2,1,0:T(8,128)S(1)} %multiply_add_fusion.2), channel_id=1, source_target_pairs={{0,16},{16,32},{32,48},{48,64},{64,80},{80,96},{96,112},{112,128},... | collective-permute-start | bytes 786440 | tf_op jit(solution)/shard_map/while/body/eval_jaxpr/ppermute | solution.py:18
  54.5 7.8 %collective-permute-start = (f32[4]{0:T(128)S(1)}, f32[4]{0:T(128)S(1)}, u32[]{:S(2)}, u32[]{:S(2)}) collective-permute-start(f32[4]{0:T(128)S(1)} %add.76), channel_id=1, source_target_pairs={{0,16},{16,32},{32,48},{48,64},{64,80},{80,96},{96,112},{112,128},... | collective-permute-start | bytes 56 | tf_op jit(solution)/shard_map/while/body/eval_jaxpr/ppermute | solution.py:18
  62.4 12.4 %collective-permute-start.1 = (f32[4,128,128]{2,1,0:T(8,128)S(1)}, f32[4,128,128]{2,1,0:T(8,128)S(1)}, u32[]{:S(2)}, u32[]{:S(2)}) collective-permute-start(f32[4,128,128]{2,1,0:T(8,128)S(1)} %multiply_add_fusion.2), channel_id=1, source_target_pairs={{0,16},{16,32},{32,48},{48,64},{64,80},{80,96},{96,112},{112,128},... | collective-permute-start | bytes 786440 | tf_op jit(solution)/shard_map/while/body/eval_jaxpr/ppermute | solution.py:18
  66.8 8.0 %collective-permute-start = (f32[4]{0:T(128)S(1)}, f32[4]{0:T(128)S(1)}, u32[]{:S(2)}, u32[]{:S(2)}) collective-permute-start(f32[4]{0:T(128)S(1)} %add.76), channel_id=1, source_target_pairs={{0,16},{16,32},{32,48},{48,64},{64,80},{80,96},{96,112},{112,128},... | collective-permute-start | bytes 56 | tf_op jit(solution)/shard_map/while/body/eval_jaxpr/ppermute | solution.py:18
  74.9 9.5 %collective-permute-start.1 = (f32[4,128,128]{2,1,0:T(8,128)S(1)}, f32[4,128,128]{2,1,0:T(8,128)S(1)}, u32[]{:S(2)}, u32[]{:S(2)}) collective-permute-start(f32[4,128,128]{2,1,0:T(8,128)S(1)} %multiply_add_fusion.2), channel_id=1, source_target_pairs={{0,16},{16,32},{32,48},{48,64},{64,80},{80,96},{96,112},{112,128},... | collective-permute-start | bytes 786440 | tf_op jit(solution)/shard_map/while/body/eval_jaxpr/ppermute | solution.py:18
  79.3 5.1 collective-permute-start
  84.6 8.2 %collective-permute-start.1 = (f32[4,128,128]{2,1,0:T(8,128)S(1)}, f32[4,128,128]{2,1,0:T(8,128)S(1)}, u32[]{:S(2)}, u32[]{:S(2)}) collective-permute-start(f32[4,128,128]{2,1,0:T(8,128)S(1)} %multiply_add_fusion.2), channel_id=1, source_target_pairs={{0,16},{16,32},{32,48},{48,64},{64,80},{80,96},{96,112},{112,128},... | collective-permute-start | bytes 786440 | tf_op jit(solution)/shard_map/while/body/eval_jaxpr/ppermute | solution.py:18
  89.0 3.7 collective-permute-start
  92.9 9.0 %collective-permute-start.1 = (f32[4,128,128]{2,1,0:T(8,128)S(1)}, f32[4,128,128]{2,1,0:T(8,128)S(1)}, u32[]{:S(2)}, u32[]{:S(2)}) collective-permute-start(f32[4,128,128]{2,1,0:T(8,128)S(1)} %multiply_add_fusion.2), channel_id=1, source_target_pairs={{0,16},{16,32},{32,48},{48,64},{64,80},{80,96},{96,112},{112,128},... | collective-permute-start | bytes 786440 | tf_op jit(solution)/shard_map/while/body/eval_jaxpr/ppermute | solution.py:18
  97.3 4.5 collective-permute-start
  102.0 9.3 %collective-permute-start.1 = (f32[4,128,128]{2,1,0:T(8,128)S(1)}, f32[4,128,128]{2,1,0:T(8,128)S(1)}, u32[]{:S(2)}, u32[]{:S(2)}) collective-permute-start(f32[4,128,128]{2,1,0:T(8,128)S(1)} %multiply_add_fusion.2), channel_id=1, source_target_pairs={{0,16},{16,32},{32,48},{48,64},{64,80},{80,96},{96,112},{112,128},... | collective-permute-start | bytes 786440 | tf_op jit(solution)/shard_map/while/body/eval_jaxpr/ppermute | solution.py:18
  111.4 9.0 %collective-permute-start.1 = (f32[4,128,128]{2,1,0:T(8,128)S(1)}, f32[4,128,128]{2,1,0:T(8,128)S(1)}, u32[]{:S(2)}, u32[]{:S(2)}) collective-permute-start(f32[4,128,128]{2,1,0:T(8,128)S(1)} %multiply_add_fusion.2), channel_id=1, source_target_pairs={{0,16},{16,32},{32,48},{48,64},{64,80},{80,96},{96,112},{112,128},... | collective-permute-start | bytes 786440 | tf_op jit(solution)/shard_map/while/body/eval_jaxpr/ppermute | solution.py:18
  120.4 9.0 %collective-permute-start.1 = (f32[4,128,128]{2,1,0:T(8,128)S(1)}, f32[4,128,128]{2,1,0:T(8,128)S(1)}, u32[]{:S(2)}, u32[]{:S(2)}) collective-permute-start(f32[4,128,128]{2,1,0:T(8,128)S(1)} %multiply_add_fusion.2), channel_id=1, source_target_pairs={{0,16},{16,32},{32,48},{48,64},{64,80},{80,96},{96,112},{112,128},... | collective-permute-start | bytes 786440 | tf_op jit(solution)/shard_map/while/body/eval_jaxpr/ppermute | solution.py:18
  129.5 9.0 %collective-permute-start.1 = (f32[4,128,128]{2,1,0:T(8,128)S(1)}, f32[4,128,128]{2,1,0:T(8,128)S(1)}, u32[]{:S(2)}, u32[]{:S(2)}) collective-permute-start(f32[4,128,128]{2,1,0:T(8,128)S(1)} %multiply_add_fusion.2), channel_id=1, source_target_pairs={{0,16},{16,32},{32,48},{48,64},{64,80},{80,96},{96,112},{112,128},... | collective-permute-start | bytes 786440 | tf_op jit(solution)/shard_map/while/body/eval_jaxpr/ppermute | solution.py:18
  135.2 3.3 collective-permute-start
  138.6 9.0 %collective-permute-start.1 = (f32[4,128,128]{2,1,0:T(8,128)S(1)}, f32[4,128,128]{2,1,0:T(8,128)S(1)}, u32[]{:S(2)}, u32[]{:S(2)}) collective-permute-start(f32[4,128,128]{2,1,0:T(8,128)S(1)} %multiply_add_fusion.2), channel_id=1, source_target_pairs={{0,16},{16,32},{32,48},{48,64},{64,80},{80,96},{96,112},{112,128},... | collective-permute-start | bytes 786440 | tf_op jit(solution)/shard_map/while/body/eval_jaxpr/ppermute | solution.py:18
  144.3 3.3 collective-permute-start
  147.7 9.0 %collective-permute-start.1 = (f32[4,128,128]{2,1,0:T(8,128)S(1)}, f32[4,128,128]{2,1,0:T(8,128)S(1)}, u32[]{:S(2)}, u32[]{:S(2)}) collective-permute-start(f32[4,128,128]{2,1,0:T(8,128)S(1)} %multiply_add_fusion.2), channel_id=1, source_target_pairs={{0,16},{16,32},{32,48},{48,64},{64,80},{80,96},{96,112},{112,128},... | collective-permute-start | bytes 786440 | tf_op jit(solution)/shard_map/while/body/eval_jaxpr/ppermute | solution.py:18
  153.4 3.3 collective-permute-start
  156.8 9.0 %collective-permute-start.1 = (f32[4,128,128]{2,1,0:T(8,128)S(1)}, f32[4,128,128]{2,1,0:T(8,128)S(1)}, u32[]{:S(2)}, u32[]{:S(2)}) collective-permute-start(f32[4,128,128]{2,1,0:T(8,128)S(1)} %multiply_add_fusion.2), channel_id=1, source_target_pairs={{0,16},{16,32},{32,48},{48,64},{64,80},{80,96},{96,112},{112,128},... | collective-permute-start | bytes 786440 | tf_op jit(solution)/shard_map/while/body/eval_jaxpr/ppermute | solution.py:18
  162.5 3.3 collective-permute-start
  165.9 9.0 %collective-permute-start.1 = (f32[4,128,128]{2,1,0:T(8,128)S(1)}, f32[4,128,128]{2,1,0:T(8,128)S(1)}, u32[]{:S(2)}, u32[]{:S(2)}) collective-permute-start(f32[4,128,128]{2,1,0:T(8,128)S(1)} %multiply_add_fusion.2), channel_id=1, source_target_pairs={{0,16},{16,32},{32,48},{48,64},{64,80},{80,96},{96,112},{112,128},... | collective-permute-start | bytes 786440 | tf_op jit(solution)/shard_map/while/body/eval_jaxpr/ppermute | solution.py:18
  171.6 3.3 collective-permute-start
  175.0 9.0 %collective-permute-start.1 = (f32[4,128,128]{2,1,0:T(8,128)S(1)}, f32[4,128,128]{2,1,0:T(8,128)S(1)}, u32[]{:S(2)}, u32[]{:S(2)}) collective-permute-start(f32[4,128,128]{2,1,0:T(8,128)S(1)} %multiply_add_fusion.2), channel_id=1, source_target_pairs={{0,16},{16,32},{32,48},{48,64},{64,80},{80,96},{96,112},{112,128},... | collective-permute-start | bytes 786440 | tf_op jit(solution)/shard_map/while/body/eval_jaxpr/ppermute | solution.py:18
  184.1 9.0 %collective-permute-start.1 = (f32[4,128,128]{2,1,0:T(8,128)S(1)}, f32[4,128,128]{2,1,0:T(8,128)S(1)}, u32[]{:S(2)}, u32[]{:S(2)}) collective-permute-start(f32[4,128,128]{2,1,0:T(8,128)S(1)} %multiply_add_fusion.2), channel_id=1, source_target_pairs={{0,16},{16,32},{32,48},{48,64},{64,80},{80,96},{96,112},{112,128},... | collective-permute-start | bytes 786440 | tf_op jit(solution)/shard_map/while/body/eval_jaxpr/ppermute | solution.py:18
  193.2 9.0 %collective-permute-start.1 = (f32[4,128,128]{2,1,0:T(8,128)S(1)}, f32[4,128,128]{2,1,0:T(8,128)S(1)}, u32[]{:S(2)}, u32[]{:S(2)}) collective-permute-start(f32[4,128,128]{2,1,0:T(8,128)S(1)} %multiply_add_fusion.2), channel_id=1, source_target_pairs={{0,16},{16,32},{32,48},{48,64},{64,80},{80,96},{96,112},{112,128},... | collective-permute-start | bytes 786440 | tf_op jit(solution)/shard_map/while/body/eval_jaxpr/ppermute | solution.py:18
  202.3 9.0 %collective-permute-start.1 = (f32[4,128,128]{2,1,0:T(8,128)S(1)}, f32[4,128,128]{2,1,0:T(8,128)S(1)}, u32[]{:S(2)}, u32[]{:S(2)}) collective-permute-start(f32[4,128,128]{2,1,0:T(8,128)S(1)} %multiply_add_fusion.2), channel_id=1, source_target_pairs={{0,16},{16,32},{32,48},{48,64},{64,80},{80,96},{96,112},{112,128},... | collective-permute-start | bytes 786440 | tf_op jit(solution)/shard_map/while/body/eval_jaxpr/ppermute | solution.py:18
  211.4 9.0 %collective-permute-start.1 = (f32[4,128,128]{2,1,0:T(8,128)S(1)}, f32[4,128,128]{2,1,0:T(8,128)S(1)}, u32[]{:S(2)}, u32[]{:S(2)}) collective-permute-start(f32[4,128,128]{2,1,0:T(8,128)S(1)} %multiply_add_fusion.2), channel_id=1, source_target_pairs={{0,16},{16,32},{32,48},{48,64},{64,80},{80,96},{96,112},{112,128},... | collective-permute-start | bytes 786440 | tf_op jit(solution)/shard_map/while/body/eval_jaxpr/ppermute | solution.py:18
  220.5 9.0 %collective-permute-start.1 = (f32[4,128,128]{2,1,0:T(8,128)S(1)}, f32[4,128,128]{2,1,0:T(8,128)S(1)}, u32[]{:S(2)}, u32[]{:S(2)}) collective-permute-start(f32[4,128,128]{2,1,0:T(8,128)S(1)} %multiply_add_fusion.2), channel_id=1, source_target_pairs={{0,16},{16,32},{32,48},{48,64},{64,80},{80,96},{96,112},{112,128},... | collective-permute-start | bytes 786440 | tf_op jit(solution)/shard_map/while/body/eval_jaxpr/ppermute | solution.py:18
  229.5 9.0 %collective-permute-start.1 = (f32[4,128,128]{2,1,0:T(8,128)S(1)}, f32[4,128,128]{2,1,0:T(8,128)S(1)}, u32[]{:S(2)}, u32[]{:S(2)}) collective-permute-start(f32[4,128,128]{2,1,0:T(8,128)S(1)} %multiply_add_fusion.2), channel_id=1, source_target_pairs={{0,16},{16,32},{32,48},{48,64},{64,80},{80,96},{96,112},{112,128},... | collective-permute-start | bytes 786440 | tf_op jit(solution)/shard_map/while/body/eval_jaxpr/ppermute | solution.py:18
  238.6 9.0 %collective-permute-start.1 = (f32[4,128,128]{2,1,0:T(8,128)S(1)}, f32[4,128,128]{2,1,0:T(8,128)S(1)}, u32[]{:S(2)}, u32[]{:S(2)}) collective-permute-start(f32[4,128,128]{2,1,0:T(8,128)S(1)} %multiply_add_fusion.2), channel_id=1, source_target_pairs={{0,16},{16,32},{32,48},{48,64},{64,80},{80,96},{96,112},{112,128},... | collective-permute-start | bytes 786440 | tf_op jit(solution)/shard_map/while/body/eval_jaxpr/ppermute | solution.py:18
  247.7 9.0 %collective-permute-start.1 = (f32[4,128,128]{2,1,0:T(8,128)S(1)}, f32[4,128,128]{2,1,0:T(8,128)S(1)}, u32[]{:S(2)}, u32[]{:S(2)}) collective-permute-start(f32[4,128,128]{2,1,0:T(8,128)S(1)} %multiply_add_fusion.2), channel_id=1, source_target_pairs={{0,16},{16,32},{32,48},{48,64},{64,80},{80,96},{96,112},{112,128},... | collective-permute-start | bytes 786440 | tf_op jit(solution)/shard_map/while/body/eval_jaxpr/ppermute | solution.py:18
  256.8 9.0 %collective-permute-start.1 = (f32[4,128,128]{2,1,0:T(8,128)S(1)}, f32[4,128,128]{2,1,0:T(8,128)S(1)}, u32[]{:S(2)}, u32[]{:S(2)}) collective-permute-start(f32[4,128,128]{2,1,0:T(8,128)S(1)} %multiply_add_fusion.2), channel_id=1, source_target_pairs={{0,16},{16,32},{32,48},{48,64},{64,80},{80,96},{96,112},{112,128},... | collective-permute-start | bytes 786440 | tf_op jit(solution)/shard_map/while/body/eval_jaxpr/ppermute | solution.py:18
  265.9 9.0 %collective-permute-start.1 = (f32[4,128,128]{2,1,0:T(8,128)S(1)}, f32[4,128,128]{2,1,0:T(8,128)S(1)}, u32[]{:S(2)}, u32[]{:S(2)}) collective-permute-start(f32[4,128,128]{2,1,0:T(8,128)S(1)} %multiply_add_fusion.2), channel_id=1, source_target_pairs={{0,16},{16,32},{32,48},{48,64},{64,80},{80,96},{96,112},{112,128},... | collective-permute-start | bytes 786440 | tf_op jit(solution)/shard_map/while/body/eval_jaxpr/ppermute | solution.py:18
  275.0 9.0 %collective-permute-start.1 = (f32[4,128,128]{2,1,0:T(8,128)S(1)}, f32[4,128,128]{2,1,0:T(8,128)S(1)}, u32[]{:S(2)}, u32[]{:S(2)}) collective-permute-start(f32[4,128,128]{2,1,0:T(8,128)S(1)} %multiply_add_fusion.2), channel_id=1, source_target_pairs={{0,16},{16,32},{32,48},{48,64},{64,80},{80,96},{96,112},{112,128},... | collective-permute-start | bytes 786440 | tf_op jit(solution)/shard_map/while/body/eval_jaxpr/ppermute | solution.py:18
  284.1 9.0 %collective-permute-start.1 = (f32[4,128,128]{2,1,0:T(8,128)S(1)}, f32[4,128,128]{2,1,0:T(8,128)S(1)}, u32[]{:S(2)}, u32[]{:S(2)}) collective-permute-start(f32[4,128,128]{2,1,0:T(8,128)S(1)} %multiply_add_fusion.2), channel_id=1, source_target_pairs={{0,16},{16,32},{32,48},{48,64},{64,80},{80,96},{96,112},{112,128},... | collective-permute-start | bytes 786440 | tf_op jit(solution)/shard_map/while/body/eval_jaxpr/ppermute | solution.py:18
  293.2 9.0 %collective-permute-start.1 = (f32[4,128,128]{2,1,0:T(8,128)S(1)}, f32[4,128,128]{2,1,0:T(8,128)S(1)}, u32[]{:S(2)}, u32[]{:S(2)}) collective-permute-start(f32[4,128,128]{2,1,0:T(8,128)S(1)} %multiply_add_fusion.2), channel_id=1, source_target_pairs={{0,16},{16,32},{32,48},{48,64},{64,80},{80,96},{96,112},{112,128},... | collective-permute-start | bytes 786440 | tf_op jit(solution)/shard_map/while/body/eval_jaxpr/ppermute | solution.py:18
  303.1 320.0 %reduce-scatter.4.cloned.1.call-start = ((), (), s32[]{:S(2)}) async-start(), calls=%async_computation.3 | async-start | bytes 3342336
  (21 other events, 1272.9 us)
Sparse Core Ops, SparseCore 0:
  10.1 83.9 all-gather.1
  303.2 225.3 all-reduce.1
  532.8 90.1 reduce-scatter.3
where the time goes:
time: 634 us; the launch traced here: 631 us
  waiting for transfers between devices  320 us (50%)
  starting transfers between devices  239 us (38%)
  blocking collectives  36.2 us (6%)
  between operations  13.9 us (2%)
  local copies, waits for them, and re-layouts  8.45 us (1%)
  matrix products  6.9 us (1%)
    ppermute x62, starting transfers between devices, shifted(): return lax.ppermute(x, axis, pairs)  239 us
    psum x1, waiting for transfers between devices, broadcast(): return lax.psum(jnp.where(mine, x, jnp.zeros_like(x)), axis)  179 us
    unnamed x4, waiting for transfers between devices  93.8 us
    ppermute x62, waiting for transfers between devices, shifted(): return lax.ppermute(x, axis, pairs)  46.7 us
    psum x1, blocking collectives, per_device(): squares = lax.psum(jnp.sum(attended * attended, axis=1), 'tp')  36.2 us
  transfers between devices with their start and end apart: 65, of which 33 were waited for; matrix products, arithmetic and copies ran while one was open for 3% of the time, Pallas kernels for 0%

commit v1 on v0

v1 whole, which is shorter than its diff:
```python
import jax
import jax.numpy as jnp
from jax import lax
from jax.sharding import Mesh, PartitionSpec as P

H = 64
DH = 128
EPSILON = 1e-06
CTX = ("za", "zb", "core")
TP = ("x", "y")
HIGH = lax.Precision.HIGHEST
BF16 = jnp.bfloat16
F32 = jnp.float32


def split3(x):
    hi = lax.reduce_precision(x, 8, 7)
    rest = x - hi
    mid = lax.reduce_precision(rest, 8, 7)
    low = rest - mid
    return jnp.stack([hi.astype(BF16), mid.astype(BF16), low.astype(BF16)])


def join3(parts):
    parts = parts.astype(F32)
    return parts[0] + (parts[1] + parts[2])


def with_rows(block, vector):
    width = block.shape[-1]
    flat = split3(vector).reshape(-1)
    tail = jnp.pad(flat, (0, 16 * width - flat.shape[0])).reshape(16, width)
    lead = block.shape[:-2]
    tail = jnp.broadcast_to(tail, lead + tail.shape)
    return jnp.concatenate([block, tail], axis=-2)


def rows_of(tail, n):
    count = tail.shape[0]
    flat = tail.reshape(count, -1)[:, : 3 * n].reshape(count, 3, n)
    return jnp.sum(join3(jnp.moveaxis(flat, 1, 0)), axis=0)


def per_device(queries, keys, values, log_keep, state_in, norm_gain, out_weight):
    tokens = queries.shape[0]
    heads = log_keep.shape[0]
    parts = lax.axis_size(CTX)
    rows = DH // parts
    nx, ny = lax.axis_size("x"), lax.axis_size("y")

    swap = [(a * nx + b, b * nx + a) for a in range(nx) for b in range(nx)]
    moved = lax.ppermute(out_weight.T, ("za", "x"), swap)
    gathered = lax.all_gather(moved, CTX, axis=0, tiled=True)
    cols = out_weight.shape[1] * parts // (nx * ny)
    gathered = gathered.reshape(nx, ny * cols, out_weight.shape[0])

    q = queries.reshape(tokens, heads, DH)
    k = keys.reshape(tokens, heads, DH)
    v = values.reshape(tokens, heads, DH)
    within = jnp.cumsum(log_keep, axis=1)
    own_log = within[:, -1]
    key_factor = jnp.exp(own_log[:, None] - within).T
    kdec = (k * key_factor[:, :, None]).astype(BF16)
    inc = jnp.einsum("shd,she->hde", kdec, v, preferred_element_type=F32)

    out = inc.astype(BF16).reshape(heads, parts, rows, DH).transpose(1, 0, 2, 3)
    logs = jnp.pad(split3(own_log), ((0, rows - 3), (0, DH - heads)))
    logs = jnp.broadcast_to(logs[None, None], (parts, 1, rows, DH))
    got = lax.all_to_all(jnp.concatenate([out, logs], axis=1), CTX, 0, 0, tiled=True)

    causal = jnp.tril(jnp.ones((tokens, tokens), dtype=bool))
    spread = within[:, :, None] - within[:, None, :]
    decay = jnp.where(causal, jnp.exp(jnp.minimum(spread, 0.0)), 0.0)
    scores = jnp.einsum("shd,thd->hst", q, k, preferred_element_type=F32)
    weights = (scores * decay).astype(BF16)
    intra = jnp.einsum("hst,thd->shd", weights, v, preferred_element_type=F32)

    incs = got[:, :heads].astype(F32)
    every = join3(jnp.moveaxis(got[:, heads, :3, :heads], 1, 0))
    upto = jnp.concatenate([jnp.zeros((1, heads), F32), jnp.cumsum(every, axis=0)])
    order = jnp.arange(parts)
    before = order[None, :] < jnp.arange(parts + 1)[:, None]
    gap = upto[:, None] - upto[None, 1:]
    mixing = jnp.where(before[:, :, None], jnp.exp(jnp.minimum(gap, 0.0)), 0.0)
    me = lax.axis_index(CTX)
    first = lax.dynamic_slice_in_dim(state_in, me * rows, rows, 1)
    states = jnp.einsum("cjh,jhrd->chrd", mixing, incs, precision=HIGH)
    states = states + jnp.exp(upto)[:, :, None, None] * first[None]
    final = states[parts]
    back = lax.all_to_all(states[:parts].astype(BF16), CTX, 0, 0, tiled=True)
    start = back.transpose(1, 0, 2, 3).reshape(heads, DH, DH)

    inter = jnp.einsum("shd,hde->she", q, start, preferred_element_type=F32)
    inter = inter * jnp.exp(within).T[:, :, None]
    attended = (intra + inter).reshape(tokens, heads * DH)
    squares = jnp.sum(attended * attended, axis=1)
    gained = attended * norm_gain

    message = with_rows(gained.astype(BF16), squares)
    message = jnp.broadcast_to(message[None], (nx,) + message.shape)
    acts = lax.all_to_all(message, "x", 0, 0, tiled=True)
    squares = rows_of(acts[:, tokens:], tokens)
    partial = sum(
        lax.dot_general(
            acts[i, :tokens], gathered[i], (((1,), (1,)), ((), ())), preferred_element_type=F32
        )
        for i in range(nx)
    )
    partial = partial.astype(BF16).reshape(tokens, ny, cols).transpose(1, 0, 2)
    shares = lax.all_to_all(with_rows(partial, squares), "y", 0, 0, tiled=True)
    squares = rows_of(shares[:, tokens:], tokens)
    scale = lax.rsqrt(squares / (H * DH) + EPSILON)[:, None]
    normed = (attended * scale * norm_gain).astype(BF16)
    layer_out = (jnp.sum(shares[:, :tokens].astype(F32), axis=0) * scale).astype(BF16)
    return (normed, final, layer_out)


def solution(mesh):
    fine = Mesh(mesh.devices.reshape(4, 4, 2, 4, 4), CTX + TP)
    return jax.shard_map(
        per_device,
        mesh=fine,
        in_specs=(
            P(CTX, TP),
            P(CTX, TP),
            P(CTX, TP),
            P(TP, CTX),
            P(TP, None, None),
            P(TP),
            P(TP, CTX),
        ),
        out_specs=(P(CTX, TP), P(TP, CTX, None), P(CTX, TP)),
        check_vma=False,
    )
```

time: 634 us -> 167 us (0.26)
  waiting for transfers between devices: 320 us -> 54.5 us
  starting transfers between devices: 239 us -> 58.9 us
  blocking collectives: 36.2 us -> 19.2 us
    ppermute x62 -> x1, starting transfers between devices: 239 us -> 1.72 us  [per_device(): moved = lax.ppermute(out_weight.T, ('za', 'x'), swap)]
    psum x1 -> x0, waiting for transfers between devices: 179 us -> none  [broadcast(): return lax.psum(jnp.where(mine, x, jnp.zeros_like(x)), axis)]
    unnamed x4 -> x1, waiting for transfers between devices: 93.8 us -> 0.02 us
    all_to_all x0 -> x3, starting transfers between devices: none -> 57.2 us  [the longest x1 48 us: per_device(): lax.all_to_all(jnp.concatenate([out, logs], axis=1), CTX, 0, 0, tiled=True)]
    all_to_all x0 -> x3, waiting for transfers between devices: none -> 47.5 us  [the longest x1 18 us: per_device(): lax.all_to_all(jnp.concatenate([out, logs], axis=1), CTX, 0, 0, tiled=True)]
    ppermute x62 -> x1, waiting for transfers between devices: 46.7 us -> 0.01 us  [per_device(): moved = lax.ppermute(out_weight.T, ('za', 'x'), swap)]
    psum x1 -> x0, blocking collectives: 36.2 us -> none  [per_device(): squares = lax.psum(jnp.sum(attended * attended, axis=1), 'tp')]
    all_to_all x0 -> x1, blocking collectives: none -> 19.2 us  [per_device(): acts = lax.all_to_all(message, 'x', 0, 0, tiled=True)]
  transfers between devices with their start and end apart: 65 -> 5, of which waited for: 33 -> 4; matrix products, arithmetic and copies ran while one was open for 3% -> 6% of each run, Pallas kernels for 0% -> 0%
where the time goes in v1:
time: 167 us; the launch traced here: 166 us
  starting transfers between devices  58.9 us (35%)
  waiting for transfers between devices  54.5 us (33%)
  blocking collectives  19.2 us (11%)
  between operations  14.4 us (9%)
  matrix products  8 us (5%)
  local copies, waits for them, and re-layouts  5.87 us (4%)
  other arithmetic  5.18 us (3%)
    all_to_all x1, starting transfers between devices, per_device(): lax.all_to_all(jnp.concatenate([out, logs], axis=1), CTX, 0, 0, tiled=True)  48 us
    all_to_all x1, blocking collectives, per_device(): acts = lax.all_to_all(message, 'x', 0, 0, tiled=True)  19.2 us
    all_to_all x1, waiting for transfers between devices, per_device(): lax.all_to_all(jnp.concatenate([out, logs], axis=1), CTX, 0, 0, tiled=True)  18 us
    all_to_all x1, waiting for transfers between devices, per_device(): back = lax.all_to_all(states[:parts].astype(BF16), CTX, 0, 0, tiled=True)  17.8 us
    all_to_all x1, waiting for transfers between devices, per_device(): shares = lax.all_to_all(with_rows(partial, squares), 'y', 0, 0, tiled=True)  11.7 us
    all_gather x1, waiting for transfers between devices, per_device(): gathered = lax.all_gather(moved, CTX, axis=0, tiled=True)  6.9 us
    dot_general x4, matrix products, per_device(): lax.dot_general(acts[i, :tokens], gathered[i], (((1,), (1,)), ((), ())),...  5.51 us
    all_to_all x1, starting transfers between devices, per_device(): back = lax.all_to_all(states[:parts].astype(BF16), CTX, 0, 0, tiled=True)  5.24 us
  transfers between devices with their start and end apart: 5, of which 4 were waited for; matrix products, arithmetic and copies ran while one was open for 6% of the time, Pallas kernels for 0%

profile of v1, /device:TPU:1, one launch (start us, length us, event | category | flops | bytes accessed | tf_op | source)
XLA Modules:
  0.0 166.0 jit_solution(13289621185079224274)
XLA Ops:
  7.2 0.0 copy-start
  7.2 0.0 all-gather.2.cloned.1.call-start
  7.2 1.7 %collective-permute-start = (bf16[192,512]{1,0:T(8,128)(2,1)}, bf16[192,512]{1,0:T(8,128)(2,1)S(1)}, u32[]{:S(2)}, u32[]{:S(2)}) collective-permute-start(bf16[192,512]{1,0:T(8,128)(2,1)} %bitcast.143), channel_id=1, source_target_pairs={{0,0},{4,128},{8,256},{12,384},{128,4},{132,132},{136,260},{140,38... | collective-permute-start | bytes 589832 | tf_op jit(solution)/shard_map/ppermute | solution.py:52
  8.9 0.7 copy-done.2
  9.6 0.0 all-gather.2.cloned.1.call-update
  9.6 0.7 reshape.243
  10.3 1.2 reduce-window.6
  11.6 0.1 slice.121
  11.6 0.1 copy.66
  11.8 0.1 copy.67
  11.9 0.1 add_bitcast_fusion
  12.0 0.1 slice.122
  12.0 0.1 copy.88
  12.1 1.1 copy.90
  13.2 0.1 exponential_bitcast_fusion
  13.3 1.2 convolution_convert_fusion
  14.5 0.0 copy-start.4
  14.6 0.8 pad_maximum_fusion.2
  15.4 48.0 %all-to-all-start = ((bf16[32,5,4,128]{3,2,1,0:T(4,128)(2,1)}), bf16[32,5,4,128]{3,2,1,0:T(4,128)(2,1)S(1)}, u32[]{:S(2)}, u32[]{:S(2)}) async-start(bf16[32,5,4,128]{3,2,1,0:T(4,128)(2,1)} %pad_maximum_fusion.2), calls=%async_computation | async-start | bytes 327680 | tf_op jit(solution)/shard_map/all_to_all | solution.py:69
  63.4 0.7 constant_dynamic-slice_fusion
  64.1 18.0 %all-to-all-done = bf16[32,5,4,128]{3,2,1,0:T(4,128)(2,1)S(1)} async-done(((bf16[32,5,4,128]{3,2,1,0:T(4,128)(2,1)}), bf16[32,5,4,128]{3,2,1,0:T(4,128)(2,1)S(1)}, u32[]{:S(2)}, u32[]{:S(2)}) %all-to-all-start) | async-done | bytes 163872 | tf_op jit(solution)/shard_map/all_to_all | solution.py:69
  82.2 0.1 reduce_window_sum.36
  82.2 0.1 copy.76
  82.4 0.1 fusion.62
  82.4 0.4 fusion.13
  82.9 0.7 copy.78
  83.6 5.2 %all-to-all-start.1 = ((bf16[32,4,4,128]{3,2,1,0:T(4,128)(2,1)}), bf16[32,4,4,128]{3,2,1,0:T(4,128)(2,1)S(1)}, u32[]{:S(2)}, u32[]{:S(2)}) async-start(bf16[32,4,4,128]{3,2,1,0:T(4,128)(2,1)} %copy.78), calls=%async_computation.1 | async-start | bytes 262144 | tf_op jit(solution)/shard_map/all_to_all | solution.py:90
  88.9 0.6 convolution_bitcast_fusion.1
  89.5 0.0 copy-start.3
  89.5 17.8 %all-to-all-done.1 = bf16[32,4,4,128]{3,2,1,0:T(4,128)(2,1)S(1)} async-done(((bf16[32,4,4,128]{3,2,1,0:T(4,128)(2,1)}), bf16[32,4,4,128]{3,2,1,0:T(4,128)(2,1)S(1)}, u32[]{:S(2)}, u32[]{:S(2)}) %all-to-all-start.1) | async-done | bytes 131104 | tf_op jit(solution)/shard_map/all_to_all | solution.py:90
  107.4 0.3 multiply_reduce_fusion
  107.7 0.2 copy.84
  108.1 0.1 broadcast_in_dim.27
  108.2 19.2 %all_to_all.20 = bf16[4,272,512]{2,1,0:T(8,128)(2,1)S(1)} all-to-all(bf16[4,272,512]{2,1,0:T(8,128)(2,1)S(1)} %broadcast_in_dim.27), channel_id=1, replica_groups=mesh['za'=4,'zb'=4,'core'=2,'x'=4,'y'=4] {'x'}, dimensions={0} | all-to-all | bytes 2228224 | tf_op jit(solution)/shard_map/all_to_all | solution.py:101
  127.3 0.1 copy.95
  127.5 6.9 %all-gather.2.cloned.1.call-done = bf16[6144,512]{1,0:T(8,128)(2,1)} async-done(((bf16[192,512]{1,0:T(8,128)(2,1)}), bf16[6144,512]{1,0:T(8,128)(2,1)}) %all-gather.2.cloned.1.call-update) | async-done | bytes 6291472 | tf_op jit(solution)/shard_map/all_gather | solution.py:53
  134.4 2.2 %fusion.3 = f32[256,1536]{1,0:T(8,128)S(1)} fusion(bf16[6144,512]{1,0:T(8,128)(2,1)} %all-gather.2.cloned.1.call-done, bf16[4,272,512]{2,1,0:T(8,128)(2,1)S(1)} %all_to_all.20), kind=kOutput, calls=%fused_computation.4 | convolution fusion | flops 402653184 | bytes 3407872 | tf_op jit(solution)/shard_map/dot_general | solution.py:104
  136.6 2.1 %fusion.5 = f32[256,1536]{1,0:T(8,128)S(1)} fusion(bf16[6144,512]{1,0:T(8,128)(2,1)} %all-gather.2.cloned.1.call-done, bf16[4,272,512]{2,1,0:T(8,128)(2,1)S(1)} %all_to_all.20), kind=kOutput, calls=%fused_computation.6 | convolution fusion | flops 402653184 | bytes 3407872 | tf_op jit(solution)/shard_map/dot_general | solution.py:104
  138.7 0.6 fusion.7
  139.4 0.6 fusion.2
  140.0 0.1 copy.125
  140.1 1.0 pad_maximum_fusion
  141.1 3.9 %all-to-all-start.3 = ((bf16[4,272,384]{2,1,0:T(8,128)(2,1)}), bf16[4,272,384]{2,1,0:T(8,128)(2,1)S(1)}, u32[]{:S(2)}, u32[]{:S(2)}) async-start(bf16[4,272,384]{2,1,0:T(8,128)(2,1)} %pad_maximum_fusion), calls=%async_computation.3 | async-start | bytes 1671168 | tf_op jit(solution)/shard_map/all_to_all | solution.py:110
  145.0 0.6 slice.147
  145.6 11.7 %all-to-all-done.3 = bf16[4,272,384]{2,1,0:T(8,128)(2,1)S(1)} async-done(((bf16[4,272,384]{2,1,0:T(8,128)(2,1)}), bf16[4,272,384]{2,1,0:T(8,128)(2,1)S(1)}, u32[]{:S(2)}, u32[]{:S(2)}) %all-to-all-start.3) | async-done | bytes 835616 | tf_op jit(solution)/shard_map/all_to_all | solution.py:110
  157.5 0.8 multiply_convert_fusion
  158.3 0.1 convert_reduce_fusion
  158.4 0.8 multiply_convert_fusion.3
  (44 shorter events, 0.6 us)
Async XLA Ops:
  7.2 81.7 %copy-start = (bf16[256,512]{1,0:T(8,128)(2,1)S(1)}, bf16[256,512]{1,0:T(8,128)(2,1)}, u32[]{:S(2)}) copy-start(bf16[256,512]{1,0:T(8,128)(2,1)} %param.7) | copy-start | bytes 786436
  7.2 127.3 %all-gather.2.cloned.1.call-start = ((), (), s32[]{:S(2)}) async-start(), calls=%async_computation.4 | async-start | bytes 6488064 | tf_op jit(solution)/shard_map/all_gather | solution.py:53
  7.2 1.7 %collective-permute-start = (bf16[192,512]{1,0:T(8,128)(2,1)}, bf16[192,512]{1,0:T(8,128)(2,1)S(1)}, u32[]{:S(2)}, u32[]{:S(2)}) collective-permute-start(bf16[192,512]{1,0:T(8,128)(2,1)} %bitcast.143), channel_id=1, source_target_pairs={{0,0},{4,128},{8,256},{12,384},{128,4},{132,132},{136,260},{140,38... | collective-permute-start | bytes 589832 | tf_op jit(solution)/shard_map/ppermute | solution.py:52
  8.9 0.7 copy-start.2
  14.5 74.4 %copy-start.4 = (bf16[256,512]{1,0:T(8,128)(2,1)S(1)}, bf16[256,512]{1,0:T(8,128)(2,1)}, u32[]{:S(2)}) copy-start(bf16[256,512]{1,0:T(8,128)(2,1)} %param.9) | copy-start | bytes 786436
  15.4 66.7 %all-to-all-start = ((bf16[32,5,4,128]{3,2,1,0:T(4,128)(2,1)}), bf16[32,5,4,128]{3,2,1,0:T(4,128)(2,1)S(1)}, u32[]{:S(2)}, u32[]{:S(2)}) async-start(bf16[32,5,4,128]{3,2,1,0:T(4,128)(2,1)} %pad_maximum_fusion.2), calls=%async_computation | async-start | bytes 327680 | tf_op jit(solution)/shard_map/all_to_all | solution.py:69
  83.6 23.7 %all-to-all-start.1 = ((bf16[32,4,4,128]{3,2,1,0:T(4,128)(2,1)}), bf16[32,4,4,128]{3,2,1,0:T(4,128)(2,1)S(1)}, u32[]{:S(2)}, u32[]{:S(2)}) async-start(bf16[32,4,4,128]{3,2,1,0:T(4,128)(2,1)} %copy.78), calls=%async_computation.1 | async-start | bytes 262144 | tf_op jit(solution)/shard_map/all_to_all | solution.py:90
  89.5 18.5 %copy-start.3 = (f32[512]{0:T(512)S(1)}, f32[512]{0:T(512)}, u32[]{:S(2)}) copy-start(f32[512]{0:T(512)} %param.12) | copy-start | bytes 6148
  134.4 4.3 %copy-start.1 = (bf16[6144,512]{1,0:T(8,128)(2,1)S(1)}, bf16[6144,512]{1,0:T(8,128)(2,1)}, u32[]{:S(2)}) copy-start(bf16[6144,512]{1,0:T(8,128)(2,1)} %all-gather.2.cloned.1.call-done) | copy-start | bytes 18874372
  141.1 16.3 %all-to-all-start.3 = ((bf16[4,272,384]{2,1,0:T(8,128)(2,1)}), bf16[4,272,384]{2,1,0:T(8,128)(2,1)S(1)}, u32[]{:S(2)}, u32[]{:S(2)}) async-start(bf16[4,272,384]{2,1,0:T(8,128)(2,1)} %pad_maximum_fusion), calls=%async_computation.3 | async-start | bytes 1671168 | tf_op jit(solution)/shard_map/all_to_all | solution.py:110
Sparse Core Ops, SparseCore 0:
  10.7 123.7 all-gather.1

commit v2 on v1

--- a/solution.py
+++ b/solution.py
@@ -7,6 +7,7 @@
 DH = 128
 EPSILON = 1e-06
 CTX = ("za", "zb", "core")
+INNER = ("zb", "core")
 TP = ("x", "y")
 HIGH = lax.Precision.HIGHEST
 BF16 = jnp.bfloat16
@@ -41,11 +42,22 @@
     return jnp.sum(join3(jnp.moveaxis(flat, 1, 0)), axis=0)
 
 
+def mixer(logs):
+    count, heads = logs.shape
+    upto = jnp.concatenate([jnp.zeros((1, heads), F32), jnp.cumsum(logs, axis=0)])
+    before = jnp.arange(count)[None, :] < jnp.arange(count + 1)[:, None]
+    gap = upto[:, None] - upto[None, 1:]
+    factor = jnp.where(before[:, :, None], jnp.exp(jnp.minimum(gap, 0.0)), 0.0)
+    return upto, factor
+
+
 def per_device(queries, keys, values, log_keep, state_in, norm_gain, out_weight):
     tokens = queries.shape[0]
     heads = log_keep.shape[0]
     parts = lax.axis_size(CTX)
+    quads, inner = lax.axis_size("za"), lax.axis_size(INNER)
     rows = DH // parts
+    slab = heads * quads * rows
     nx, ny = lax.axis_size("x"), lax.axis_size("y")
 
     swap = [(a * nx + b, b * nx + a) for a in range(nx) for b in range(nx)]
@@ -63,10 +75,11 @@
     kdec = (k * key_factor[:, :, None]).astype(BF16)
     inc = jnp.einsum("shd,she->hde", kdec, v, preferred_element_type=F32)
 
-    out = inc.astype(BF16).reshape(heads, parts, rows, DH).transpose(1, 0, 2, 3)
-    logs = jnp.pad(split3(own_log), ((0, rows - 3), (0, DH - heads)))
-    logs = jnp.broadcast_to(logs[None, None], (parts, 1, rows, DH))
-    got = lax.all_to_all(jnp.concatenate([out, logs], axis=1), CTX, 0, 0, tiled=True)
+    out = inc.astype(BF16).reshape(heads, quads, inner, rows, DH)
+    out = out.transpose(2, 0, 1, 3, 4).reshape(inner, slab, DH)
+    logs = jnp.pad(split3(own_log), ((0, 5), (0, DH - heads)))
+    logs = jnp.broadcast_to(logs[None], (inner,) + logs.shape)
+    got = lax.all_to_all(jnp.concatenate([out, logs], axis=1), INNER, 0, 0, tiled=True)
 
     causal = jnp.tril(jnp.ones((tokens, tokens), dtype=bool))
     spread = within[:, :, None] - within[:, None, :]
@@ -75,20 +88,34 @@
     weights = (scores * decay).astype(BF16)
     intra = jnp.einsum("hst,thd->shd", weights, v, preferred_element_type=F32)
 
-    incs = got[:, :heads].astype(F32)
-    every = join3(jnp.moveaxis(got[:, heads, :3, :heads], 1, 0))
-    upto = jnp.concatenate([jnp.zeros((1, heads), F32), jnp.cumsum(every, axis=0)])
-    order = jnp.arange(parts)
-    before = order[None, :] < jnp.arange(parts + 1)[:, None]
-    gap = upto[:, None] - upto[None, 1:]
-    mixing = jnp.where(before[:, :, None], jnp.exp(jnp.minimum(gap, 0.0)), 0.0)
-    me = lax.axis_index(CTX)
-    first = lax.dynamic_slice_in_dim(state_in, me * rows, rows, 1)
-    states = jnp.einsum("cjh,jhrd->chrd", mixing, incs, precision=HIGH)
-    states = states + jnp.exp(upto)[:, :, None, None] * first[None]
-    final = states[parts]
-    back = lax.all_to_all(states[:parts].astype(BF16), CTX, 0, 0, tiled=True)
-    start = back.transpose(1, 0, 2, 3).reshape(heads, DH, DH)
+    incs = got[:, :slab].astype(F32).reshape(inner, heads, -1)
+    upto, mixing = mixer(join3(jnp.moveaxis(got[:, slab : slab + 3, :heads], 1, 0)))
+    local = jnp.einsum("cjh,jhn->chn", mixing, incs, precision=HIGH)
+
+    total_log = jnp.pad(upto[inner], (0, DH - heads))
+    total_log = jnp.pad(total_log[None], ((0, 7), (0, 0)))
+    total = jnp.concatenate([local[inner].reshape(slab, DH), total_log])
+    totals = lax.all_to_all(
+        jnp.broadcast_to(total[None], (quads,) + total.shape), "za", 0, 0, tiled=True
+    )
+    after, across = mixer(totals[:, slab, :heads])
+    first = lax.dynamic_index_in_dim(
+        state_in.reshape(heads, quads, inner, rows, DH), lax.axis_index(INNER), 2, keepdims=False
+    ).reshape(heads, -1)
+    bounds = jnp.einsum(
+        "cjh,jhn->chn", across, totals[:, :slab].reshape(quads, heads, -1), precision=HIGH
+    )
+    bounds = bounds + jnp.exp(after)[:, :, None] * first[None]
+    quad = lax.axis_index("za")
+    final = lax.dynamic_index_in_dim(
+        bounds[quads].reshape(heads, quads, rows, DH), quad, 1, keepdims=False
+    )
+    opening = lax.dynamic_index_in_dim(bounds, quad, 0, keepdims=False)
+    states = local[:inner] + jnp.exp(upto[:inner])[:, :, None] * opening[None]
+    states = states.astype(BF16).reshape(inner, slab, DH)
+    back = lax.all_to_all(states, INNER, 0, 0, tiled=True)
+    start = back.reshape(inner, heads, quads, rows, DH).transpose(1, 2, 0, 3, 4)
+    start = start.reshape(heads, DH, DH)
 
     inter = jnp.einsum("shd,hde->she", q, start, preferred_element_type=F32)
     inter = inter * jnp.exp(within).T[:, :, None]

time: 167 us -> 163 us (0.976)
  waiting for transfers between devices: 54.5 us -> 45.3 us
  starting transfers between devices: 58.9 us -> 60.9 us
    all_to_all x2 -> x3, waiting for transfers between devices: 35.8 us -> 28.9 us  [the longest x1 17.1 us: per_device(): lax.all_to_all(jnp.broadcast_to(total[None], (quads,) + total.shape), 'za...]
    all_gather x1, waiting for transfers between devices: 6.9 us -> 4.58 us  [per_device(): gathered = lax.all_gather(moved, CTX, axis=0, tiled=True)]
    all_to_all x2 -> x3, starting transfers between devices: 53.2 us -> 55.3 us  [the longest x1 40.7 us: per_device(): lax.all_to_all(jnp.broadcast_to(total[None], (quads,) + total.shape), 'za...]
  transfers between devices with their start and end apart: 5 -> 6, of which waited for: 4 -> 5; matrix products, arithmetic and copies ran while one was open for 6% -> 8% of each run, Pallas kernels for 0% -> 0%
where the time goes in v2:
time: 163 us; the launch traced here: 162 us
  starting transfers between devices  60.9 us (37%)
  waiting for transfers between devices  45.3 us (28%)
  blocking collectives  20.1 us (12%)
  between operations  14.4 us (9%)
  matrix products  8.61 us (5%)
  local copies, waits for them, and re-layouts  7.5 us (5%)
  other arithmetic  5.33 us (3%)
    all_to_all x1, starting transfers between devices, per_device(): lax.all_to_all(jnp.broadcast_to(total[None], (quads,) + total.shape), 'za...  40.7 us
    all_to_all x1, blocking collectives, per_device(): acts = lax.all_to_all(message, 'x', 0, 0, tiled=True)  20.1 us
    all_to_all x1, waiting for transfers between devices, per_device(): lax.all_to_all(jnp.broadcast_to(total[None], (quads,) + total.shape), 'za...  17.1 us
    all_to_all x1, waiting for transfers between devices, per_device(): shares = lax.all_to_all(with_rows(partial, squares), 'y', 0, 0, tiled=True)  11.7 us
    all_to_all x1, starting transfers between devices, per_device(): lax.all_to_all(jnp.concatenate([out, logs], axis=1), INNER, 0, 0, tiled=T...  10.1 us
    all_to_all x1, waiting for transfers between devices, per_device(): lax.all_to_all(jnp.concatenate([out, logs], axis=1), INNER, 0, 0, tiled=T...  5.99 us
    all_to_all x1, waiting for transfers between devices, per_device(): back = lax.all_to_all(states, INNER, 0, 0, tiled=True)  5.79 us
    dot_general x4, matrix products, per_device(): lax.dot_general(acts[i, :tokens], gathered[i], (((1,), (1,)), ((), ())),...  5.51 us
  transfers between devices with their start and end apart: 6, of which 5 were waited for; matrix products, arithmetic and copies ran while one was open for 8% of the time, Pallas kernels for 0%

profile of v2, /device:TPU:1, one launch (start us, length us, event | category | flops | bytes accessed | tf_op | source)
XLA Modules:
  0.0 162.1 jit_solution(14570729606733894209)
XLA Ops:
  7.2 1.7 %collective-permute-start = (bf16[192,512]{1,0:T(8,128)(2,1)}, bf16[192,512]{1,0:T(8,128)(2,1)S(1)}, u32[]{:S(2)}, u32[]{:S(2)}) collective-permute-start(bf16[192,512]{1,0:T(8,128)(2,1)} %bitcast.151), channel_id=1, source_target_pairs={{0,0},{4,128},{8,256},{12,384},{128,4},{132,132},{136,260},{140,38... | collective-permute-start | bytes 589832 | tf_op jit(solution)/shard_map/ppermute | solution.py:64
  8.9 0.7 copy-done.2
  9.6 0.7 reshape.274
  10.3 1.2 reduce-window.6
  11.6 0.1 copy.66
  11.8 0.1 copy.67
  12.0 0.1 copy.89
  12.1 1.1 copy.90
  13.3 1.2 convolution_convert_fusion
  14.6 0.7 pad_maximum_fusion.2
  15.2 10.1 %all-to-all-start = ((bf16[8,72,128]{2,1,0:T(8,128)(2,1)}), bf16[8,72,128]{2,1,0:T(8,128)(2,1)S(1)}, u32[]{:S(2)}, u32[]{:S(2)}) async-start(bf16[8,72,128]{2,1,0:T(8,128)(2,1)} %pad_maximum_fusion.2), calls=%async_computation | async-start | bytes 294912 | tf_op jit(solution)/shard_map/all_to_all | solution.py:82
  25.4 6.0 %all-to-all-done = bf16[8,72,128]{2,1,0:T(8,128)(2,1)S(1)} async-done(((bf16[8,72,128]{2,1,0:T(8,128)(2,1)}), bf16[8,72,128]{2,1,0:T(8,128)(2,1)S(1)}, u32[]{:S(2)}, u32[]{:S(2)}) %all-to-all-start) | async-done | bytes 147488 | tf_op jit(solution)/shard_map/all_to_all | solution.py:82
  31.4 0.1 copy.73
  31.5 0.2 reduce_window_sum.47
  31.8 0.5 convolution_bitcast_fusion
  32.3 0.2 slice_reduce_fusion
  32.5 0.7 broadcast_in_dim.38
  33.2 40.7 %all-to-all-start.1 = ((f32[4,72,128]{2,1,0:T(8,128)}), f32[4,72,128]{2,1,0:T(8,128)S(1)}, u32[]{:S(2)}, u32[]{:S(2)}) async-start(f32[4,72,128]{2,1,0:T(8,128)} %broadcast_in_dim.38), calls=%async_computation.1 | async-start | bytes 294912 | tf_op jit(solution)/shard_map/all_to_all | solution.py:98
  73.9 0.8 constant_dynamic-slice_fusion.1
  74.8 17.1 %all-to-all-done.1 = f32[4,72,128]{2,1,0:T(8,128)S(1)} async-done(((f32[4,72,128]{2,1,0:T(8,128)}), f32[4,72,128]{2,1,0:T(8,128)S(1)}, u32[]{:S(2)}, u32[]{:S(2)}) %all-to-all-start.1) | async-done | bytes 147488 | tf_op jit(solution)/shard_map/all_to_all | solution.py:98
  92.0 0.1 copy.76
  92.1 0.1 concatenate.21.clone
  92.1 0.1 copy.78
  92.3 0.5 fusion.3
  92.9 0.1 fusion.27
  93.0 0.1 copy.79
  93.1 0.7 reshape.282
  93.9 4.5 %all-to-all-start.2 = ((bf16[8,64,128]{2,1,0:T(8,128)(2,1)}), bf16[8,64,128]{2,1,0:T(8,128)(2,1)S(1)}, u32[]{:S(2)}, u32[]{:S(2)}) async-start(bf16[8,64,128]{2,1,0:T(8,128)(2,1)} %reshape.282), calls=%async_computation.2 | async-start | bytes 262144 | tf_op jit(solution)/shard_map/all_to_all | solution.py:116
  98.4 0.6 convolution_bitcast_fusion.3
  99.0 5.8 %all-to-all-done.2 = bf16[8,64,128]{2,1,0:T(8,128)(2,1)S(1)} async-done(((bf16[8,64,128]{2,1,0:T(8,128)(2,1)}), bf16[8,64,128]{2,1,0:T(8,128)(2,1)S(1)}, u32[]{:S(2)}, u32[]{:S(2)}) %all-to-all-start.2) | async-done | bytes 131104 | tf_op jit(solution)/shard_map/all_to_all | solution.py:116
  104.8 0.1 copy.80
  105.0 0.3 multiply_reduce_fusion
  105.3 0.2 copy.86
  105.7 0.1 broadcast_in_dim.40
  105.8 20.1 %all_to_all.25 = bf16[4,272,512]{2,1,0:T(8,128)(2,1)S(1)} all-to-all(bf16[4,272,512]{2,1,0:T(8,128)(2,1)S(1)} %broadcast_in_dim.40), channel_id=1, replica_groups=mesh['za'=4,'zb'=4,'core'=2,'x'=4,'y'=4] {'x'}, dimensions={0} | all-to-all | bytes 2228224 | tf_op jit(solution)/shard_map/all_to_all | solution.py:128
  126.0 4.6 %all-gather.2.cloned.1.call-done = bf16[6144,512]{1,0:T(8,128)(2,1)} async-done(((bf16[192,512]{1,0:T(8,128)(2,1)}), bf16[6144,512]{1,0:T(8,128)(2,1)}) %all-gather.2.cloned.1.call-update) | async-done | bytes 6291472 | tf_op jit(solution)/shard_map/all_gather | solution.py:65
  130.6 2.2 %fusion.4 = f32[256,1536]{1,0:T(8,128)S(1)} fusion(bf16[6144,512]{1,0:T(8,128)(2,1)} %all-gather.2.cloned.1.call-done, bf16[4,272,512]{2,1,0:T(8,128)(2,1)S(1)} %all_to_all.25), kind=kOutput, calls=%fused_computation.7 | convolution fusion | flops 402653184 | bytes 3407872 | tf_op jit(solution)/shard_map/dot_general | solution.py:131
  132.8 2.1 %fusion.6 = f32[256,1536]{1,0:T(8,128)S(1)} fusion(bf16[6144,512]{1,0:T(8,128)(2,1)} %all-gather.2.cloned.1.call-done, bf16[4,272,512]{2,1,0:T(8,128)(2,1)S(1)} %all_to_all.25), kind=kOutput, calls=%fused_computation.9 | convolution fusion | flops 402653184 | bytes 3407872 | tf_op jit(solution)/shard_map/dot_general | solution.py:131
  134.9 0.6 fusion.8
  135.5 0.6 fusion.2
  136.1 0.1 copy.128
  136.2 1.0 pad_maximum_fusion
  137.2 3.9 %all-to-all-start.4 = ((bf16[4,272,384]{2,1,0:T(8,128)(2,1)}), bf16[4,272,384]{2,1,0:T(8,128)(2,1)S(1)}, u32[]{:S(2)}, u32[]{:S(2)}) async-start(bf16[4,272,384]{2,1,0:T(8,128)(2,1)} %pad_maximum_fusion), calls=%async_computation.4 | async-start | bytes 1671168 | tf_op jit(solution)/shard_map/all_to_all | solution.py:137
  141.1 0.6 dynamic-slice_bitcast_fusion
  141.7 11.7 %all-to-all-done.4 = bf16[4,272,384]{2,1,0:T(8,128)(2,1)S(1)} async-done(((bf16[4,272,384]{2,1,0:T(8,128)(2,1)}), bf16[4,272,384]{2,1,0:T(8,128)(2,1)S(1)}, u32[]{:S(2)}, u32[]{:S(2)}) %all-to-all-start.4) | async-done | bytes 835616 | tf_op jit(solution)/shard_map/all_to_all | solution.py:137
  153.5 0.8 multiply_convert_fusion
  154.4 0.1 convert_reduce_fusion
  154.5 0.8 multiply_convert_fusion.3
  (68 shorter events, 1.4 us)
Async XLA Ops:
  7.2 91.2 %copy-start = (bf16[256,512]{1,0:T(8,128)(2,1)S(1)}, bf16[256,512]{1,0:T(8,128)(2,1)}, u32[]{:S(2)}) copy-start(bf16[256,512]{1,0:T(8,128)(2,1)} %param.7) | copy-start | bytes 786436
  7.2 123.4 %all-gather.2.cloned.1.call-start = ((), (), s32[]{:S(2)}) async-start(), calls=%async_computation.5 | async-start | bytes 6488064 | tf_op jit(solution)/shard_map/all_gather | solution.py:65
  7.2 1.7 %collective-permute-start = (bf16[192,512]{1,0:T(8,128)(2,1)}, bf16[192,512]{1,0:T(8,128)(2,1)S(1)}, u32[]{:S(2)}, u32[]{:S(2)}) collective-permute-start(bf16[192,512]{1,0:T(8,128)(2,1)} %bitcast.151), channel_id=1, source_target_pairs={{0,0},{4,128},{8,256},{12,384},{128,4},{132,132},{136,260},{140,38... | collective-permute-start | bytes 589832 | tf_op jit(solution)/shard_map/ppermute | solution.py:64
  8.9 0.7 copy-start.2
  15.2 16.1 %all-to-all-start = ((bf16[8,72,128]{2,1,0:T(8,128)(2,1)}), bf16[8,72,128]{2,1,0:T(8,128)(2,1)S(1)}, u32[]{:S(2)}, u32[]{:S(2)}) async-start(bf16[8,72,128]{2,1,0:T(8,128)(2,1)} %pad_maximum_fusion.2), calls=%async_computation | async-start | bytes 294912 | tf_op jit(solution)/shard_map/all_to_all | solution.py:82
  32.5 65.9 %copy-start.4 = (bf16[256,512]{1,0:T(8,128)(2,1)S(1)}, bf16[256,512]{1,0:T(8,128)(2,1)}, u32[]{:S(2)}) copy-start(bf16[256,512]{1,0:T(8,128)(2,1)} %param.9) | copy-start | bytes 786436
  33.2 58.7 %all-to-all-start.1 = ((f32[4,72,128]{2,1,0:T(8,128)}), f32[4,72,128]{2,1,0:T(8,128)S(1)}, u32[]{:S(2)}, u32[]{:S(2)}) async-start(f32[4,72,128]{2,1,0:T(8,128)} %broadcast_in_dim.38), calls=%async_computation.1 | async-start | bytes 294912 | tf_op jit(solution)/shard_map/all_to_all | solution.py:98
  93.9 10.9 %all-to-all-start.2 = ((bf16[8,64,128]{2,1,0:T(8,128)(2,1)}), bf16[8,64,128]{2,1,0:T(8,128)(2,1)S(1)}, u32[]{:S(2)}, u32[]{:S(2)}) async-start(bf16[8,64,128]{2,1,0:T(8,128)(2,1)} %reshape.282), calls=%async_computation.2 | async-start | bytes 262144 | tf_op jit(solution)/shard_map/all_to_all | solution.py:116
  99.0 6.6 %copy-start.3 = (f32[512]{0:T(512)S(1)}, f32[512]{0:T(512)}, u32[]{:S(2)}) copy-start(f32[512]{0:T(512)} %param.12) | copy-start | bytes 6148
  130.6 4.3 %copy-start.1 = (bf16[6144,512]{1,0:T(8,128)(2,1)S(1)}, bf16[6144,512]{1,0:T(8,128)(2,1)}, u32[]{:S(2)}) copy-start(bf16[6144,512]{1,0:T(8,128)(2,1)} %all-gather.2.cloned.1.call-done) | copy-start | bytes 18874372
  137.2 16.2 %all-to-all-start.4 = ((bf16[4,272,384]{2,1,0:T(8,128)(2,1)}), bf16[4,272,384]{2,1,0:T(8,128)(2,1)S(1)}, u32[]{:S(2)}, u32[]{:S(2)}) async-start(bf16[4,272,384]{2,1,0:T(8,128)(2,1)} %pad_maximum_fusion), calls=%async_computation.4 | async-start | bytes 1671168 | tf_op jit(solution)/shard_map/all_to_all | solution.py:137
Sparse Core Ops, SparseCore 0:
  10.7 119.8 all-gather.1

commit v3 on v2

--- a/solution.py
+++ b/solution.py
@@ -60,11 +60,11 @@
     slab = heads * quads * rows
     nx, ny = lax.axis_size("x"), lax.axis_size("y")
 
-    swap = [(a * nx + b, b * nx + a) for a in range(nx) for b in range(nx)]
-    moved = lax.ppermute(out_weight.T, ("za", "x"), swap)
+    swap = [(a * ny + b, b * ny + a) for a in range(ny) for b in range(ny)]
+    moved = lax.ppermute(out_weight.T, ("zb", "y"), swap)
     gathered = lax.all_gather(moved, CTX, axis=0, tiled=True)
     cols = out_weight.shape[1] * parts // (nx * ny)
-    gathered = gathered.reshape(nx, ny * cols, out_weight.shape[0])
+    gathered = gathered.reshape(nx, ny, cols, out_weight.shape[0])
 
     q = queries.reshape(tokens, heads, DH)
     k = keys.reshape(tokens, heads, DH)
@@ -124,17 +124,16 @@
     gained = attended * norm_gain
 
     message = with_rows(gained.astype(BF16), squares)
-    message = jnp.broadcast_to(message[None], (nx,) + message.shape)
-    acts = lax.all_to_all(message, "x", 0, 0, tiled=True)
+    message = jnp.broadcast_to(message[None], (ny,) + message.shape)
+    acts = lax.all_to_all(message, "y", 0, 0, tiled=True)
     squares = rows_of(acts[:, tokens:], tokens)
-    partial = sum(
+    partial = jnp.stack([sum(
         lax.dot_general(
-            acts[i, :tokens], gathered[i], (((1,), (1,)), ((), ())), preferred_element_type=F32
+            acts[i, :tokens], gathered[j, i], (((1,), (1,)), ((), ())), preferred_element_type=F32
         )
-        for i in range(nx)
-    )
-    partial = partial.astype(BF16).reshape(tokens, ny, cols).transpose(1, 0, 2)
-    shares = lax.all_to_all(with_rows(partial, squares), "y", 0, 0, tiled=True)
+        for i in range(ny)
+    ).astype(BF16) for j in range(nx)])
+    shares = lax.all_to_all(with_rows(partial, squares), "x", 0, 0, tiled=True)
     squares = rows_of(shares[:, tokens:], tokens)
     scale = lax.rsqrt(squares / (H * DH) + EPSILON)[:, None]
     normed = (attended * scale * norm_gain).astype(BF16)

time: 163 us -> 152 us (0.933)
  starting transfers between devices: 60.9 us -> 44 us
  matrix products: 8.61 us -> 14.7 us
    all_to_all x1, starting transfers between devices: 40.7 us -> 13.7 us  [per_device(): lax.all_to_all(jnp.broadcast_to(total[None], (quads,) + total.shape), 'za...]
    all_to_all x1, starting transfers between devices: 10.1 us -> 20.1 us  [per_device(): lax.all_to_all(jnp.concatenate([out, logs], axis=1), INNER, 0, 0, tiled=T...]
    dot_general x4 -> x16, matrix products: 5.51 us -> 11.6 us  [per_device(): lax.dot_general(acts[i, :tokens], gathered[j, i], (((1,), (1,)), ((), ())...]
where the time goes in v3:
time: 152 us; the launch traced here: 151 us
  waiting for transfers between devices  44.8 us (29%)
  starting transfers between devices  44 us (29%)
  blocking collectives  20.5 us (13%)
  matrix products  14.7 us (10%)
  between operations  14.5 us (10%)
  local copies, waits for them, and re-layouts  7.42 us (5%)
  other arithmetic  5.33 us (4%)
    all_to_all x1, blocking collectives, per_device(): acts = lax.all_to_all(message, 'y', 0, 0, tiled=True)  20.5 us
    all_to_all x1, starting transfers between devices, per_device(): lax.all_to_all(jnp.concatenate([out, logs], axis=1), INNER, 0, 0, tiled=T...  20.1 us
    all_to_all x1, waiting for transfers between devices, per_device(): lax.all_to_all(jnp.broadcast_to(total[None], (quads,) + total.shape), 'za...  17.3 us
    all_to_all x1, starting transfers between devices, per_device(): lax.all_to_all(jnp.broadcast_to(total[None], (quads,) + total.shape), 'za...  13.7 us
    all_to_all x1, waiting for transfers between devices, per_device(): shares = lax.all_to_all(with_rows(partial, squares), 'x', 0, 0, tiled=True)  11.7 us
    dot_general x16, matrix products, per_device(): lax.dot_general(acts[i, :tokens], gathered[j, i], (((1,), (1,)), ((), ())...  11.6 us
    all_to_all x1, waiting for transfers between devices, per_device(): lax.all_to_all(jnp.concatenate([out, logs], axis=1), INNER, 0, 0, tiled=T...  5.96 us
    all_to_all x1, waiting for transfers between devices, per_device(): back = lax.all_to_all(states, INNER, 0, 0, tiled=True)  5.68 us
  transfers between devices with their start and end apart: 6, of which 5 were waited for; matrix products, arithmetic and copies ran while one was open for 8% of the time, Pallas kernels for 0%

profile of v3, /device:TPU:1, one launch (start us, length us, event | category | flops | bytes accessed | tf_op | source)
XLA Modules:
  0.0 151.2 jit_solution(5033377000865142325)
XLA Ops:
  7.2 1.7 %collective-permute-start = (bf16[192,512]{1,0:T(8,128)(2,1)}, bf16[192,512]{1,0:T(8,128)(2,1)S(1)}, u32[]{:S(2)}, u32[]{:S(2)}) collective-permute-start(bf16[192,512]{1,0:T(8,128)(2,1)} %bitcast.227), channel_id=1, source_target_pairs={{0,0},{1,32},{2,64},{3,96},{32,1},{33,33},{34,65},{35,97},{64,2},{... | collective-permute-start | bytes 589832 | tf_op jit(solution)/shard_map/ppermute | solution.py:64
  8.9 0.7 copy-done.2
  9.6 0.7 reshape.265
  10.3 1.2 reduce-window.6
  12.1 1.1 copy.88
  13.3 1.2 convolution_convert_fusion
  14.6 0.7 pad_maximum_fusion.2
  15.2 20.1 %all-to-all-start = ((bf16[8,72,128]{2,1,0:T(8,128)(2,1)}), bf16[8,72,128]{2,1,0:T(8,128)(2,1)S(1)}, u32[]{:S(2)}, u32[]{:S(2)}) async-start(bf16[8,72,128]{2,1,0:T(8,128)(2,1)} %pad_maximum_fusion.2), calls=%async_computation | async-start | bytes 294912 | tf_op jit(solution)/shard_map/all_to_all | solution.py:82
  35.3 6.0 %all-to-all-done = bf16[8,72,128]{2,1,0:T(8,128)(2,1)S(1)} async-done(((bf16[8,72,128]{2,1,0:T(8,128)(2,1)}), bf16[8,72,128]{2,1,0:T(8,128)(2,1)S(1)}, u32[]{:S(2)}, u32[]{:S(2)}) %all-to-all-start) | async-done | bytes 147488 | tf_op jit(solution)/shard_map/all_to_all | solution.py:82
  41.4 0.2 reduce_window_sum.47
  41.7 0.5 convolution_bitcast_fusion
  42.3 0.2 slice_reduce_fusion
  42.5 0.7 broadcast_in_dim.38
  43.1 13.7 %all-to-all-start.1 = ((f32[4,72,128]{2,1,0:T(8,128)}), f32[4,72,128]{2,1,0:T(8,128)S(1)}, u32[]{:S(2)}, u32[]{:S(2)}) async-start(f32[4,72,128]{2,1,0:T(8,128)} %broadcast_in_dim.38), calls=%async_computation.1 | async-start | bytes 294912 | tf_op jit(solution)/shard_map/all_to_all | solution.py:98
  56.9 0.8 constant_dynamic-slice_fusion.1
  57.7 17.3 %all-to-all-done.1 = f32[4,72,128]{2,1,0:T(8,128)S(1)} async-done(((f32[4,72,128]{2,1,0:T(8,128)}), f32[4,72,128]{2,1,0:T(8,128)S(1)}, u32[]{:S(2)}, u32[]{:S(2)}) %all-to-all-start.1) | async-done | bytes 147488 | tf_op jit(solution)/shard_map/all_to_all | solution.py:98
  75.4 0.5 fusion
  76.1 0.1 copy.78
  76.2 0.7 reshape.273
  77.0 4.3 %all-to-all-start.2 = ((bf16[8,64,128]{2,1,0:T(8,128)(2,1)}), bf16[8,64,128]{2,1,0:T(8,128)(2,1)S(1)}, u32[]{:S(2)}, u32[]{:S(2)}) async-start(bf16[8,64,128]{2,1,0:T(8,128)(2,1)} %reshape.273), calls=%async_computation.2 | async-start | bytes 262144 | tf_op jit(solution)/shard_map/all_to_all | solution.py:116
  81.3 0.6 convolution_bitcast_fusion.3
  81.9 5.7 %all-to-all-done.2 = bf16[8,64,128]{2,1,0:T(8,128)(2,1)S(1)} async-done(((bf16[8,64,128]{2,1,0:T(8,128)(2,1)}), bf16[8,64,128]{2,1,0:T(8,128)(2,1)S(1)}, u32[]{:S(2)}, u32[]{:S(2)}) %all-to-all-start.2) | async-done | bytes 131104 | tf_op jit(solution)/shard_map/all_to_all | solution.py:116
  87.8 0.3 multiply_reduce_fusion
  88.1 0.2 copy.84
  88.6 20.5 %all_to_all.25 = bf16[4,272,512]{2,1,0:T(8,128)(2,1)S(1)} all-to-all(bf16[4,272,512]{2,1,0:T(8,128)(2,1)S(1)} %broadcast_in_dim.40), channel_id=1, replica_groups=mesh['za'=4,'zb'=4,'core'=2,'x'=4,'y'=4] {'y'}, dimensions={0} | all-to-all | bytes 2228224 | tf_op jit(solution)/shard_map/all_to_all | solution.py:128
  109.2 4.1 %all-gather.2.cloned.1.call-done = bf16[6144,512]{1,0:T(8,128)(2,1)} async-done(((bf16[192,512]{1,0:T(8,128)(2,1)}), bf16[6144,512]{1,0:T(8,128)(2,1)}) %all-gather.2.cloned.1.call-update) | async-done | bytes 6291472 | tf_op jit(solution)/shard_map/all_gather | solution.py:65
  113.4 1.5 fusion.23
  114.8 1.7 %fusion.22 = f32[256,384]{1,0:T(8,128)S(1)} fusion(bf16[4,4,384,512]{3,2,1,0:T(8,128)(2,1)} %bitcast.189, bf16[4,272,512]{2,1,0:T(8,128)(2,1)S(1)} %all_to_all.25), kind=kOutput, calls=%fused_computation.57 | convolution fusion | flops 100663296 | bytes 1048576 | tf_op jit(solution)/shard_map/dot_general | solution.py:131
  116.5 1.3 fusion.21
  117.8 1.3 fusion.20
  119.1 1.3 convolution_add_fusion.11
  120.5 1.3 convolution_add_fusion.10
  121.8 0.3 fusion.11
  122.1 0.3 convolution_add_fusion.8
  122.4 0.3 convolution_add_fusion.7
  122.8 0.3 fusion.10
  123.1 0.3 convolution_add_fusion.5
  123.4 0.3 convolution_add_fusion.4
  123.8 0.3 fusion.9
  124.1 0.3 convolution_add_fusion.2
  124.4 0.3 convolution_add_fusion.1
  124.7 0.3 fusion.8
  125.1 1.0 pad_maximum_fusion
  126.1 4.1 %all-to-all-start.4 = ((bf16[4,272,384]{2,1,0:T(8,128)(2,1)}), bf16[4,272,384]{2,1,0:T(8,128)(2,1)S(1)}, u32[]{:S(2)}, u32[]{:S(2)}) async-start(bf16[4,272,384]{2,1,0:T(8,128)(2,1)} %pad_maximum_fusion), calls=%async_computation.4 | async-start | bytes 1671168 | tf_op jit(solution)/shard_map/all_to_all | solution.py:136
  130.2 0.6 dynamic-slice_bitcast_fusion
  130.8 11.7 %all-to-all-done.4 = bf16[4,272,384]{2,1,0:T(8,128)(2,1)S(1)} async-done(((bf16[4,272,384]{2,1,0:T(8,128)(2,1)}), bf16[4,272,384]{2,1,0:T(8,128)(2,1)S(1)}, u32[]{:S(2)}, u32[]{:S(2)}) %all-to-all-start.4) | async-done | bytes 835616 | tf_op jit(solution)/shard_map/all_to_all | solution.py:136
  142.6 0.8 multiply_convert_fusion
  143.5 0.8 multiply_convert_fusion.3
  (79 shorter events, 2.4 us)
Async XLA Ops:
  7.2 74.1 %copy-start = (bf16[256,512]{1,0:T(8,128)(2,1)S(1)}, bf16[256,512]{1,0:T(8,128)(2,1)}, u32[]{:S(2)}) copy-start(bf16[256,512]{1,0:T(8,128)(2,1)} %param.7) | copy-start | bytes 786436
  7.2 106.2 %all-gather.2.cloned.1.call-start = ((), (), s32[]{:S(2)}) async-start(), calls=%async_computation.5 | async-start | bytes 6488064 | tf_op jit(solution)/shard_map/all_gather | solution.py:65
  7.2 1.7 %collective-permute-start = (bf16[192,512]{1,0:T(8,128)(2,1)}, bf16[192,512]{1,0:T(8,128)(2,1)S(1)}, u32[]{:S(2)}, u32[]{:S(2)}) collective-permute-start(bf16[192,512]{1,0:T(8,128)(2,1)} %bitcast.227), channel_id=1, source_target_pairs={{0,0},{1,32},{2,64},{3,96},{32,1},{33,33},{34,65},{35,97},{64,2},{... | collective-permute-start | bytes 589832 | tf_op jit(solution)/shard_map/ppermute | solution.py:64
  8.9 0.7 copy-start.2
  15.2 26.1 %all-to-all-start = ((bf16[8,72,128]{2,1,0:T(8,128)(2,1)}), bf16[8,72,128]{2,1,0:T(8,128)(2,1)S(1)}, u32[]{:S(2)}, u32[]{:S(2)}) async-start(bf16[8,72,128]{2,1,0:T(8,128)(2,1)} %pad_maximum_fusion.2), calls=%async_computation | async-start | bytes 294912 | tf_op jit(solution)/shard_map/all_to_all | solution.py:82
  42.2 39.1 %copy-start.4 = (bf16[256,512]{1,0:T(8,128)(2,1)S(1)}, bf16[256,512]{1,0:T(8,128)(2,1)}, u32[]{:S(2)}) copy-start(bf16[256,512]{1,0:T(8,128)(2,1)} %param.9) | copy-start | bytes 786436
  43.1 31.9 %all-to-all-start.1 = ((f32[4,72,128]{2,1,0:T(8,128)}), f32[4,72,128]{2,1,0:T(8,128)S(1)}, u32[]{:S(2)}, u32[]{:S(2)}) async-start(f32[4,72,128]{2,1,0:T(8,128)} %broadcast_in_dim.38), calls=%async_computation.1 | async-start | bytes 294912 | tf_op jit(solution)/shard_map/all_to_all | solution.py:98
  77.0 10.6 %all-to-all-start.2 = ((bf16[8,64,128]{2,1,0:T(8,128)(2,1)}), bf16[8,64,128]{2,1,0:T(8,128)(2,1)S(1)}, u32[]{:S(2)}, u32[]{:S(2)}) async-start(bf16[8,64,128]{2,1,0:T(8,128)(2,1)} %reshape.273), calls=%async_computation.2 | async-start | bytes 262144 | tf_op jit(solution)/shard_map/all_to_all | solution.py:116
  81.9 6.5 %copy-start.3 = (f32[512]{0:T(512)S(1)}, f32[512]{0:T(512)}, u32[]{:S(2)}) copy-start(f32[512]{0:T(512)} %param.12) | copy-start | bytes 6148
  113.4 8.4 %copy-start.1 = (bf16[6144,512]{1,0:T(8,128)(2,1)S(1)}, bf16[6144,512]{1,0:T(8,128)(2,1)}, u32[]{:S(2)}) copy-start(bf16[6144,512]{1,0:T(8,128)(2,1)} %all-gather.2.cloned.1.call-done) | copy-start | bytes 18874372
  126.1 16.4 %all-to-all-start.4 = ((bf16[4,272,384]{2,1,0:T(8,128)(2,1)}), bf16[4,272,384]{2,1,0:T(8,128)(2,1)S(1)}, u32[]{:S(2)}, u32[]{:S(2)}) async-start(bf16[4,272,384]{2,1,0:T(8,128)(2,1)} %pad_maximum_fusion), calls=%async_computation.4 | async-start | bytes 1671168 | tf_op jit(solution)/shard_map/all_to_all | solution.py:136
Sparse Core Ops, SparseCore 0:
  10.7 102.6 all-gather.1

commit v4 on v3

--- a/solution.py
+++ b/solution.py
@@ -1,6 +1,8 @@
 import jax
 import jax.numpy as jnp
 from jax import lax
+from jax.experimental import pallas as pl
+from jax.experimental.pallas import tpu as pltpu
 from jax.sharding import Mesh, PartitionSpec as P
 
 H = 64
@@ -27,13 +29,9 @@
     return parts[0] + (parts[1] + parts[2])
 
 
-def with_rows(block, vector):
-    width = block.shape[-1]
+def tail_of(vector, width):
     flat = split3(vector).reshape(-1)
-    tail = jnp.pad(flat, (0, 16 * width - flat.shape[0])).reshape(16, width)
-    lead = block.shape[:-2]
-    tail = jnp.broadcast_to(tail, lead + tail.shape)
-    return jnp.concatenate([block, tail], axis=-2)
+    return jnp.pad(flat, (0, 16 * width - flat.shape[0])).reshape(16, width)
 
 
 def rows_of(tail, n):
@@ -49,6 +47,53 @@
     gap = upto[:, None] - upto[None, 1:]
     factor = jnp.where(before[:, :, None], jnp.exp(jnp.minimum(gap, 0.0)), 0.0)
     return upto, factor
+
+
+def project_kernel(x_ref, acts_ref, weights_ref, tail_ref, *refs):
+    outs, total = refs[:-1], refs[-1]
+    tokens = total.shape[0]
+    block, half = pl.program_id(0), pl.program_id(1)
+    depth = weights_ref.shape[1]
+    value = sum(
+        lax.dot_general(
+            acts_ref[half * depth + i, :tokens, :],
+            weights_ref[0, i],
+            (((1,), (1,)), ((), ())),
+            preferred_element_type=F32,
+        )
+        for i in range(depth)
+    )
+
+    @pl.when(half == 0)
+    def _():
+        total[...] = value
+
+    for j, out in enumerate(outs):
+        @pl.when((half == 1) & (block == j))
+        def _():
+            out[:tokens, :] = (total[...] + value).astype(BF16)
+            out[tokens:, :] = tail_ref[...]
+
+
+def project(acts, weights, tail, x):
+    nx, ny, cols, inner = weights.shape
+    rows = acts.shape[1]
+    return pl.pallas_call(
+        project_kernel,
+        out_shape=[jax.ShapeDtypeStruct((rows, cols), BF16)] * nx,
+        grid_spec=pltpu.PrefetchScalarGridSpec(
+            num_scalar_prefetch=1,
+            grid=(nx, 2),
+            in_specs=[
+                pl.BlockSpec(acts.shape, lambda j, h, x: (0, 0, 0)),
+                pl.BlockSpec((1, ny // 2, cols, inner), lambda j, h, x: (lax.rem(x[0] + j, nx), h, 0, 0)),
+                pl.BlockSpec(tail.shape, lambda j, h, x: (0, 0)),
+            ],
+            out_specs=[pl.BlockSpec((rows, cols), lambda j, h, x: (0, 0))] * nx,
+            scratch_shapes=[pltpu.VMEM((rows - tail.shape[0], cols), F32)],
+        ),
+        name="project",
+    )(x.reshape(1).astype(jnp.int32), acts, weights, tail)
 
 
 def per_device(queries, keys, values, log_keep, state_in, norm_gain, out_weight):
@@ -62,9 +107,6 @@
 
     swap = [(a * ny + b, b * ny + a) for a in range(ny) for b in range(ny)]
     moved = lax.ppermute(out_weight.T, ("zb", "y"), swap)
-    gathered = lax.all_gather(moved, CTX, axis=0, tiled=True)
-    cols = out_weight.shape[1] * parts // (nx * ny)
-    gathered = gathered.reshape(nx, ny, cols, out_weight.shape[0])
 
     q = queries.reshape(tokens, heads, DH)
     k = keys.reshape(tokens, heads, DH)
@@ -79,7 +121,13 @@
     out = out.transpose(2, 0, 1, 3, 4).reshape(inner, slab, DH)
     logs = jnp.pad(split3(own_log), ((0, 5), (0, DH - heads)))
     logs = jnp.broadcast_to(logs[None], (inner,) + logs.shape)
-    got = lax.all_to_all(jnp.concatenate([out, logs], axis=1), INNER, 0, 0, tiled=True)
+    opener = jnp.concatenate([out, logs], axis=1)
+    got = lax.all_to_all(opener, INNER, 0, 0, tiled=True)
+
+    moved, opener = lax.optimization_barrier((moved, opener))
+    gathered = lax.all_gather(moved, CTX, axis=0, tiled=True)
+    cols = out_weight.shape[1] * parts // (nx * ny)
+    gathered = gathered.reshape(nx, ny, cols, out_weight.shape[0])
 
     causal = jnp.tril(jnp.ones((tokens, tokens), dtype=bool))
     spread = within[:, :, None] - within[:, None, :]
@@ -123,21 +171,19 @@
     squares = jnp.sum(attended * attended, axis=1)
     gained = attended * norm_gain
 
-    message = with_rows(gained.astype(BF16), squares)
+    message = jnp.concatenate([gained.astype(BF16), tail_of(squares, heads * DH)])
     message = jnp.broadcast_to(message[None], (ny,) + message.shape)
     acts = lax.all_to_all(message, "y", 0, 0, tiled=True)
     squares = rows_of(acts[:, tokens:], tokens)
-    partial = jnp.stack([sum(
-        lax.dot_general(
-            acts[i, :tokens], gathered[j, i], (((1,), (1,)), ((), ())), preferred_element_type=F32
-        )
-        for i in range(ny)
-    ).astype(BF16) for j in range(nx)])
-    shares = lax.all_to_all(with_rows(partial, squares), "x", 0, 0, tiled=True)
-    squares = rows_of(shares[:, tokens:], tokens)
+    blocks = project(acts, gathered, tail_of(squares, cols), lax.axis_index("x"))
+    shares = [blocks[0]]
+    for step in (2, 1, 3):
+        ring = [(i, (i + step) % nx) for i in range(nx)]
+        shares.append(lax.ppermute(blocks[step], "x", ring))
+    squares = rows_of(jnp.stack([share[tokens:] for share in shares]), tokens)
     scale = lax.rsqrt(squares / (H * DH) + EPSILON)[:, None]
     normed = (attended * scale * norm_gain).astype(BF16)
-    layer_out = (jnp.sum(shares[:, :tokens].astype(F32), axis=0) * scale).astype(BF16)
+    layer_out = (sum(share[:tokens].astype(F32) for share in shares) * scale).astype(BF16)
     return (normed, final, layer_out)
 
 

time: 152 us -> 148 us (0.974); the launches traced: 151 us -> 145 us
  blocking collectives: 20.5 us -> 0 us
  matrix products: 14.7 us -> 3.08 us
  waiting for transfers between devices: 44.8 us -> 53.4 us
  Pallas kernels: 0 us -> 8.56 us
  starting transfers between devices: 44 us -> 51.6 us
  local copies, waits for them, and re-layouts: 7.42 us -> 10.1 us
    all_to_all x1 -> x0, blocking collectives: 20.5 us -> none  [per_device(): acts = lax.all_to_all(message, 'y', 0, 0, tiled=True)]
    dot_general x16 -> x0, matrix products: 11.6 us -> none  [per_device(): lax.dot_general(acts[i, :tokens], gathered[j, i], (((1,), (1,)), ((), ())...]
    ppermute x0 -> x3, starting transfers between devices: none -> 11.5 us  [per_device(): shares.append(lax.ppermute(blocks[step], 'x', ring))]
    pallas_call x0 -> x1, Pallas kernels: none -> 8.56 us  [project(): pl.pallas_call(project_kernel, out_shape=[jax.ShapeDtypeStruct((rows, col...]
    all_to_all x2, starting transfers between devices: 24.2 us -> 20.2 us  [the longest x1 14.5 us: per_device(): got = lax.all_to_all(opener, INNER, 0, 0, tiled=True)]
    ppermute x0 -> x3, waiting for transfers between devices: none -> 3.15 us  [per_device(): shares.append(lax.ppermute(blocks[step], 'x', ring))]
    all_gather x1, waiting for transfers between devices: 4.13 us -> 6.95 us  [per_device(): gathered = lax.all_gather(moved, CTX, axis=0, tiled=True)]
    all_to_all x2, waiting for transfers between devices: 17.7 us -> 19.7 us  [the longest x1 13.8 us: per_device(): acts = lax.all_to_all(message, 'y', 0, 0, tiled=True)]
  transfers between devices with their start and end apart: 6 -> 9, of which waited for: 5 -> 7; matrix products, arithmetic and copies ran while one was open for 8% -> 10% of each run, Pallas kernels for 0% -> 0%
where the time goes in v4:
time: 148 us; the launch traced here: 145 us
  waiting for transfers between devices  53.4 us (36%)
  starting transfers between devices  51.6 us (35%)
  between operations  14.4 us (10%)
  local copies, waits for them, and re-layouts  10.1 us (7%)
  Pallas kernels  8.56 us (6%)
  other arithmetic  4.28 us (3%)
  matrix products  3.08 us (2%)
    all_to_all x1, waiting for transfers between devices, per_device(): lax.all_to_all(jnp.broadcast_to(total[None], (quads,) + total.shape), 'za...  17.2 us
    all_to_all x1, starting transfers between devices, per_device(): got = lax.all_to_all(opener, INNER, 0, 0, tiled=True)  14.5 us
    all_to_all x1, waiting for transfers between devices, per_device(): acts = lax.all_to_all(message, 'y', 0, 0, tiled=True)  13.8 us
    all_to_all x1, starting transfers between devices, per_device(): lax.all_to_all(jnp.broadcast_to(total[None], (quads,) + total.shape), 'za...  13.7 us
    ppermute x3, starting transfers between devices, per_device(): shares.append(lax.ppermute(blocks[step], 'x', ring))  11.5 us
    pallas_call x1, Pallas kernels, project(): pl.pallas_call(project_kernel, out_shape=[jax.ShapeDtypeStruct((rows, col...  8.56 us
    all_gather x1, waiting for transfers between devices, per_device(): gathered = lax.all_gather(moved, CTX, axis=0, tiled=True)  6.95 us
    all_to_all x1, waiting for transfers between devices, per_device(): back = lax.all_to_all(states, INNER, 0, 0, tiled=True)  6.31 us
  transfers between devices with their start and end apart: 9, of which 7 were waited for; matrix products, arithmetic and copies ran while one was open for 10% of the time, Pallas kernels for 0%

profile of v4, /device:TPU:1, one launch (start us, length us, event | category | flops | bytes accessed | tf_op | source)
XLA Modules:
  0.0 145.4 jit_solution(9065950090914166520)
XLA Ops:
  7.2 1.7 %collective-permute-start = (bf16[192,512]{1,0:T(8,128)(2,1)}, bf16[192,512]{1,0:T(8,128)(2,1)S(1)}, u32[]{:S(2)}, u32[]{:S(2)}) collective-permute-start(bf16[192,512]{1,0:T(8,128)(2,1)} %bitcast.149), channel_id=1, source_target_pairs={{0,0},{1,32},{2,64},{3,96},{32,1},{33,33},{34,65},{35,97},{64,2},{... | collective-permute-start | bytes 589832 | tf_op jit(solution)/shard_map/ppermute | solution.py:109
  8.9 0.7 reshape.274
  9.6 1.2 reduce-window.6
  10.9 0.1 copy.65
  11.1 0.1 copy.66
  11.3 0.1 copy.87
  11.5 1.1 copy.88
  12.6 1.2 convolution_convert_fusion
  13.9 0.7 pad_maximum_fusion.1
  14.5 0.7 copy-done.3
  15.2 14.5 %all-to-all-start = ((bf16[8,72,128]{2,1,0:T(8,128)(2,1)}), bf16[8,72,128]{2,1,0:T(8,128)(2,1)S(1)}, u32[]{:S(2)}, u32[]{:S(2)}) async-start(bf16[8,72,128]{2,1,0:T(8,128)(2,1)} %pad_maximum_fusion.1), calls=%async_computation | async-start | bytes 294912 | tf_op jit(solution)/shard_map/all_to_all | solution.py:125
  29.8 6.0 %all-to-all-done = bf16[8,72,128]{2,1,0:T(8,128)(2,1)S(1)} async-done(((bf16[8,72,128]{2,1,0:T(8,128)(2,1)}), bf16[8,72,128]{2,1,0:T(8,128)(2,1)S(1)}, u32[]{:S(2)}, u32[]{:S(2)}) %all-to-all-start) | async-done | bytes 147488 | tf_op jit(solution)/shard_map/all_to_all | solution.py:125
  35.7 0.1 copy.72
  35.8 0.2 reduce_window_sum.47
  36.0 0.1 concatenate.17
  36.1 0.5 convolution_bitcast_fusion
  36.7 0.2 slice_reduce_fusion
  36.9 0.7 broadcast_in_dim.36
  37.5 13.7 %all-to-all-start.1 = ((f32[4,72,128]{2,1,0:T(8,128)}), f32[4,72,128]{2,1,0:T(8,128)S(1)}, u32[]{:S(2)}, u32[]{:S(2)}) async-start(f32[4,72,128]{2,1,0:T(8,128)} %broadcast_in_dim.36), calls=%async_computation.1 | async-start | bytes 294912 | tf_op jit(solution)/shard_map/all_to_all | solution.py:146
  51.3 0.8 constant_dynamic-slice_fusion.1
  52.1 17.2 %all-to-all-done.1 = f32[4,72,128]{2,1,0:T(8,128)S(1)} async-done(((f32[4,72,128]{2,1,0:T(8,128)}), f32[4,72,128]{2,1,0:T(8,128)S(1)}, u32[]{:S(2)}, u32[]{:S(2)}) %all-to-all-start.1) | async-done | bytes 147488 | tf_op jit(solution)/shard_map/all_to_all | solution.py:146
  69.4 0.1 copy.75
  69.5 0.1 copy.77
  69.7 0.5 fusion
  70.3 0.1 fusion.17
  70.4 0.1 copy.78
  70.6 0.7 reshape.282
  71.3 4.4 %all-to-all-start.2 = ((bf16[8,64,128]{2,1,0:T(8,128)(2,1)}), bf16[8,64,128]{2,1,0:T(8,128)(2,1)S(1)}, u32[]{:S(2)}, u32[]{:S(2)}) async-start(bf16[8,64,128]{2,1,0:T(8,128)(2,1)} %reshape.282), calls=%async_computation.2 | async-start | bytes 262144 | tf_op jit(solution)/shard_map/all_to_all | solution.py:164
  75.7 0.6 convolution_bitcast_fusion.3
  76.4 6.3 %all-to-all-done.2 = bf16[8,64,128]{2,1,0:T(8,128)(2,1)S(1)} async-done(((bf16[8,64,128]{2,1,0:T(8,128)(2,1)}), bf16[8,64,128]{2,1,0:T(8,128)(2,1)S(1)}, u32[]{:S(2)}, u32[]{:S(2)}) %all-to-all-start.2) | async-done | bytes 131104 | tf_op jit(solution)/shard_map/all_to_all | solution.py:164
  82.7 0.1 copy.79
  82.8 0.3 multiply_reduce_fusion
  83.2 0.2 copy.84
  83.6 1.1 broadcast_in_dim.38
  84.7 5.7 %all-to-all-start.3 = ((bf16[4,272,512]{2,1,0:T(8,128)(2,1)}), bf16[4,272,512]{2,1,0:T(8,128)(2,1)S(1)}, u32[]{:S(2)}, u32[]{:S(2)}) async-start(bf16[4,272,512]{2,1,0:T(8,128)(2,1)} %broadcast_in_dim.38), calls=%async_computation.3 | async-start | bytes 2228224 | tf_op jit(solution)/shard_map/all_to_all | solution.py:176
  90.4 0.6 dynamic-slice_bitcast_fusion
  91.0 13.8 %all-to-all-done.3.acts_ref = bf16[4,272,512]{2,1,0:T(8,128)(2,1)S(1)} async-done(((bf16[4,272,512]{2,1,0:T(8,128)(2,1)}), bf16[4,272,512]{2,1,0:T(8,128)(2,1)S(1)}, u32[]{:S(2)}, u32[]{:S(2)}) %all-to-all-start.3) | async-done | bytes 1114144 | tf_op jit(solution)/shard_map/all_to_all | solution.py:176
  105.0 0.8 reshape.292.tail_ref
  105.8 7.0 %all-gather.2.cloned.1.call-done = bf16[6144,512]{1,0:T(8,128)(2,1)} async-done(((bf16[192,512]{1,0:T(8,128)(2,1)}), bf16[6144,512]{1,0:T(8,128)(2,1)}) %all-gather.2.cloned.1.call-update) | async-done | bytes 6291472 | tf_op jit(solution)/shard_map/all_gather | solution.py:128
  112.7 8.6 %project.1 = (bf16[272,384]{1,0:T(8,128)(2,1)}, bf16[272,384]{1,0:T(8,128)(2,1)}, bf16[272,384]{1,0:T(8,128)(2,1)}, bf16[272,384]{1,0:T(8,128)(2,1)}) custom-call(s32[1]{0:T(128)} %bitcast.22.x_ref, bf16[4,272,512]{2,1,0:T(8,128)(2,1)} %copy-done.1, bf16[4,4,384,512]{3,2,1,0:T(8,128)(2,1)} %bitcast.122, bf16[16,384]{1,0:T(8,128)(2,1)} %reshape.292.tail_ref), custom_call_target="tpu_custom_call" | custom-call | tf_op jit(solution)/shard_map/project/pallas_call | solution.py:81
  121.3 5.0 %collective-permute-start.1 = (bf16[272,384]{1,0:T(8,128)(2,1)}, bf16[272,384]{1,0:T(8,128)(2,1)S(1)}, u32[]{:S(2)}, u32[]{:S(2)}) collective-permute-start(bf16[272,384]{1,0:T(8,128)(2,1)} %get-tuple-element.10), channel_id=1, source_target_pairs={{0,8},{4,12},{8,0},{12,4},{1,9},{5,13},{9,1},{13,5},{2,10},{6,14},... | collective-permute-start | bytes 626696 | tf_op jit(solution)/shard_map/ppermute | solution.py:182
  126.3 2.1 %collective-permute-start.2 = (bf16[272,384]{1,0:T(8,128)(2,1)}, bf16[272,384]{1,0:T(8,128)(2,1)S(1)}, u32[]{:S(2)}, u32[]{:S(2)}) collective-permute-start(bf16[272,384]{1,0:T(8,128)(2,1)} %get-tuple-element.11), channel_id=1, source_target_pairs={{0,4},{4,8},{8,12},{12,0},{1,5},{5,9},{9,13},{13,1},{2,6},{6,10},{... | collective-permute-start | bytes 626696 | tf_op jit(solution)/shard_map/ppermute | solution.py:182
  128.5 4.4 %collective-permute-start.3 = (bf16[272,384]{1,0:T(8,128)(2,1)}, bf16[272,384]{1,0:T(8,128)(2,1)S(1)}, u32[]{:S(2)}, u32[]{:S(2)}) collective-permute-start(bf16[272,384]{1,0:T(8,128)(2,1)} %get-tuple-element.12), channel_id=1, source_target_pairs={{0,12},{4,0},{8,4},{12,8},{1,13},{5,1},{9,5},{13,9},{2,14},{6,2},{... | collective-permute-start | bytes 626696 | tf_op jit(solution)/shard_map/ppermute | solution.py:182
  132.8 0.7 slice_bitcast_fusion.4
  133.6 2.8 %collective-permute-done.2 = bf16[272,384]{1,0:T(8,128)(2,1)S(1)} collective-permute-done((bf16[272,384]{1,0:T(8,128)(2,1)}, bf16[272,384]{1,0:T(8,128)(2,1)S(1)}, u32[]{:S(2)}, u32[]{:S(2)}) %collective-permute-start.2) | collective-permute-done | bytes 208928 | tf_op jit(solution)/shard_map/ppermute | solution.py:182
  136.4 0.4 collective-permute-done.3
  136.9 0.8 multiply_convert_fusion
  137.7 0.8 multiply_convert_fusion.3
  (74 shorter events, 1.5 us)
Async XLA Ops:
  7.2 68.6 %copy-start = (bf16[256,512]{1,0:T(8,128)(2,1)S(1)}, bf16[256,512]{1,0:T(8,128)(2,1)}, u32[]{:S(2)}) copy-start(bf16[256,512]{1,0:T(8,128)(2,1)} %param.7) | copy-start | bytes 786436
  7.2 105.5 %all-gather.2.cloned.1.call-start = ((), (), s32[]{:S(2)}) async-start(), calls=%async_computation.4 | async-start | bytes 6488064 | tf_op jit(solution)/shard_map/all_gather | solution.py:128
  7.2 7.3 %collective-permute-start = (bf16[192,512]{1,0:T(8,128)(2,1)}, bf16[192,512]{1,0:T(8,128)(2,1)S(1)}, u32[]{:S(2)}, u32[]{:S(2)}) collective-permute-start(bf16[192,512]{1,0:T(8,128)(2,1)} %bitcast.149), channel_id=1, source_target_pairs={{0,0},{1,32},{2,64},{3,96},{32,1},{33,33},{34,65},{35,97},{64,2},{... | collective-permute-start | bytes 589832 | tf_op jit(solution)/shard_map/ppermute | solution.py:109
  14.5 0.7 copy-start.3
  15.2 20.5 %all-to-all-start = ((bf16[8,72,128]{2,1,0:T(8,128)(2,1)}), bf16[8,72,128]{2,1,0:T(8,128)(2,1)S(1)}, u32[]{:S(2)}, u32[]{:S(2)}) async-start(bf16[8,72,128]{2,1,0:T(8,128)(2,1)} %pad_maximum_fusion.1), calls=%async_computation | async-start | bytes 294912 | tf_op jit(solution)/shard_map/all_to_all | solution.py:125
  37.5 31.8 %all-to-all-start.1 = ((f32[4,72,128]{2,1,0:T(8,128)}), f32[4,72,128]{2,1,0:T(8,128)S(1)}, u32[]{:S(2)}, u32[]{:S(2)}) async-start(f32[4,72,128]{2,1,0:T(8,128)} %broadcast_in_dim.36), calls=%async_computation.1 | async-start | bytes 294912 | tf_op jit(solution)/shard_map/all_to_all | solution.py:146
  69.7 6.1 %copy-start.5 = (bf16[256,512]{1,0:T(8,128)(2,1)S(1)}, bf16[256,512]{1,0:T(8,128)(2,1)}, u32[]{:S(2)}) copy-start(bf16[256,512]{1,0:T(8,128)(2,1)} %param.9) | copy-start | bytes 786436
  71.3 11.4 %all-to-all-start.2 = ((bf16[8,64,128]{2,1,0:T(8,128)(2,1)}), bf16[8,64,128]{2,1,0:T(8,128)(2,1)S(1)}, u32[]{:S(2)}, u32[]{:S(2)}) async-start(bf16[8,64,128]{2,1,0:T(8,128)(2,1)} %reshape.282), calls=%async_computation.2 | async-start | bytes 262144 | tf_op jit(solution)/shard_map/all_to_all | solution.py:164
  82.8 0.7 copy-start.4
  84.7 20.1 %all-to-all-start.3 = ((bf16[4,272,512]{2,1,0:T(8,128)(2,1)}), bf16[4,272,512]{2,1,0:T(8,128)(2,1)S(1)}, u32[]{:S(2)}, u32[]{:S(2)}) async-start(bf16[4,272,512]{2,1,0:T(8,128)(2,1)} %broadcast_in_dim.38), calls=%async_computation.3 | async-start | bytes 2228224 | tf_op jit(solution)/shard_map/all_to_all | solution.py:176
  104.8 7.9 %copy-start.1 = (bf16[4,272,512]{2,1,0:T(8,128)(2,1)}, bf16[4,272,512]{2,1,0:T(8,128)(2,1)S(1)}, u32[]{:S(2)}) copy-start(bf16[4,272,512]{2,1,0:T(8,128)(2,1)S(1)} %all-to-all-done.3.acts_ref) | copy-start | bytes 3342340
  121.3 16.4 %copy-start.2 = (bf16[272,384]{1,0:T(8,128)(2,1)S(1)}, bf16[272,384]{1,0:T(8,128)(2,1)}, u32[]{:S(2)}) copy-start(bf16[272,384]{1,0:T(8,128)(2,1)} %get-tuple-element.9) | copy-start | bytes 626692
  121.3 12.3 %collective-permute-start.1 = (bf16[272,384]{1,0:T(8,128)(2,1)}, bf16[272,384]{1,0:T(8,128)(2,1)S(1)}, u32[]{:S(2)}, u32[]{:S(2)}) collective-permute-start(bf16[272,384]{1,0:T(8,128)(2,1)} %get-tuple-element.10), channel_id=1, source_target_pairs={{0,8},{4,12},{8,0},{12,4},{1,9},{5,13},{9,1},{13,5},{2,10},{6,14},... | collective-permute-start | bytes 626696 | tf_op jit(solution)/shard_map/ppermute | solution.py:182
  126.3 10.1 %collective-permute-start.2 = (bf16[272,384]{1,0:T(8,128)(2,1)}, bf16[272,384]{1,0:T(8,128)(2,1)S(1)}, u32[]{:S(2)}, u32[]{:S(2)}) collective-permute-start(bf16[272,384]{1,0:T(8,128)(2,1)} %get-tuple-element.11), channel_id=1, source_target_pairs={{0,4},{4,8},{8,12},{12,0},{1,5},{5,9},{9,13},{13,1},{2,6},{6,10},{... | collective-permute-start | bytes 626696 | tf_op jit(solution)/shard_map/ppermute | solution.py:182
  128.5 8.3 %collective-permute-start.3 = (bf16[272,384]{1,0:T(8,128)(2,1)}, bf16[272,384]{1,0:T(8,128)(2,1)S(1)}, u32[]{:S(2)}, u32[]{:S(2)}) collective-permute-start(bf16[272,384]{1,0:T(8,128)(2,1)} %get-tuple-element.12), channel_id=1, source_target_pairs={{0,12},{4,0},{8,4},{12,8},{1,13},{5,1},{9,5},{13,9},{2,14},{6,2},{... | collective-permute-start | bytes 626696 | tf_op jit(solution)/shard_map/ppermute | solution.py:182
Sparse Core Ops, SparseCore 0:
  15.4 97.3 all-gather.1

commit v5 on v3

--- a/solution.py
+++ b/solution.py
@@ -1,6 +1,10 @@
+import functools
+
 import jax
 import jax.numpy as jnp
 from jax import lax
+from jax.experimental import pallas as pl
+from jax.experimental.pallas import tpu as pltpu
 from jax.sharding import Mesh, PartitionSpec as P
 
 H = 64
@@ -9,6 +13,7 @@
 CTX = ("za", "zb", "core")
 INNER = ("zb", "core")
 TP = ("x", "y")
+FLIGHT = 6
 HIGH = lax.Precision.HIGHEST
 BF16 = jnp.bfloat16
 F32 = jnp.float32
@@ -27,13 +32,9 @@
     return parts[0] + (parts[1] + parts[2])
 
 
-def with_rows(block, vector):
-    width = block.shape[-1]
+def tail_of(vector, width):
     flat = split3(vector).reshape(-1)
-    tail = jnp.pad(flat, (0, 16 * width - flat.shape[0])).reshape(16, width)
-    lead = block.shape[:-2]
-    tail = jnp.broadcast_to(tail, lead + tail.shape)
-    return jnp.concatenate([block, tail], axis=-2)
+    return jnp.pad(flat, (0, 16 * width - flat.shape[0])).reshape(16, width)
 
 
 def rows_of(tail, n):
@@ -49,6 +50,73 @@
     gap = upto[:, None] - upto[None, 1:]
     factor = jnp.where(before[:, :, None], jnp.exp(jnp.minimum(gap, 0.0)), 0.0)
     return upto, factor
+
+
+def place_of(z, y, count):
+    return lax.rem(z + jnp.where(y == 3, count - 1, y), count)
+
+
+def project_kernel(targets, at_ref, acts_ref, weights_ref, tail_ref, *refs):
+    outs, (left, right, sems) = refs[: len(targets)], refs[len(targets) :]
+    tokens = acts_ref.shape[1] - tail_ref.shape[0]
+    ny = acts_ref.shape[0]
+    x, y = at_ref[0], at_ref[1]
+    count = weights_ref.shape[0]
+    nx = count // ny
+    copies = []
+    for n, step in enumerate(targets):
+        z = lax.rem(x + step, nx) * ny + y
+        for i in range(ny):
+            pair = []
+            if n == 0:
+                pair.append(pltpu.make_async_copy(acts_ref.at[i], left.at[i], sems.at[len(targets), i]))
+            source = weights_ref.at[place_of(z, i, count)]
+            pair.append(pltpu.make_async_copy(source, right.at[n, i], sems.at[n, i]))
+            copies.append(pair)
+    for pair in copies[:FLIGHT]:
+        for copy in pair:
+            copy.start()
+    m = 0
+    for n, out in enumerate(outs):
+        total = None
+        for i in range(ny):
+            for copy in copies[m]:
+                copy.wait()
+            if m + FLIGHT < len(copies):
+                for copy in copies[m + FLIGHT]:
+                    copy.start()
+            m += 1
+            value = lax.dot_general(
+                left[i, :tokens, :],
+                right[n, i],
+                (((1,), (1,)), ((), ())),
+                preferred_element_type=F32,
+            )
+            total = value if total is None else total + value
+        out[:tokens, :] = total.astype(BF16)
+        out[tokens:, :] = tail_ref[...]
+
+
+def project(acts, weights, tail, at, targets):
+    ny, rows, depth = acts.shape
+    cols = weights.shape[1]
+    vmem = pl.BlockSpec(memory_space=pltpu.VMEM)
+    return pl.pallas_call(
+        functools.partial(project_kernel, targets),
+        out_shape=[jax.ShapeDtypeStruct((rows, cols), BF16)] * len(targets),
+        grid_spec=pltpu.PrefetchScalarGridSpec(
+            num_scalar_prefetch=1,
+            grid=(),
+            in_specs=[pl.BlockSpec(memory_space=pl.ANY)] * 2 + [vmem],
+            out_specs=[vmem] * len(targets),
+            scratch_shapes=[
+                pltpu.VMEM(acts.shape, BF16),
+                pltpu.VMEM((len(targets), ny, cols, depth), BF16),
+                pltpu.SemaphoreType.DMA((len(targets) + 1, ny)),
+            ],
+        ),
+        name="project",
+    )(at, acts, weights, tail)
 
 
 def per_device(queries, keys, values, log_keep, state_in, norm_gain, out_weight):
@@ -60,11 +128,13 @@
     slab = heads * quads * rows
     nx, ny = lax.axis_size("x"), lax.axis_size("y")
 
-    swap = [(a * ny + b, b * ny + a) for a in range(ny) for b in range(ny)]
-    moved = lax.ppermute(out_weight.T, ("zb", "y"), swap)
-    gathered = lax.all_gather(moved, CTX, axis=0, tiled=True)
-    cols = out_weight.shape[1] * parts // (nx * ny)
-    gathered = gathered.reshape(nx, ny, cols, out_weight.shape[0])
+    chips = parts // lax.axis_size("core")
+    swap = [
+        (z * ny + y, ((z + (y if y < 3 else -1)) % chips) * ny + z % ny)
+        for z in range(chips)
+        for y in range(ny)
+    ]
+    moved = lax.ppermute(out_weight.T, ("za", "zb", "y"), swap)
 
     q = queries.reshape(tokens, heads, DH)
     k = keys.reshape(tokens, heads, DH)
@@ -79,7 +149,13 @@
     out = out.transpose(2, 0, 1, 3, 4).reshape(inner, slab, DH)
     logs = jnp.pad(split3(own_log), ((0, 5), (0, DH - heads)))
     logs = jnp.broadcast_to(logs[None], (inner,) + logs.shape)
-    got = lax.all_to_all(jnp.concatenate([out, logs], axis=1), INNER, 0, 0, tiled=True)
+    opener = jnp.concatenate([out, logs], axis=1)
+    got = lax.all_to_all(opener, INNER, 0, 0, tiled=True)
+
+    moved, opener = lax.optimization_barrier((moved, opener))
+    gathered = lax.all_gather(moved, CTX, axis=0, tiled=True)
+    cols = out_weight.shape[1] * parts // (nx * ny)
+    gathered = gathered.reshape(nx * ny, cols, out_weight.shape[0])
 
     causal = jnp.tril(jnp.ones((tokens, tokens), dtype=bool))
     spread = within[:, :, None] - within[:, None, :]
@@ -123,21 +199,22 @@
     squares = jnp.sum(attended * attended, axis=1)
     gained = attended * norm_gain
 
-    message = with_rows(gained.astype(BF16), squares)
+    message = jnp.concatenate([gained.astype(BF16), tail_of(squares, heads * DH)])
     message = jnp.broadcast_to(message[None], (ny,) + message.shape)
     acts = lax.all_to_all(message, "y", 0, 0, tiled=True)
     squares = rows_of(acts[:, tokens:], tokens)
-    partial = jnp.stack([sum(
-        lax.dot_general(
-            acts[i, :tokens], gathered[j, i], (((1,), (1,)), ((), ())), preferred_element_type=F32
-        )
-        for i in range(ny)
-    ).astype(BF16) for j in range(nx)])
-    shares = lax.all_to_all(with_rows(partial, squares), "x", 0, 0, tiled=True)
-    squares = rows_of(shares[:, tokens:], tokens)
+    at = jnp.stack([lax.axis_index("x"), lax.axis_index("y")]).astype(jnp.int32)
+    tail = tail_of(squares, cols)
+    far = project(acts, gathered, tail, at, (2,))
+    near = project(acts, gathered, tail, at, (1, 3, 0))
+    shares = [near[2]]
+    for step, block in ((2, far[0]), (1, near[0]), (3, near[1])):
+        ring = [(i, (i + step) % nx) for i in range(nx)]
+        shares.append(lax.ppermute(block, "x", ring))
+    squares = rows_of(jnp.stack([share[tokens:] for share in shares]), tokens)
     scale = lax.rsqrt(squares / (H * DH) + EPSILON)[:, None]
     normed = (attended * scale * norm_gain).astype(BF16)
-    layer_out = (jnp.sum(shares[:, :tokens].astype(F32), axis=0) * scale).astype(BF16)
+    layer_out = (sum(share[:tokens].astype(F32) for share in shares) * scale).astype(BF16)
     return (normed, final, layer_out)
 
 

time: 152 us -> 149 us (0.980); the launches traced: 151 us -> 147 us
  blocking collectives: 20.5 us -> 0 us
  matrix products: 14.7 us -> 3.08 us
  Pallas kernels: 0 us -> 10.6 us
  waiting for transfers between devices: 44.8 us -> 52.4 us
  starting transfers between devices: 44 us -> 51.1 us
  local copies, waits for them, and re-layouts: 7.42 us -> 10.1 us
    all_to_all x1 -> x0, blocking collectives: 20.5 us -> none  [per_device(): acts = lax.all_to_all(message, 'y', 0, 0, tiled=True)]
    dot_general x16 -> x0, matrix products: 11.6 us -> none  [per_device(): lax.dot_general(acts[i, :tokens], gathered[j, i], (((1,), (1,)), ((), ())...]
    ppermute x1 -> x4, starting transfers between devices: 1.72 us -> 13 us  [the longest x3 11.3 us: per_device(): shares.append(lax.ppermute(block, 'x', ring))]
    pallas_call x0 -> x2, Pallas kernels: none -> 10.6 us  [project(): pl.pallas_call(functools.partial(project_kernel, targets), out_shape=[jax...]
    all_to_all x2, starting transfers between devices: 24.2 us -> 16.3 us  [the longest x1 12.8 us: per_device(): got = lax.all_to_all(opener, INNER, 0, 0, tiled=True)]
    all_gather x1, waiting for transfers between devices: 4.13 us -> 8.35 us  [per_device(): gathered = lax.all_gather(moved, CTX, axis=0, tiled=True)]
    ppermute x1 -> x4, waiting for transfers between devices: 0.01 us -> 3.16 us  [the longest x3 3.16 us: per_device(): shares.append(lax.ppermute(block, 'x', ring))]
    all_to_all x1, starting transfers between devices: 4.29 us -> 6.43 us  [per_device(): back = lax.all_to_all(states, INNER, 0, 0, tiled=True)]
  transfers between devices with their start and end apart: 6 -> 9, of which waited for: 5 -> 7; matrix products, arithmetic and copies ran while one was open for 8% -> 11% of each run, Pallas kernels for 0% -> 4%
where the time goes in v5:
time: 149 us; the launch traced here: 147 us
  waiting for transfers between devices  52.4 us (35%)
  starting transfers between devices  51.1 us (34%)
  between operations  14.4 us (10%)
  Pallas kernels  10.6 us (7%)
  local copies, waits for them, and re-layouts  10.1 us (7%)
  other arithmetic  4.86 us (3%)
  matrix products  3.08 us (2%)
    all_to_all x1, starting transfers between devices, per_device(): lax.all_to_all(jnp.broadcast_to(total[None], (quads,) + total.shape), 'za...  15.3 us
    all_to_all x1, waiting for transfers between devices, per_device(): lax.all_to_all(jnp.broadcast_to(total[None], (quads,) + total.shape), 'za...  15.2 us
    all_to_all x1, waiting for transfers between devices, per_device(): acts = lax.all_to_all(message, 'y', 0, 0, tiled=True)  13.3 us
    all_to_all x1, starting transfers between devices, per_device(): got = lax.all_to_all(opener, INNER, 0, 0, tiled=True)  12.8 us
    ppermute x3, starting transfers between devices, per_device(): shares.append(lax.ppermute(block, 'x', ring))  11.3 us
    pallas_call x2, Pallas kernels, project(): pl.pallas_call(functools.partial(project_kernel, targets), out_shape=[jax...  10.6 us
    all_gather x1, waiting for transfers between devices, per_device(): gathered = lax.all_gather(moved, CTX, axis=0, tiled=True)  8.35 us
    all_to_all x1, waiting for transfers between devices, per_device(): back = lax.all_to_all(states, INNER, 0, 0, tiled=True)  6.45 us
  transfers between devices with their start and end apart: 9, of which 7 were waited for; matrix products, arithmetic and copies ran while one was open for 11% of the time, Pallas kernels for 4%

profile of v5, /device:TPU:1, one launch (start us, length us, event | category | flops | bytes accessed | tf_op | source)
XLA Modules:
  0.0 146.6 jit_solution(13029433011661294280)
XLA Ops:
  7.2 1.7 %collective-permute-start = (bf16[192,512]{1,0:T(8,128)(2,1)}, bf16[192,512]{1,0:T(8,128)(2,1)S(1)}, u32[]{:S(2)}, u32[]{:S(2)}) collective-permute-start(bf16[192,512]{1,0:T(8,128)(2,1)} %bitcast.151), channel_id=1, source_target_pairs={{0,0},{1,32},{2,64},{3,480},{32,33},{33,65},{34,97},{35,1},{64,66}... | collective-permute-start | bytes 589832 | tf_op jit(solution)/shard_map/ppermute | solution.py:137
  8.9 0.7 reshape.271
  9.6 1.2 reduce-window.6
  10.9 0.1 copy.65
  11.1 0.1 copy.66
  11.3 0.1 copy.87
  11.5 1.1 copy.88
  12.6 1.2 convolution_convert_fusion
  13.9 0.7 pad_maximum_fusion.1
  14.5 0.7 copy-done.3
  15.2 12.8 %all-to-all-start = ((bf16[8,72,128]{2,1,0:T(8,128)(2,1)}), bf16[8,72,128]{2,1,0:T(8,128)(2,1)S(1)}, u32[]{:S(2)}, u32[]{:S(2)}) async-start(bf16[8,72,128]{2,1,0:T(8,128)(2,1)} %pad_maximum_fusion.1), calls=%async_computation | async-start | bytes 294912 | tf_op jit(solution)/shard_map/all_to_all | solution.py:153
  28.1 6.0 %all-to-all-done = bf16[8,72,128]{2,1,0:T(8,128)(2,1)S(1)} async-done(((bf16[8,72,128]{2,1,0:T(8,128)(2,1)}), bf16[8,72,128]{2,1,0:T(8,128)(2,1)S(1)}, u32[]{:S(2)}, u32[]{:S(2)}) %all-to-all-start) | async-done | bytes 147488 | tf_op jit(solution)/shard_map/all_to_all | solution.py:153
  34.1 0.2 reduce_window_sum.47
  34.4 0.5 convolution_bitcast_fusion
  35.0 0.2 slice_reduce_fusion
  35.2 0.7 broadcast_in_dim.36
  35.8 15.3 %all-to-all-start.1 = ((f32[4,72,128]{2,1,0:T(8,128)}), f32[4,72,128]{2,1,0:T(8,128)S(1)}, u32[]{:S(2)}, u32[]{:S(2)}) async-start(f32[4,72,128]{2,1,0:T(8,128)} %broadcast_in_dim.36), calls=%async_computation.1 | async-start | bytes 294912 | tf_op jit(solution)/shard_map/all_to_all | solution.py:174
  51.2 0.8 constant_dynamic-slice_fusion.1
  52.0 15.2 %all-to-all-done.1 = f32[4,72,128]{2,1,0:T(8,128)S(1)} async-done(((f32[4,72,128]{2,1,0:T(8,128)}), f32[4,72,128]{2,1,0:T(8,128)S(1)}, u32[]{:S(2)}, u32[]{:S(2)}) %all-to-all-start.1) | async-done | bytes 147488 | tf_op jit(solution)/shard_map/all_to_all | solution.py:174
  67.2 0.1 copy.75
  67.4 0.1 copy.77
  67.6 0.5 fusion
  68.2 0.1 fusion.17
  68.3 0.1 copy.78
  68.4 0.7 reshape.279
  69.2 6.4 %all-to-all-start.2 = ((bf16[8,64,128]{2,1,0:T(8,128)(2,1)}), bf16[8,64,128]{2,1,0:T(8,128)(2,1)S(1)}, u32[]{:S(2)}, u32[]{:S(2)}) async-start(bf16[8,64,128]{2,1,0:T(8,128)(2,1)} %reshape.279), calls=%async_computation.2 | async-start | bytes 262144 | tf_op jit(solution)/shard_map/all_to_all | solution.py:192
  75.7 0.6 convolution_bitcast_fusion.3
  76.3 6.4 %all-to-all-done.2 = bf16[8,64,128]{2,1,0:T(8,128)(2,1)S(1)} async-done(((bf16[8,64,128]{2,1,0:T(8,128)(2,1)}), bf16[8,64,128]{2,1,0:T(8,128)(2,1)S(1)}, u32[]{:S(2)}, u32[]{:S(2)}) %all-to-all-start.2) | async-done | bytes 131104 | tf_op jit(solution)/shard_map/all_to_all | solution.py:192
  82.7 0.1 copy.79
  82.9 0.3 multiply_reduce_fusion
  83.2 0.2 copy.84
  83.6 1.1 broadcast_in_dim.38
  84.7 3.5 %all-to-all-start.3 = ((bf16[4,272,512]{2,1,0:T(8,128)(2,1)}), bf16[4,272,512]{2,1,0:T(8,128)(2,1)S(1)}, u32[]{:S(2)}, u32[]{:S(2)}) async-start(bf16[4,272,512]{2,1,0:T(8,128)(2,1)} %broadcast_in_dim.38), calls=%async_computation.3 | async-start | bytes 2228224 | tf_op jit(solution)/shard_map/all_to_all | solution.py:204
  88.3 0.6 pad_add_fusion.at_ref
  88.9 0.6 dynamic-slice_bitcast_fusion
  89.5 13.3 %all-to-all-done.3.acts_ref = bf16[4,272,512]{2,1,0:T(8,128)(2,1)S(1)} async-done(((bf16[4,272,512]{2,1,0:T(8,128)(2,1)}), bf16[4,272,512]{2,1,0:T(8,128)(2,1)S(1)}, u32[]{:S(2)}, u32[]{:S(2)}) %all-to-all-start.3) | async-done | bytes 1114144 | tf_op jit(solution)/shard_map/all_to_all | solution.py:204
  103.0 0.8 reshape.288.tail_ref
  103.7 8.3 %all-gather.2.cloned.1.call-done = bf16[6144,512]{1,0:T(8,128)(2,1)} async-done(((bf16[192,512]{1,0:T(8,128)(2,1)}), bf16[6144,512]{1,0:T(8,128)(2,1)}) %all-gather.2.cloned.1.call-update) | async-done | bytes 6291472 | tf_op jit(solution)/shard_map/all_gather | solution.py:156
  112.1 4.3 %project.3 = bf16[272,384]{1,0:T(8,128)(2,1)} custom-call(s32[2]{0:T(128)} %pad_add_fusion.at_ref, bf16[4,272,512]{2,1,0:T(8,128)(2,1)} %copy-done.1, bf16[16,384,512]{2,1,0:T(8,128)(2,1)} %bitcast.123, bf16[16,384]{1,0:T(8,128)(2,1)} %reshape.288.tail_ref), custom_call_target="tpu_custom_call" | custom-call | tf_op jit(solution)/shard_map/project/pallas_call | solution.py:104
  116.4 4.7 %collective-permute-start.1 = (bf16[272,384]{1,0:T(8,128)(2,1)}, bf16[272,384]{1,0:T(8,128)(2,1)S(1)}, u32[]{:S(2)}, u32[]{:S(2)}) collective-permute-start(bf16[272,384]{1,0:T(8,128)(2,1)} %project.3), channel_id=1, source_target_pairs={{0,8},{4,12},{8,0},{12,4},{1,9},{5,13},{9,1},{13,5},{2,10},{6,14},... | collective-permute-start | bytes 626696 | tf_op jit(solution)/shard_map/ppermute | solution.py:213
  121.1 6.3 %project.2 = (bf16[272,384]{1,0:T(8,128)(2,1)}, bf16[272,384]{1,0:T(8,128)(2,1)}, bf16[272,384]{1,0:T(8,128)(2,1)}) custom-call(s32[2]{0:T(128)} %pad_add_fusion.at_ref, bf16[4,272,512]{2,1,0:T(8,128)(2,1)} %copy-done.1, bf16[16,384,512]{2,1,0:T(8,128)(2,1)} %bitcast.124, bf16[16,384]{1,0:T(8,128)(2,1)} %reshape.288.tail_ref), custom_call_target="tpu_custom_call" | custom-call | tf_op jit(solution)/shard_map/project/pallas_call | solution.py:104
  127.4 2.4 %collective-permute-start.2 = (bf16[272,384]{1,0:T(8,128)(2,1)}, bf16[272,384]{1,0:T(8,128)(2,1)S(1)}, u32[]{:S(2)}, u32[]{:S(2)}) collective-permute-start(bf16[272,384]{1,0:T(8,128)(2,1)} %get-tuple-element.9), channel_id=1, source_target_pairs={{0,4},{4,8},{8,12},{12,0},{1,5},{5,9},{9,13},{13,1},{2,6},{6,10},{... | collective-permute-start | bytes 626696 | tf_op jit(solution)/shard_map/ppermute | solution.py:213
  129.7 4.3 %collective-permute-start.3 = (bf16[272,384]{1,0:T(8,128)(2,1)}, bf16[272,384]{1,0:T(8,128)(2,1)S(1)}, u32[]{:S(2)}, u32[]{:S(2)}) collective-permute-start(bf16[272,384]{1,0:T(8,128)(2,1)} %get-tuple-element.10), channel_id=1, source_target_pairs={{0,12},{4,0},{8,4},{12,8},{1,13},{5,1},{9,5},{13,9},{2,14},{6,2},{... | collective-permute-start | bytes 626696 | tf_op jit(solution)/shard_map/ppermute | solution.py:213
  134.0 0.7 slice_bitcast_fusion.4
  134.8 2.2 %collective-permute-done.2 = bf16[272,384]{1,0:T(8,128)(2,1)S(1)} collective-permute-done((bf16[272,384]{1,0:T(8,128)(2,1)}, bf16[272,384]{1,0:T(8,128)(2,1)S(1)}, u32[]{:S(2)}, u32[]{:S(2)}) %collective-permute-start.2) | collective-permute-done | bytes 208928 | tf_op jit(solution)/shard_map/ppermute | solution.py:213
  137.0 1.0 collective-permute-done.3
  138.1 0.8 multiply_convert_fusion
  138.9 0.8 multiply_convert_fusion.3
  (76 shorter events, 1.7 us)
Async XLA Ops:
  7.2 68.5 %copy-start = (bf16[256,512]{1,0:T(8,128)(2,1)S(1)}, bf16[256,512]{1,0:T(8,128)(2,1)}, u32[]{:S(2)}) copy-start(bf16[256,512]{1,0:T(8,128)(2,1)} %param.7) | copy-start | bytes 786436
  7.2 104.9 %all-gather.2.cloned.1.call-start = ((), (), s32[]{:S(2)}) async-start(), calls=%async_computation.4 | async-start | bytes 6488064 | tf_op jit(solution)/shard_map/all_gather | solution.py:156
  7.2 7.3 %collective-permute-start = (bf16[192,512]{1,0:T(8,128)(2,1)}, bf16[192,512]{1,0:T(8,128)(2,1)S(1)}, u32[]{:S(2)}, u32[]{:S(2)}) collective-permute-start(bf16[192,512]{1,0:T(8,128)(2,1)} %bitcast.151), channel_id=1, source_target_pairs={{0,0},{1,32},{2,64},{3,480},{32,33},{33,65},{34,97},{35,1},{64,66}... | collective-permute-start | bytes 589832 | tf_op jit(solution)/shard_map/ppermute | solution.py:137
  14.5 0.7 copy-start.3
  15.2 18.8 %all-to-all-start = ((bf16[8,72,128]{2,1,0:T(8,128)(2,1)}), bf16[8,72,128]{2,1,0:T(8,128)(2,1)S(1)}, u32[]{:S(2)}, u32[]{:S(2)}) async-start(bf16[8,72,128]{2,1,0:T(8,128)(2,1)} %pad_maximum_fusion.1), calls=%async_computation | async-start | bytes 294912 | tf_op jit(solution)/shard_map/all_to_all | solution.py:153
  35.8 31.4 %all-to-all-start.1 = ((f32[4,72,128]{2,1,0:T(8,128)}), f32[4,72,128]{2,1,0:T(8,128)S(1)}, u32[]{:S(2)}, u32[]{:S(2)}) async-start(f32[4,72,128]{2,1,0:T(8,128)} %broadcast_in_dim.36), calls=%async_computation.1 | async-start | bytes 294912 | tf_op jit(solution)/shard_map/all_to_all | solution.py:174
  67.5 8.1 %copy-start.5 = (bf16[256,512]{1,0:T(8,128)(2,1)S(1)}, bf16[256,512]{1,0:T(8,128)(2,1)}, u32[]{:S(2)}) copy-start(bf16[256,512]{1,0:T(8,128)(2,1)} %param.9) | copy-start | bytes 786436
  69.2 13.5 %all-to-all-start.2 = ((bf16[8,64,128]{2,1,0:T(8,128)(2,1)}), bf16[8,64,128]{2,1,0:T(8,128)(2,1)S(1)}, u32[]{:S(2)}, u32[]{:S(2)}) async-start(bf16[8,64,128]{2,1,0:T(8,128)(2,1)} %reshape.279), calls=%async_computation.2 | async-start | bytes 262144 | tf_op jit(solution)/shard_map/all_to_all | solution.py:192
  82.9 0.7 copy-start.4
  84.7 18.0 %all-to-all-start.3 = ((bf16[4,272,512]{2,1,0:T(8,128)(2,1)}), bf16[4,272,512]{2,1,0:T(8,128)(2,1)S(1)}, u32[]{:S(2)}, u32[]{:S(2)}) async-start(bf16[4,272,512]{2,1,0:T(8,128)(2,1)} %broadcast_in_dim.38), calls=%async_computation.3 | async-start | bytes 2228224 | tf_op jit(solution)/shard_map/all_to_all | solution.py:204
  102.8 9.3 %copy-start.1 = (bf16[4,272,512]{2,1,0:T(8,128)(2,1)}, bf16[4,272,512]{2,1,0:T(8,128)(2,1)S(1)}, u32[]{:S(2)}) copy-start(bf16[4,272,512]{2,1,0:T(8,128)(2,1)S(1)} %all-to-all-done.3.acts_ref) | copy-start | bytes 3342340
  116.4 18.4 %collective-permute-start.1 = (bf16[272,384]{1,0:T(8,128)(2,1)}, bf16[272,384]{1,0:T(8,128)(2,1)S(1)}, u32[]{:S(2)}, u32[]{:S(2)}) collective-permute-start(bf16[272,384]{1,0:T(8,128)(2,1)} %project.3), channel_id=1, source_target_pairs={{0,8},{4,12},{8,0},{12,4},{1,9},{5,13},{9,1},{13,5},{2,10},{6,14},... | collective-permute-start | bytes 626696 | tf_op jit(solution)/shard_map/ppermute | solution.py:213
  127.4 11.5 %copy-start.2 = (bf16[272,384]{1,0:T(8,128)(2,1)S(1)}, bf16[272,384]{1,0:T(8,128)(2,1)}, u32[]{:S(2)}) copy-start(bf16[272,384]{1,0:T(8,128)(2,1)} %get-tuple-element.8) | copy-start | bytes 626692
  127.4 9.6 %collective-permute-start.2 = (bf16[272,384]{1,0:T(8,128)(2,1)}, bf16[272,384]{1,0:T(8,128)(2,1)S(1)}, u32[]{:S(2)}, u32[]{:S(2)}) collective-permute-start(bf16[272,384]{1,0:T(8,128)(2,1)} %get-tuple-element.9), channel_id=1, source_target_pairs={{0,4},{4,8},{8,12},{12,0},{1,5},{5,9},{9,13},{13,1},{2,6},{6,10},{... | collective-permute-start | bytes 626696 | tf_op jit(solution)/shard_map/ppermute | solution.py:213
  129.7 8.2 %collective-permute-start.3 = (bf16[272,384]{1,0:T(8,128)(2,1)}, bf16[272,384]{1,0:T(8,128)(2,1)S(1)}, u32[]{:S(2)}, u32[]{:S(2)}) collective-permute-start(bf16[272,384]{1,0:T(8,128)(2,1)} %get-tuple-element.10), channel_id=1, source_target_pairs={{0,12},{4,0},{8,4},{12,8},{1,13},{5,1},{9,5},{13,9},{2,14},{6,2},{... | collective-permute-start | bytes 626696 | tf_op jit(solution)/shard_map/ppermute | solution.py:213
Sparse Core Ops, SparseCore 0:
  15.4 96.6 all-gather.1

commit v6 on v5

v6 whole, which is shorter than its diff:
```python
import functools

import jax
import jax.numpy as jnp
from jax import lax
from jax.experimental import pallas as pl
from jax.experimental.pallas import tpu as pltpu
from jax.sharding import Mesh, PartitionSpec as P

H = 64
DH = 128
EPSILON = 1e-06
CTX = ("za", "zb", "core")
INNER = ("zb", "core")
TP = ("x", "y")
FLIGHT = 6
HIGH = lax.Precision.HIGHEST
BF16 = jnp.bfloat16
F32 = jnp.float32


def split3(x):
    hi = lax.reduce_precision(x, 8, 7)
    rest = x - hi
    mid = lax.reduce_precision(rest, 8, 7)
    low = rest - mid
    return jnp.stack([hi.astype(BF16), mid.astype(BF16), low.astype(BF16)])


def join3(parts):
    parts = parts.astype(F32)
    return parts[0] + (parts[1] + parts[2])


def tail_of(vector, width):
    flat = split3(vector).reshape(-1)
    return jnp.pad(flat, (0, 16 * width - flat.shape[0])).reshape(16, width)


def rows_of(tail, n):
    count = tail.shape[0]
    flat = tail.reshape(count, -1)[:, : 3 * n].reshape(count, 3, n)
    return jnp.sum(join3(jnp.moveaxis(flat, 1, 0)), axis=0)


def mixer(logs):
    count, heads = logs.shape
    upto = jnp.concatenate([jnp.zeros((1, heads), F32), jnp.cumsum(logs, axis=0)])
    before = jnp.arange(count)[None, :] < jnp.arange(count + 1)[:, None]
    gap = upto[:, None] - upto[None, 1:]
    factor = jnp.where(before[:, :, None], jnp.exp(jnp.minimum(gap, 0.0)), 0.0)
    return upto, factor


def z_step(y, core):
    return (0, 1, 2 - 4 * core, -1)[y]


def project_kernel(at_ref, acts_ref, weights_ref, tail_ref, out_ref, left, right, done, sems, out_sems):
    tokens = acts_ref.shape[1] - tail_ref.shape[0]
    ny = acts_ref.shape[0]
    chips, cores, share, _ = weights_ref.shape
    y = at_ref[0]
    copies = []
    for n in range(chips // ny):
        for i in range(ny):
            group = []
            if n == 0:
                group.append(pltpu.make_async_copy(acts_ref.at[i], left.at[i], sems.at[n, i, cores]))
            for c in range(cores):
                z = lax.rem(n * ny + y + chips + z_step(i, c), chips)
                part = right.at[n, i, pl.ds(c * share, share)]
                group.append(pltpu.make_async_copy(weights_ref.at[z, c], part, sems.at[n, i, c]))
            copies.append(group)
    for group in copies[:FLIGHT]:
        for copy in group:
            copy.start()
    m = 0
    leaving = []
    for n in range(chips // ny):
        total = None
        for i in range(ny):
            for copy in copies[m]:
                copy.wait()
            if m + FLIGHT < len(copies):
                for copy in copies[m + FLIGHT]:
                    copy.start()
            m += 1
            value = lax.dot_general(
                left[i, :tokens, :],
                right[n, i],
                (((1,), (1,)), ((), ())),
                preferred_element_type=F32,
            )
            total = value if total is None else total + value
        done[n, :tokens, :] = total.astype(BF16)
        done[n, tokens:, :] = tail_ref[...]
        leaving.append(pltpu.make_async_copy(done.at[n], out_ref.at[n], out_sems.at[n]))
        leaving[-1].start()
    for copy in leaving:
        copy.wait()


def project(acts, weights, tail, at):
    ny, rows, depth = acts.shape
    chips, cores, share, _ = weights.shape
    nx, cols = chips // ny, cores * share
    hbm = pl.BlockSpec(memory_space=pl.ANY)
    return pl.pallas_call(
        project_kernel,
        out_shape=jax.ShapeDtypeStruct((nx, rows, cols), BF16),
        grid_spec=pltpu.PrefetchScalarGridSpec(
            num_scalar_prefetch=1,
            grid=(),
            in_specs=[hbm, hbm, pl.BlockSpec(memory_space=pltpu.VMEM)],
            out_specs=hbm,
            scratch_shapes=[
                pltpu.VMEM(acts.shape, BF16),
                pltpu.VMEM((nx, ny, cols, depth), BF16),
                pltpu.VMEM((nx, rows, cols), BF16),
                pltpu.SemaphoreType.DMA((nx, ny, cores + 1)),
                pltpu.SemaphoreType.DMA((nx,)),
            ],
        ),
        name="project",
    )(at, acts, weights, tail)


def open_kernel(quads, keep_ref, keys_ref, values_ref, message_ref, across_ref, down_ref):
    tokens = keys_ref.shape[0]
    heads = keep_ref.shape[0]
    inner = message_ref.shape[0]
    each = DH // inner
    step = each // quads
    row = lax.broadcasted_iota(jnp.int32, (tokens, tokens), 0)
    col = lax.broadcasted_iota(jnp.int32, (tokens, tokens), 1)
    sums = (col <= row).astype(F32)
    keep = keep_ref[...]
    down = lax.dot_general(sums, keep, (((1,), (1,)), ((), ())), precision=HIGH, preferred_element_type=F32)
    across_ref[...] = lax.dot_general(
        keep, sums, (((1,), (1,)), ((), ())), precision=HIGH, preferred_element_type=F32
    )
    down_ref[...] = down
    last = down[tokens - 1 :, :]
    factor = jnp.exp(last - down)
    to = lax.broadcasted_iota(jnp.int32, (DH, DH), 0)
    of = lax.broadcasted_iota(jnp.int32, (DH, DH), 1)
    wanted = (to % each) // step * (inner * step) + to // each * step + to % step
    order = (of == wanted).astype(BF16)
    for h in range(heads):
        span = slice(h * DH, (h + 1) * DH)
        decayed = (keys_ref[:, span].astype(F32) * factor[:, h : h + 1]).astype(BF16)
        inc = lax.dot_general(
            decayed, values_ref[:, span], (((0,), (0,)), ((), ())), preferred_element_type=F32
        )
        inc = jnp.dot(order, inc.astype(BF16), preferred_element_type=F32).astype(BF16)
        for i in range(inner):
            message_ref[i, h * each : (h + 1) * each, :] = inc[i * each : (i + 1) * each, :]
    lane = lax.broadcasted_iota(jnp.int32, (8, DH), 1)
    line = lax.broadcasted_iota(jnp.int32, (8, DH), 0)
    logs = jnp.zeros((8, DH), F32)
    for h in range(heads):
        logs = jnp.where(lane == h, last[:, h : h + 1], logs)
    hi = logs.astype(BF16).astype(F32)
    mid = (logs - hi).astype(BF16).astype(F32)
    low = logs - hi - mid
    logs = jnp.where(line == 0, hi, jnp.where(line == 1, mid, jnp.where(line == 2, low, 0.0)))
    for i in range(inner):
        message_ref[i, heads * each :, :] = logs.astype(BF16)


def open_scan(log_keep, keys, values, quads, inner):
    heads, tokens = log_keep.shape
    vmem = pl.BlockSpec(memory_space=pltpu.VMEM)
    return pl.pallas_call(
        functools.partial(open_kernel, quads),
        out_shape=[
            jax.ShapeDtypeStruct((inner, heads * DH // inner + 8, DH), BF16),
            jax.ShapeDtypeStruct((heads, tokens), F32),
            jax.ShapeDtypeStruct((tokens, heads), F32),
        ],
        in_specs=[vmem] * 3,
        out_specs=[vmem] * 3,
        name="open_scan",
    )(log_keep, keys, values)


def per_device(queries, keys, values, log_keep, state_in, norm_gain, out_weight):
    tokens = queries.shape[0]
    heads = log_keep.shape[0]
    parts = lax.axis_size(CTX)
    quads, inner = lax.axis_size("za"), lax.axis_size(INNER)
    rows = DH // parts
    slab = heads * quads * rows
    nx, ny = lax.axis_size("x"), lax.axis_size("y")

    cores = lax.axis_size("core")
    chips = parts // cores
    swap = [
        (
            (z * cores + c) * ny + y,
            ((z + z_step(y, c)) % chips * cores + c) * ny + z % ny,
        )
        for z in range(chips)
        for c in range(cores)
        for y in range(ny)
    ]
    moved = lax.ppermute(out_weight.T, CTX + ("y",), swap)

    q = queries.reshape(tokens, heads, DH)
    k = keys.reshape(tokens, heads, DH)
    v = values.reshape(tokens, heads, DH)
    opener, within, within_down = open_scan(log_keep, keys, values, quads, inner)
    got = lax.all_to_all(opener, INNER, 0, 0, tiled=True)

    moved, opener = lax.optimization_barrier((moved, opener))
    gathered = lax.all_gather(moved, CTX, axis=0, tiled=True)
    cols = out_weight.shape[1] * parts // (nx * ny)
    gathered = gathered.reshape(chips, cores, cols // cores, out_weight.shape[0])

    causal = jnp.tril(jnp.ones((tokens, tokens), dtype=bool))
    spread = within[:, :, None] - within[:, None, :]
    decay = jnp.where(causal, jnp.exp(jnp.minimum(spread, 0.0)), 0.0)
    scores = jnp.einsum("shd,thd->hst", q, k, preferred_element_type=F32)
    weights = (scores * decay).astype(BF16)
    intra = jnp.einsum("hst,thd->shd", weights, v, preferred_element_type=F32)

    incs = got[:, :slab].astype(F32).reshape(inner, heads, -1)
    upto, mixing = mixer(join3(jnp.moveaxis(got[:, slab : slab + 3, :heads], 1, 0)))
    local = jnp.einsum("cjh,jhn->chn", mixing, incs, precision=HIGH)

    total_log = jnp.pad(split3(upto[inner]), ((0, 5), (0, DH - heads)))
    total = jnp.concatenate([local[inner].reshape(slab, DH).astype(BF16), total_log])
    totals = lax.all_to_all(
        jnp.broadcast_to(total[None], (quads,) + total.shape), "za", 0, 0, tiled=True
    ).astype(F32)
    after, across = mixer(join3(jnp.moveaxis(totals[:, slab : slab + 3, :heads], 1, 0)))
    first = lax.dynamic_index_in_dim(
        state_in.reshape(heads, quads, inner, rows, DH), lax.axis_index(INNER), 2, keepdims=False
    ).reshape(heads, -1)
    bounds = jnp.einsum(
        "cjh,jhn->chn", across, totals[:, :slab].reshape(quads, heads, -1), precision=HIGH
    )
    bounds = bounds + jnp.exp(after)[:, :, None] * first[None]
    quad = lax.axis_index("za")
    final = lax.dynamic_index_in_dim(
        bounds[quads].reshape(heads, quads, rows, DH), quad, 1, keepdims=False
    )
    opening = lax.dynamic_index_in_dim(bounds, quad, 0, keepdims=False)
    states = local[:inner] + jnp.exp(upto[:inner])[:, :, None] * opening[None]
    states = states.astype(BF16).reshape(inner, slab, DH)
    back = lax.all_to_all(states, INNER, 0, 0, tiled=True)
    start = back.reshape(inner, heads, quads, rows, DH).transpose(1, 2, 0, 3, 4)
    start = start.reshape(heads, DH, DH)

    inter = jnp.einsum("shd,hde->she", q, start, preferred_element_type=F32)
    inter = inter * jnp.exp(within_down)[:, :, None]
    attended = (intra + inter).reshape(tokens, heads * DH)
    squares = jnp.sum(attended * attended, axis=1)
    gained = attended * norm_gain

    message = jnp.concatenate([gained.astype(BF16), tail_of(squares, heads * DH)])
    message = jnp.broadcast_to(message[None], (ny,) + message.shape)
    acts = lax.all_to_all(message, "y", 0, 0, tiled=True)
    squares = rows_of(acts[:, tokens:], tokens)
    at = lax.axis_index("y").astype(jnp.int32).reshape(1)
    blocks = project(acts, gathered, tail_of(squares, cols), at)
    shares = lax.all_to_all(blocks, "x", 0, 0, tiled=True)
    squares = rows_of(shares[:, tokens:], tokens)
    scale = lax.rsqrt(squares / (H * DH) + EPSILON)[:, None]
    normed = (attended * scale * norm_gain).astype(BF16)
    layer_out = (jnp.sum(shares[:, :tokens].astype(F32), axis=0) * scale).astype(BF16)
    return (normed, final, layer_out)


def solution(mesh):
    fine = Mesh(mesh.devices.reshape(4, 4, 2, 4, 4), CTX + TP)
    return jax.shard_map(
        per_device,
        mesh=fine,
        in_specs=(
            P(CTX, TP),
            P(CTX, TP),
            P(CTX, TP),
            P(TP, CTX),
            P(TP, None, None),
            P(TP),
            P(TP, CTX),
        ),
        out_specs=(P(CTX, TP), P(TP, CTX, None), P(CTX, TP)),
        check_vma=False,
    )
```

time: 149 us -> 138 us (0.926); the launches traced: 147 us -> 138 us
  starting transfers between devices: 51.1 us -> 41.9 us
  waiting for transfers between devices: 52.4 us -> 59.9 us
  local copies, waits for them, and re-layouts: 10.1 us -> 7.2 us
  other arithmetic: 4.86 us -> 2.43 us
    all_to_all x0 -> x1, waiting for transfers between devices: none -> 11.7 us  [per_device(): shares = lax.all_to_all(blocks, 'x', 0, 0, tiled=True)]
    ppermute x4 -> x1, starting transfers between devices: 13 us -> 1.72 us  [per_device(): moved = lax.ppermute(out_weight.T, CTX + ('y',), swap)]
    all_to_all x0 -> x1, starting transfers between devices: none -> 3.62 us  [per_device(): shares = lax.all_to_all(blocks, 'x', 0, 0, tiled=True)]
    all_to_all x1, starting transfers between devices: 15.3 us -> 12 us  [per_device(): lax.all_to_all(jnp.broadcast_to(total[None], (quads,) + total.shape), 'za...]
    ppermute x4 -> x1, waiting for transfers between devices: 3.16 us -> 0.01 us  [per_device(): moved = lax.ppermute(out_weight.T, CTX + ('y',), swap)]
    all_to_all x1, starting transfers between devices: 12.8 us -> 15.2 us  [per_device(): got = lax.all_to_all(opener, INNER, 0, 0, tiled=True)]
    all_to_all x1, waiting for transfers between devices: 15.2 us -> 13.1 us  [per_device(): lax.all_to_all(jnp.broadcast_to(total[None], (quads,) + total.shape), 'za...]
    another operation x4 -> x0, other arithmetic: 1.85 us -> none
  transfers between devices with their start and end apart: 9 -> 7, of which waited for: 7 -> 6; matrix products, arithmetic and copies ran while one was open for 11% -> 6% of each run, Pallas kernels for 4% -> 2%
where the time goes in v6:
time: 138 us
  waiting for transfers between devices  59.9 us (43%)
  starting transfers between devices  41.9 us (30%)
  between operations  14.4 us (10%)
  Pallas kernels  10.1 us (7%)
  local copies, waits for them, and re-layouts  7.2 us (5%)
  other arithmetic  2.43 us (2%)
  matrix products  1.77 us (1%)
    all_to_all x1, starting transfers between devices, per_device(): got = lax.all_to_all(opener, INNER, 0, 0, tiled=True)  15.2 us
    all_to_all x1, waiting for transfers between devices, per_device(): acts = lax.all_to_all(message, 'y', 0, 0, tiled=True)  14.3 us
    all_to_all x1, waiting for transfers between devices, per_device(): lax.all_to_all(jnp.broadcast_to(total[None], (quads,) + total.shape), 'za...  13.1 us
    all_to_all x1, starting transfers between devices, per_device(): lax.all_to_all(jnp.broadcast_to(total[None], (quads,) + total.shape), 'za...  12 us
    all_to_all x1, waiting for transfers between devices, per_device(): shares = lax.all_to_all(blocks, 'x', 0, 0, tiled=True)  11.7 us
    all_gather x1, waiting for transfers between devices, per_device(): gathered = lax.all_gather(moved, CTX, axis=0, tiled=True)  9.71 us
    pallas_call x1, Pallas kernels, project(): pl.pallas_call(project_kernel, out_shape=jax.ShapeDtypeStruct((nx, rows,...  6.96 us
    all_to_all x1, waiting for transfers between devices, per_device(): back = lax.all_to_all(states, INNER, 0, 0, tiled=True)  5.84 us
  transfers between devices with their start and end apart: 7, of which 6 were waited for; matrix products, arithmetic and copies ran while one was open for 6% of the time, Pallas kernels for 2%

profile of v6, /device:TPU:1, one launch (start us, length us, event | category | flops | bytes accessed | tf_op | source)
XLA Modules:
  0.0 137.7 jit_solution(6467896221038610232)
XLA Ops:
  7.2 1.7 %collective-permute-start = (bf16[192,512]{1,0:T(8,128)(2,1)}, bf16[192,512]{1,0:T(8,128)(2,1)S(1)}, u32[]{:S(2)}, u32[]{:S(2)}) collective-permute-start(bf16[192,512]{1,0:T(8,128)(2,1)} %bitcast.95), channel_id=1, source_target_pairs={{0,0},{1,32},{2,64},{3,480},{16,16},{17,48},{18,464},{19,496},{32,... | collective-permute-start | bytes 589832 | tf_op jit(solution)/shard_map/ppermute | solution.py:208
  8.9 3.2 %open_scan.1 = (bf16[8,72,128]{2,1,0:T(8,128)(2,1)}, f32[4,256]{1,0:T(4,128)}, f32[256,4]{1,0:T(8,128)}) custom-call(f32[4,256]{1,0:T(4,128)} %keep_ref.1, bf16[256,512]{1,0:T(8,128)(2,1)} %keys_ref.1, bf16[256,512]{1,0:T(8,128)(2,1)} %values_ref.1), custom_call_target="tpu_custom_call" | custom-call | tf_op jit(solution)/shard_map/open_scan/pallas_call | solution.py:175
  12.1 0.7 copy-done.4
  12.8 15.2 %all-to-all-start = ((bf16[8,72,128]{2,1,0:T(8,128)(2,1)}), bf16[8,72,128]{2,1,0:T(8,128)(2,1)S(1)}, u32[]{:S(2)}, u32[]{:S(2)}) async-start(bf16[8,72,128]{2,1,0:T(8,128)(2,1)} %get-tuple-element.8), calls=%async_computation | async-start | bytes 294912 | tf_op jit(solution)/shard_map/all_to_all | solution.py:214
  28.1 0.8 constant_dynamic-slice_fusion.1
  28.9 5.2 %all-to-all-done = bf16[8,72,128]{2,1,0:T(8,128)(2,1)S(1)} async-done(((bf16[8,72,128]{2,1,0:T(8,128)(2,1)}), bf16[8,72,128]{2,1,0:T(8,128)(2,1)S(1)}, u32[]{:S(2)}, u32[]{:S(2)}) %all-to-all-start) | async-done | bytes 147488 | tf_op jit(solution)/shard_map/all_to_all | solution.py:214
  34.0 0.1 copy.56
  34.1 0.2 reduce_window_sum.22
  34.3 0.1 concatenate.12
  34.4 0.1 reduce-precision_convert_fusion.1
  34.5 0.1 pad_maximum_fusion.3
  34.5 0.1 copy.74
  34.7 0.5 convolution_bitcast_fusion
  35.2 0.1 fusion.26
  35.3 0.6 broadcast_in_dim.30
  36.0 12.0 %all-to-all-start.1 = ((bf16[4,72,128]{2,1,0:T(8,128)(2,1)}), bf16[4,72,128]{2,1,0:T(8,128)(2,1)S(1)}, u32[]{:S(2)}, u32[]{:S(2)}) async-start(bf16[4,72,128]{2,1,0:T(8,128)(2,1)} %broadcast_in_dim.30), calls=%async_computation.1 | async-start | bytes 147456 | tf_op jit(solution)/shard_map/all_to_all | solution.py:234
  48.0 0.1 slice_exponential_fusion
  48.1 13.1 %all-to-all-done.1 = bf16[4,72,128]{2,1,0:T(8,128)(2,1)S(1)} async-done(((bf16[4,72,128]{2,1,0:T(8,128)(2,1)}), bf16[4,72,128]{2,1,0:T(8,128)(2,1)S(1)}, u32[]{:S(2)}, u32[]{:S(2)}) %all-to-all-start.1) | async-done | bytes 73760 | tf_op jit(solution)/shard_map/all_to_all | solution.py:234
  61.2 0.1 copy.60
  61.3 0.1 concatenate.14.clone
  61.4 0.1 copy.62
  61.5 0.4 fusion
  61.9 0.1 fusion.56
  62.1 0.1 fusion.19
  62.2 0.1 copy.63
  62.3 0.7 reshape.190
  63.0 5.4 %all-to-all-start.2 = ((bf16[8,64,128]{2,1,0:T(8,128)(2,1)}), bf16[8,64,128]{2,1,0:T(8,128)(2,1)S(1)}, u32[]{:S(2)}, u32[]{:S(2)}) async-start(bf16[8,64,128]{2,1,0:T(8,128)(2,1)} %reshape.190), calls=%async_computation.2 | async-start | bytes 262144 | tf_op jit(solution)/shard_map/all_to_all | solution.py:252
  68.4 0.1 copy.72
  68.6 0.1 copy.68
  68.8 0.6 convolution_bitcast_fusion.3
  69.3 5.8 %all-to-all-done.2 = bf16[8,64,128]{2,1,0:T(8,128)(2,1)S(1)} async-done(((bf16[8,64,128]{2,1,0:T(8,128)(2,1)}), bf16[8,64,128]{2,1,0:T(8,128)(2,1)S(1)}, u32[]{:S(2)}, u32[]{:S(2)}) %all-to-all-start.2) | async-done | bytes 131104 | tf_op jit(solution)/shard_map/all_to_all | solution.py:252
  75.2 0.1 copy.64
  75.3 0.3 multiply_reduce_fusion
  75.7 0.2 copy.70
  76.0 0.1 copy-done.6
  76.1 1.1 broadcast_in_dim.32
  77.2 3.9 %all-to-all-start.3 = ((bf16[4,272,512]{2,1,0:T(8,128)(2,1)}), bf16[4,272,512]{2,1,0:T(8,128)(2,1)S(1)}, u32[]{:S(2)}, u32[]{:S(2)}) async-start(bf16[4,272,512]{2,1,0:T(8,128)(2,1)} %broadcast_in_dim.32), calls=%async_computation.3 | async-start | bytes 2228224 | tf_op jit(solution)/shard_map/all_to_all | solution.py:264
  81.1 14.3 %all-to-all-done.3.acts_ref = bf16[4,272,512]{2,1,0:T(8,128)(2,1)S(1)} async-done(((bf16[4,272,512]{2,1,0:T(8,128)(2,1)}), bf16[4,272,512]{2,1,0:T(8,128)(2,1)S(1)}, u32[]{:S(2)}, u32[]{:S(2)}) %all-to-all-start.3) | async-done | bytes 1114144 | tf_op jit(solution)/shard_map/all_to_all | solution.py:264
  95.4 0.1 copy.77
  95.6 0.8 reshape.200.tail_ref
  96.4 9.7 %all-gather.2.cloned.1.call-done = bf16[6144,512]{1,0:T(8,128)(2,1)} async-done(((bf16[192,512]{1,0:T(8,128)(2,1)}), bf16[6144,512]{1,0:T(8,128)(2,1)}) %all-gather.2.cloned.1.call-update) | async-done | bytes 6291472 | tf_op jit(solution)/shard_map/all_gather | solution.py:217
  106.1 7.0 %project.1 = bf16[4,272,384]{2,1,0:T(8,128)(2,1)} custom-call(s32[1]{0:T(128)} %bitcast.14.at_ref, bf16[4,272,512]{2,1,0:T(8,128)(2,1)} %copy-done.1, bf16[16,2,192,512]{3,2,1,0:T(8,128)(2,1)} %bitcast.79, bf16[16,384]{1,0:T(8,128)(2,1)} %reshape.200.tail_ref), custom_call_target="tpu_custom_call" | custom-call | tf_op jit(solution)/shard_map/project/pallas_call | solution.py:109
  113.1 3.6 %all-to-all-start.4 = ((bf16[4,272,384]{2,1,0:T(8,128)(2,1)}), bf16[4,272,384]{2,1,0:T(8,128)(2,1)S(1)}, u32[]{:S(2)}, u32[]{:S(2)}) async-start(bf16[4,272,384]{2,1,0:T(8,128)(2,1)} %project.1), calls=%async_computation.4 | async-start | bytes 1671168 | tf_op jit(solution)/shard_map/all_to_all | solution.py:268
  116.7 0.6 dynamic-slice_bitcast_fusion
  117.3 11.7 %all-to-all-done.4 = bf16[4,272,384]{2,1,0:T(8,128)(2,1)S(1)} async-done(((bf16[4,272,384]{2,1,0:T(8,128)(2,1)}), bf16[4,272,384]{2,1,0:T(8,128)(2,1)S(1)}, u32[]{:S(2)}, u32[]{:S(2)}) %all-to-all-start.4) | async-done | bytes 835616 | tf_op jit(solution)/shard_map/all_to_all | solution.py:268
  129.1 0.8 multiply_convert_fusion
  130.0 0.1 convert_reduce_fusion
  130.1 0.8 multiply_convert_fusion.2
  (57 shorter events, 0.7 us)
Async XLA Ops:
  7.2 61.6 %copy-start = (bf16[256,512]{1,0:T(8,128)(2,1)S(1)}, bf16[256,512]{1,0:T(8,128)(2,1)}, u32[]{:S(2)}) copy-start(bf16[256,512]{1,0:T(8,128)(2,1)} %param.7) | copy-start | bytes 786436
  7.2 98.9 %all-gather.2.cloned.1.call-start = ((), (), s32[]{:S(2)}) async-start(), calls=%async_computation.5 | async-start | bytes 6488064 | tf_op jit(solution)/shard_map/all_gather | solution.py:217
  7.2 4.9 %collective-permute-start = (bf16[192,512]{1,0:T(8,128)(2,1)}, bf16[192,512]{1,0:T(8,128)(2,1)S(1)}, u32[]{:S(2)}, u32[]{:S(2)}) collective-permute-start(bf16[192,512]{1,0:T(8,128)(2,1)} %bitcast.95), channel_id=1, source_target_pairs={{0,0},{1,32},{2,64},{3,480},{16,16},{17,48},{18,464},{19,496},{32,... | collective-permute-start | bytes 589832 | tf_op jit(solution)/shard_map/ppermute | solution.py:208
  12.1 0.7 copy-start.4
  12.8 21.2 %all-to-all-start = ((bf16[8,72,128]{2,1,0:T(8,128)(2,1)}), bf16[8,72,128]{2,1,0:T(8,128)(2,1)S(1)}, u32[]{:S(2)}, u32[]{:S(2)}) async-start(bf16[8,72,128]{2,1,0:T(8,128)(2,1)} %get-tuple-element.8), calls=%async_computation | async-start | bytes 294912 | tf_op jit(solution)/shard_map/all_to_all | solution.py:214
  36.0 32.5 %copy-start.2 = (bf16[256,512]{1,0:T(8,128)(2,1)S(1)}, bf16[256,512]{1,0:T(8,128)(2,1)}, u32[]{:S(2)}) copy-start(bf16[256,512]{1,0:T(8,128)(2,1)} %values_ref.1) | copy-start | bytes 786436
  36.0 25.2 %all-to-all-start.1 = ((bf16[4,72,128]{2,1,0:T(8,128)(2,1)}), bf16[4,72,128]{2,1,0:T(8,128)(2,1)S(1)}, u32[]{:S(2)}, u32[]{:S(2)}) async-start(bf16[4,72,128]{2,1,0:T(8,128)(2,1)} %broadcast_in_dim.30), calls=%async_computation.1 | async-start | bytes 147456 | tf_op jit(solution)/shard_map/all_to_all | solution.py:234
  61.5 7.1 %copy-start.5 = (f32[256,4]{1,0:T(8,128)S(1)}, f32[256,4]{1,0:T(8,128)}, u32[]{:S(2)}) copy-start(f32[256,4]{1,0:T(8,128)} %get-tuple-element.9) | copy-start | bytes 12292
  62.0 6.7 %copy-start.3 = (bf16[256,512]{1,0:T(8,128)(2,1)S(1)}, bf16[256,512]{1,0:T(8,128)(2,1)}, u32[]{:S(2)}) copy-start(bf16[256,512]{1,0:T(8,128)(2,1)} %keys_ref.1) | copy-start | bytes 786436
  62.1 6.7 %copy-start.7 = (f32[4,256]{1,0:T(4,128)S(1)}, f32[4,256]{1,0:T(4,128)}, u32[]{:S(2)}) copy-start(f32[4,256]{1,0:T(4,128)} %get-tuple-element.7) | copy-start | bytes 12292
  63.0 12.2 %all-to-all-start.2 = ((bf16[8,64,128]{2,1,0:T(8,128)(2,1)}), bf16[8,64,128]{2,1,0:T(8,128)(2,1)S(1)}, u32[]{:S(2)}, u32[]{:S(2)}) async-start(bf16[8,64,128]{2,1,0:T(8,128)(2,1)} %reshape.190), calls=%async_computation.2 | async-start | bytes 262144 | tf_op jit(solution)/shard_map/all_to_all | solution.py:252
  75.3 0.7 copy-start.6
  77.2 18.2 %all-to-all-start.3 = ((bf16[4,272,512]{2,1,0:T(8,128)(2,1)}), bf16[4,272,512]{2,1,0:T(8,128)(2,1)S(1)}, u32[]{:S(2)}, u32[]{:S(2)}) async-start(bf16[4,272,512]{2,1,0:T(8,128)(2,1)} %broadcast_in_dim.32), calls=%async_computation.3 | async-start | bytes 2228224 | tf_op jit(solution)/shard_map/all_to_all | solution.py:264
  95.4 10.7 %copy-start.1 = (bf16[4,272,512]{2,1,0:T(8,128)(2,1)}, bf16[4,272,512]{2,1,0:T(8,128)(2,1)S(1)}, u32[]{:S(2)}) copy-start(bf16[4,272,512]{2,1,0:T(8,128)(2,1)S(1)} %all-to-all-done.3.acts_ref) | copy-start | bytes 3342340
  113.1 16.0 %all-to-all-start.4 = ((bf16[4,272,384]{2,1,0:T(8,128)(2,1)}), bf16[4,272,384]{2,1,0:T(8,128)(2,1)S(1)}, u32[]{:S(2)}, u32[]{:S(2)}) async-start(bf16[4,272,384]{2,1,0:T(8,128)(2,1)} %project.1), calls=%async_computation.4 | async-start | bytes 1671168 | tf_op jit(solution)/shard_map/all_to_all | solution.py:268
Sparse Core Ops, SparseCore 0:
  13.0 93.1 all-gather.1

commit v7 on v6

--- a/solution.py
+++ b/solution.py
@@ -32,9 +32,9 @@
     return parts[0] + (parts[1] + parts[2])
 
 
-def tail_of(vector, width):
+def tail_of(vector, rows, width):
     flat = split3(vector).reshape(-1)
-    return jnp.pad(flat, (0, 16 * width - flat.shape[0])).reshape(16, width)
+    return jnp.pad(flat, (0, rows * width - flat.shape[0])).reshape(rows, width)
 
 
 def rows_of(tail, n):
@@ -56,8 +56,8 @@
     return (0, 1, 2 - 4 * core, -1)[y]
 
 
-def project_kernel(at_ref, acts_ref, weights_ref, tail_ref, out_ref, left, right, done, sems, out_sems):
-    tokens = acts_ref.shape[1] - tail_ref.shape[0]
+def project_kernel(at_ref, acts_ref, weights_ref, scale_ref, out_ref, left, right, done, sems, out_sems):
+    tokens = scale_ref.shape[0]
     ny = acts_ref.shape[0]
     chips, cores, share, _ = weights_ref.shape
     y = at_ref[0]
@@ -66,7 +66,7 @@
         for i in range(ny):
             group = []
             if n == 0:
-                group.append(pltpu.make_async_copy(acts_ref.at[i], left.at[i], sems.at[n, i, cores]))
+                group.append(pltpu.make_async_copy(acts_ref.at[i, pl.ds(0, tokens)], left.at[i], sems.at[n, i, cores]))
             for c in range(cores):
                 z = lax.rem(n * ny + y + chips + z_step(i, c), chips)
                 part = right.at[n, i, pl.ds(c * share, share)]
@@ -87,22 +87,22 @@
                     copy.start()
             m += 1
             value = lax.dot_general(
-                left[i, :tokens, :],
+                left[i],
                 right[n, i],
                 (((1,), (1,)), ((), ())),
                 preferred_element_type=F32,
             )
             total = value if total is None else total + value
-        done[n, :tokens, :] = total.astype(BF16)
-        done[n, tokens:, :] = tail_ref[...]
+        done[n] = (total * scale_ref[...]).astype(BF16)
         leaving.append(pltpu.make_async_copy(done.at[n], out_ref.at[n], out_sems.at[n]))
         leaving[-1].start()
     for copy in leaving:
         copy.wait()
 
 
-def project(acts, weights, tail, at):
-    ny, rows, depth = acts.shape
+def project(acts, weights, scale, at):
+    ny, _, depth = acts.shape
+    rows = scale.shape[0]
     chips, cores, share, _ = weights.shape
     nx, cols = chips // ny, cores * share
     hbm = pl.BlockSpec(memory_space=pl.ANY)
@@ -115,7 +115,7 @@
             in_specs=[hbm, hbm, pl.BlockSpec(memory_space=pltpu.VMEM)],
             out_specs=hbm,
             scratch_shapes=[
-                pltpu.VMEM(acts.shape, BF16),
+                pltpu.VMEM((ny, rows, depth), BF16),
                 pltpu.VMEM((nx, ny, cols, depth), BF16),
                 pltpu.VMEM((nx, rows, cols), BF16),
                 pltpu.SemaphoreType.DMA((nx, ny, cores + 1)),
@@ -123,7 +123,7 @@
             ],
         ),
         name="project",
-    )(at, acts, weights, tail)
+    )(at, acts, weights, scale)
 
 
 def open_kernel(quads, keep_ref, keys_ref, values_ref, message_ref, across_ref, down_ref):
@@ -259,17 +259,17 @@
     squares = jnp.sum(attended * attended, axis=1)
     gained = attended * norm_gain
 
-    message = jnp.concatenate([gained.astype(BF16), tail_of(squares, heads * DH)])
+    message = jnp.concatenate([gained.astype(BF16), tail_of(squares, 16, heads * DH)])
     message = jnp.broadcast_to(message[None], (ny,) + message.shape)
     acts = lax.all_to_all(message, "y", 0, 0, tiled=True)
     squares = rows_of(acts[:, tokens:], tokens)
+    mine = tail_of(squares, 8, DH)
+    each = lax.all_to_all(jnp.broadcast_to(mine[None], (nx,) + mine.shape), "x", 0, 0, tiled=True)
+    scale = lax.rsqrt(rows_of(each, tokens) / (H * DH) + EPSILON)[:, None]
+    normed = (attended * scale * norm_gain).astype(BF16)
     at = lax.axis_index("y").astype(jnp.int32).reshape(1)
-    blocks = project(acts, gathered, tail_of(squares, cols), at)
-    shares = lax.all_to_all(blocks, "x", 0, 0, tiled=True)
-    squares = rows_of(shares[:, tokens:], tokens)
-    scale = lax.rsqrt(squares / (H * DH) + EPSILON)[:, None]
-    normed = (attended * scale * norm_gain).astype(BF16)
-    layer_out = (jnp.sum(shares[:, :tokens].astype(F32), axis=0) * scale).astype(BF16)
+    shares = lax.all_to_all(project(acts, gathered, scale, at), "x", 0, 0, tiled=True)
+    layer_out = jnp.sum(shares.astype(F32), axis=0).astype(BF16)
     return (normed, final, layer_out)
 
 

time: 138 us -> 137 us (level); the launches traced: 138 us -> 135 us
  waiting for transfers between devices: 59.9 us -> 39 us
  blocking collectives: 0 us -> 17.6 us
    all_to_all x0 -> x1, blocking collectives: none -> 17.6 us  [per_device(): acts = lax.all_to_all(message, 'y', 0, 0, tiled=True)]
    all_to_all x2, waiting for transfers between devices: 26.1 us -> 13.1 us  [the longest x1 8.87 us: per_device(): lax.all_to_all(project(acts, gathered, scale, at), 'x', 0, 0, tiled=True)]
    all_gather x1, waiting for transfers between devices: 9.71 us -> 1.89 us  [per_device(): gathered = lax.all_gather(moved, CTX, axis=0, tiled=True)]
  transfers between devices with their start and end apart: 7 -> 7, of which waited for: 6 -> 6; matrix products, arithmetic and copies ran while one was open for 6% -> 7% of each run, Pallas kernels for 2% -> 2%
where the time goes in v7:
time: 137 us; the launch traced here: 135 us
  starting transfers between devices  42.4 us (31%)
  waiting for transfers between devices  39 us (28%)
  blocking collectives  17.6 us (13%)
  between operations  14.4 us (11%)
  Pallas kernels  10.3 us (8%)
  local copies, waits for them, and re-layouts  6.96 us (5%)
  other arithmetic  2.37 us (2%)
  matrix products  1.77 us (1%)
    all_to_all x1, blocking collectives, per_device(): acts = lax.all_to_all(message, 'y', 0, 0, tiled=True)  17.6 us
    all_to_all x1, starting transfers between devices, per_device(): got = lax.all_to_all(opener, INNER, 0, 0, tiled=True)  15.2 us
    all_to_all x1, waiting for transfers between devices, per_device(): lax.all_to_all(jnp.broadcast_to(total[None], (quads,) + total.shape), 'za...  13.1 us
    all_to_all x1, starting transfers between devices, per_device(): lax.all_to_all(jnp.broadcast_to(total[None], (quads,) + total.shape), 'za...  12 us
    all_to_all x1, waiting for transfers between devices, per_device(): lax.all_to_all(project(acts, gathered, scale, at), 'x', 0, 0, tiled=True)  8.87 us
    pallas_call x1, Pallas kernels, project(): pl.pallas_call(project_kernel, out_shape=jax.ShapeDtypeStruct((nx, rows,...  7.14 us
    all_to_all x1, waiting for transfers between devices, per_device(): back = lax.all_to_all(states, INNER, 0, 0, tiled=True)  5.73 us
    all_to_all x1, starting transfers between devices, per_device(): back = lax.all_to_all(states, INNER, 0, 0, tiled=True)  5.42 us
  transfers between devices with their start and end apart: 7, of which 6 were waited for; matrix products, arithmetic and copies ran while one was open for 7% of the time, Pallas kernels for 2%

profile of v7, /device:TPU:1, one launch (start us, length us, event | category | flops | bytes accessed | tf_op | source)
XLA Modules:
  0.0 134.8 jit_solution(14740597629184919875)
XLA Ops:
  7.2 1.7 %collective-permute-start = (bf16[192,512]{1,0:T(8,128)(2,1)}, bf16[192,512]{1,0:T(8,128)(2,1)S(1)}, u32[]{:S(2)}, u32[]{:S(2)}) collective-permute-start(bf16[192,512]{1,0:T(8,128)(2,1)} %bitcast.101), channel_id=1, source_target_pairs={{0,0},{1,32},{2,64},{3,480},{16,16},{17,48},{18,464},{19,496},{32,... | collective-permute-start | bytes 589832 | tf_op jit(solution)/shard_map/ppermute | solution.py:208
  8.9 3.2 %open_scan.1 = (bf16[8,72,128]{2,1,0:T(8,128)(2,1)}, f32[4,256]{1,0:T(4,128)}, f32[256,4]{1,0:T(8,128)}) custom-call(f32[4,256]{1,0:T(4,128)} %keep_ref.1, bf16[256,512]{1,0:T(8,128)(2,1)} %keys_ref.1, bf16[256,512]{1,0:T(8,128)(2,1)} %values_ref.1), custom_call_target="tpu_custom_call" | custom-call | tf_op jit(solution)/shard_map/open_scan/pallas_call | solution.py:175
  12.1 0.7 copy-done.4
  12.8 15.2 %all-to-all-start = ((bf16[8,72,128]{2,1,0:T(8,128)(2,1)}), bf16[8,72,128]{2,1,0:T(8,128)(2,1)S(1)}, u32[]{:S(2)}, u32[]{:S(2)}) async-start(bf16[8,72,128]{2,1,0:T(8,128)(2,1)} %get-tuple-element.8), calls=%async_computation | async-start | bytes 294912 | tf_op jit(solution)/shard_map/all_to_all | solution.py:214
  28.1 0.8 constant_dynamic-slice_fusion.1
  28.9 5.2 %all-to-all-done = bf16[8,72,128]{2,1,0:T(8,128)(2,1)S(1)} async-done(((bf16[8,72,128]{2,1,0:T(8,128)(2,1)}), bf16[8,72,128]{2,1,0:T(8,128)(2,1)S(1)}, u32[]{:S(2)}, u32[]{:S(2)}) %all-to-all-start) | async-done | bytes 147488 | tf_op jit(solution)/shard_map/all_to_all | solution.py:214
  34.1 0.1 copy.58
  34.2 0.2 reduce_window_sum.22
  34.4 0.1 concatenate.12
  34.4 0.1 reduce-precision_convert_fusion.1
  34.5 0.1 pad_maximum_fusion.3
  34.6 0.1 copy.77
  34.7 0.5 convolution_bitcast_fusion
  35.2 0.1 fusion.26
  35.3 0.6 broadcast_in_dim.34
  36.0 12.0 %all-to-all-start.1 = ((bf16[4,72,128]{2,1,0:T(8,128)(2,1)}), bf16[4,72,128]{2,1,0:T(8,128)(2,1)S(1)}, u32[]{:S(2)}, u32[]{:S(2)}) async-start(bf16[4,72,128]{2,1,0:T(8,128)(2,1)} %broadcast_in_dim.34), calls=%async_computation.1 | async-start | bytes 147456 | tf_op jit(solution)/shard_map/all_to_all | solution.py:234
  48.0 0.1 slice_exponential_fusion
  48.1 13.1 %all-to-all-done.1 = bf16[4,72,128]{2,1,0:T(8,128)(2,1)S(1)} async-done(((bf16[4,72,128]{2,1,0:T(8,128)(2,1)}), bf16[4,72,128]{2,1,0:T(8,128)(2,1)S(1)}, u32[]{:S(2)}, u32[]{:S(2)}) %all-to-all-start.1) | async-done | bytes 73760 | tf_op jit(solution)/shard_map/all_to_all | solution.py:234
  61.2 0.1 copy.62
  61.3 0.1 copy.64
  61.4 0.1 concatenate.14.clone
  61.5 0.4 fusion
  61.9 0.1 fusion.56
  62.1 0.1 fusion.19
  62.2 0.1 copy.65
  62.3 0.7 reshape.201
  63.0 5.4 %all-to-all-start.2 = ((bf16[8,64,128]{2,1,0:T(8,128)(2,1)}), bf16[8,64,128]{2,1,0:T(8,128)(2,1)S(1)}, u32[]{:S(2)}, u32[]{:S(2)}) async-start(bf16[8,64,128]{2,1,0:T(8,128)(2,1)} %reshape.201), calls=%async_computation.2 | async-start | bytes 262144 | tf_op jit(solution)/shard_map/all_to_all | solution.py:252
  68.4 0.1 copy.75
  68.6 0.1 copy.70
  68.8 0.6 convolution_bitcast_fusion.3
  69.3 5.7 %all-to-all-done.2 = bf16[8,64,128]{2,1,0:T(8,128)(2,1)S(1)} async-done(((bf16[8,64,128]{2,1,0:T(8,128)(2,1)}), bf16[8,64,128]{2,1,0:T(8,128)(2,1)S(1)}, u32[]{:S(2)}, u32[]{:S(2)}) %all-to-all-start.2) | async-done | bytes 131104 | tf_op jit(solution)/shard_map/all_to_all | solution.py:252
  75.1 0.1 copy.66
  75.2 0.3 multiply_reduce_fusion
  75.5 0.2 copy.72
  75.8 0.1 copy-done.6
  76.0 0.1 broadcast_in_dim.40
  76.1 17.6 %all_to_all.30.acts_ref = bf16[4,272,512]{2,1,0:T(8,128)(2,1)S(1)} all-to-all(bf16[4,272,512]{2,1,0:T(8,128)(2,1)S(1)} %broadcast_in_dim.40), channel_id=1, replica_groups=mesh['za'=4,'zb'=4,'core'=2,'x'=4,'y'=4] {'y'}, dimensions={0} | all-to-all | bytes 2228224 | tf_op jit(solution)/shard_map/all_to_all | solution.py:264
  93.9 0.8 broadcast_in_dim.42
  94.7 4.0 %all-to-all-start.4 = ((bf16[4,8,128]{2,1,0:T(8,128)(2,1)}), bf16[4,8,128]{2,1,0:T(8,128)(2,1)S(1)}, u32[]{:S(2)}, u32[]{:S(2)}) async-start(bf16[4,8,128]{2,1,0:T(8,128)(2,1)} %broadcast_in_dim.42), calls=%async_computation.4 | async-start | bytes 16384 | tf_op jit(solution)/shard_map/all_to_all | solution.py:267
  98.7 4.3 %all-to-all-done.4 = bf16[4,8,128]{2,1,0:T(8,128)(2,1)S(1)} async-done(((bf16[4,8,128]{2,1,0:T(8,128)(2,1)}), bf16[4,8,128]{2,1,0:T(8,128)(2,1)S(1)}, u32[]{:S(2)}, u32[]{:S(2)}) %all-to-all-start.4) | async-done | bytes 8224 | tf_op jit(solution)/shard_map/all_to_all | solution.py:267
  103.0 0.8 copy.73.scale_ref
  103.8 1.9 %all-gather.2.cloned.1.call-done = bf16[6144,512]{1,0:T(8,128)(2,1)} async-done(((bf16[192,512]{1,0:T(8,128)(2,1)}), bf16[6144,512]{1,0:T(8,128)(2,1)}) %all-gather.2.cloned.1.call-update) | async-done | bytes 6291472 | tf_op jit(solution)/shard_map/all_gather | solution.py:217
  105.7 7.1 %project.1 = bf16[4,256,384]{2,1,0:T(8,128)(2,1)} custom-call(s32[1]{0:T(128)} %bitcast.25.at_ref, bf16[4,272,512]{2,1,0:T(8,128)(2,1)} %copy-done.1, bf16[16,2,192,512]{3,2,1,0:T(8,128)(2,1)} %bitcast.83, f32[256,1]{1,0:T(8,128)} %copy.73.scale_ref), custom_call_target="tpu_custom_call" | custom-call | tf_op jit(solution)/shard_map/project/pallas_call | solution.py:109
  112.9 4.0 %all-to-all-start.5 = ((bf16[4,256,384]{2,1,0:T(8,128)(2,1)}), bf16[4,256,384]{2,1,0:T(8,128)(2,1)S(1)}, u32[]{:S(2)}, u32[]{:S(2)}) async-start(bf16[4,256,384]{2,1,0:T(8,128)(2,1)} %project.1), calls=%async_computation.5 | async-start | bytes 1572864 | tf_op jit(solution)/shard_map/all_to_all | solution.py:271
  116.9 0.6 dynamic-slice_bitcast_fusion
  117.5 0.8 multiply_convert_fusion
  118.3 8.9 %all-to-all-done.5 = bf16[4,256,384]{2,1,0:T(8,128)(2,1)S(1)} async-done(((bf16[4,256,384]{2,1,0:T(8,128)(2,1)}), bf16[4,256,384]{2,1,0:T(8,128)(2,1)S(1)}, u32[]{:S(2)}, u32[]{:S(2)}) %all-to-all-start.5) | async-done | bytes 786464 | tf_op jit(solution)/shard_map/all_to_all | solution.py:271
  127.2 0.8 reduce_sum.48
  (57 shorter events, 0.8 us)
Async XLA Ops:
  7.2 61.6 %copy-start = (bf16[256,512]{1,0:T(8,128)(2,1)S(1)}, bf16[256,512]{1,0:T(8,128)(2,1)}, u32[]{:S(2)}) copy-start(bf16[256,512]{1,0:T(8,128)(2,1)} %param.7) | copy-start | bytes 786436
  7.2 98.5 %all-gather.2.cloned.1.call-start = ((), (), s32[]{:S(2)}) async-start(), calls=%async_computation.6 | async-start | bytes 6488064 | tf_op jit(solution)/shard_map/all_gather | solution.py:217
  7.2 4.9 %collective-permute-start = (bf16[192,512]{1,0:T(8,128)(2,1)}, bf16[192,512]{1,0:T(8,128)(2,1)S(1)}, u32[]{:S(2)}, u32[]{:S(2)}) collective-permute-start(bf16[192,512]{1,0:T(8,128)(2,1)} %bitcast.101), channel_id=1, source_target_pairs={{0,0},{1,32},{2,64},{3,480},{16,16},{17,48},{18,464},{19,496},{32,... | collective-permute-start | bytes 589832 | tf_op jit(solution)/shard_map/ppermute | solution.py:208
  12.1 0.7 copy-start.4
  12.8 21.2 %all-to-all-start = ((bf16[8,72,128]{2,1,0:T(8,128)(2,1)}), bf16[8,72,128]{2,1,0:T(8,128)(2,1)S(1)}, u32[]{:S(2)}, u32[]{:S(2)}) async-start(bf16[8,72,128]{2,1,0:T(8,128)(2,1)} %get-tuple-element.8), calls=%async_computation | async-start | bytes 294912 | tf_op jit(solution)/shard_map/all_to_all | solution.py:214
  36.0 32.4 %copy-start.2 = (bf16[256,512]{1,0:T(8,128)(2,1)S(1)}, bf16[256,512]{1,0:T(8,128)(2,1)}, u32[]{:S(2)}) copy-start(bf16[256,512]{1,0:T(8,128)(2,1)} %values_ref.1) | copy-start | bytes 786436
  36.0 25.2 %all-to-all-start.1 = ((bf16[4,72,128]{2,1,0:T(8,128)(2,1)}), bf16[4,72,128]{2,1,0:T(8,128)(2,1)S(1)}, u32[]{:S(2)}, u32[]{:S(2)}) async-start(bf16[4,72,128]{2,1,0:T(8,128)(2,1)} %broadcast_in_dim.34), calls=%async_computation.1 | async-start | bytes 147456 | tf_op jit(solution)/shard_map/all_to_all | solution.py:234
  61.5 7.1 %copy-start.5 = (f32[256,4]{1,0:T(8,128)S(1)}, f32[256,4]{1,0:T(8,128)}, u32[]{:S(2)}) copy-start(f32[256,4]{1,0:T(8,128)} %get-tuple-element.9) | copy-start | bytes 12292
  62.0 6.7 %copy-start.3 = (bf16[256,512]{1,0:T(8,128)(2,1)S(1)}, bf16[256,512]{1,0:T(8,128)(2,1)}, u32[]{:S(2)}) copy-start(bf16[256,512]{1,0:T(8,128)(2,1)} %keys_ref.1) | copy-start | bytes 786436
  62.0 6.7 %copy-start.7 = (f32[4,256]{1,0:T(4,128)S(1)}, f32[4,256]{1,0:T(4,128)}, u32[]{:S(2)}) copy-start(f32[4,256]{1,0:T(4,128)} %get-tuple-element.7) | copy-start | bytes 12292
  63.0 12.0 %all-to-all-start.2 = ((bf16[8,64,128]{2,1,0:T(8,128)(2,1)}), bf16[8,64,128]{2,1,0:T(8,128)(2,1)S(1)}, u32[]{:S(2)}, u32[]{:S(2)}) async-start(bf16[8,64,128]{2,1,0:T(8,128)(2,1)} %reshape.201), calls=%async_computation.2 | async-start | bytes 262144 | tf_op jit(solution)/shard_map/all_to_all | solution.py:252
  75.2 0.7 copy-start.6
  93.7 12.0 %copy-start.1 = (bf16[4,272,512]{2,1,0:T(8,128)(2,1)}, bf16[4,272,512]{2,1,0:T(8,128)(2,1)S(1)}, u32[]{:S(2)}) copy-start(bf16[4,272,512]{2,1,0:T(8,128)(2,1)S(1)} %all_to_all.30.acts_ref) | copy-start | bytes 3342340
  94.7 8.3 %all-to-all-start.4 = ((bf16[4,8,128]{2,1,0:T(8,128)(2,1)}), bf16[4,8,128]{2,1,0:T(8,128)(2,1)S(1)}, u32[]{:S(2)}, u32[]{:S(2)}) async-start(bf16[4,8,128]{2,1,0:T(8,128)(2,1)} %broadcast_in_dim.42), calls=%async_computation.4 | async-start | bytes 16384 | tf_op jit(solution)/shard_map/all_to_all | solution.py:267
  112.9 14.3 %all-to-all-start.5 = ((bf16[4,256,384]{2,1,0:T(8,128)(2,1)}), bf16[4,256,384]{2,1,0:T(8,128)(2,1)S(1)}, u32[]{:S(2)}, u32[]{:S(2)}) async-start(bf16[4,256,384]{2,1,0:T(8,128)(2,1)} %project.1), calls=%async_computation.5 | async-start | bytes 1572864 | tf_op jit(solution)/shard_map/all_to_all | solution.py:271
Sparse Core Ops, SparseCore 0:
  13.0 92.7 all-gather.1

commit v8 on v7

--- a/solution.py
+++ b/solution.py
@@ -56,7 +56,7 @@
     return (0, 1, 2 - 4 * core, -1)[y]
 
 
-def project_kernel(at_ref, acts_ref, weights_ref, scale_ref, out_ref, left, right, done, sems, out_sems):
+def project_kernel(at_ref, acts_ref, weights_ref, scale_ref, out_ref, right, sems):
     tokens = scale_ref.shape[0]
     ny = acts_ref.shape[0]
     chips, cores, share, _ = weights_ref.shape
@@ -65,8 +65,6 @@
     for n in range(chips // ny):
         for i in range(ny):
             group = []
-            if n == 0:
-                group.append(pltpu.make_async_copy(acts_ref.at[i, pl.ds(0, tokens)], left.at[i], sems.at[n, i, cores]))
             for c in range(cores):
                 z = lax.rem(n * ny + y + chips + z_step(i, c), chips)
                 part = right.at[n, i, pl.ds(c * share, share)]
@@ -76,7 +74,6 @@
         for copy in group:
             copy.start()
     m = 0
-    leaving = []
     for n in range(chips // ny):
         total = None
         for i in range(ny):
@@ -87,17 +84,13 @@
                     copy.start()
             m += 1
             value = lax.dot_general(
-                left[i],
+                acts_ref[i, :tokens, :],
                 right[n, i],
                 (((1,), (1,)), ((), ())),
                 preferred_element_type=F32,
             )
             total = value if total is None else total + value
-        done[n] = (total * scale_ref[...]).astype(BF16)
-        leaving.append(pltpu.make_async_copy(done.at[n], out_ref.at[n], out_sems.at[n]))
-        leaving[-1].start()
-    for copy in leaving:
-        copy.wait()
+        out_ref[n] = (total * scale_ref[...]).astype(BF16)
 
 
 def project(acts, weights, scale, at):
@@ -105,25 +98,22 @@
     rows = scale.shape[0]
     chips, cores, share, _ = weights.shape
     nx, cols = chips // ny, cores * share
-    hbm = pl.BlockSpec(memory_space=pl.ANY)
+    vmem = pl.BlockSpec(memory_space=pltpu.VMEM)
     return pl.pallas_call(
         project_kernel,
-        out_shape=jax.ShapeDtypeStruct((nx, rows, cols), BF16),
+        out_shape=pltpu.VMEM((nx, rows, cols), BF16),
         grid_spec=pltpu.PrefetchScalarGridSpec(
             num_scalar_prefetch=1,
             grid=(),
-            in_specs=[hbm, hbm, pl.BlockSpec(memory_space=pltpu.VMEM)],
-            out_specs=hbm,
+            in_specs=[vmem, pl.BlockSpec(memory_space=pl.ANY), vmem],
+            out_specs=vmem,
             scratch_shapes=[
-                pltpu.VMEM((ny, rows, depth), BF16),
                 pltpu.VMEM((nx, ny, cols, depth), BF16),
-                pltpu.VMEM((nx, rows, cols), BF16),
-                pltpu.SemaphoreType.DMA((nx, ny, cores + 1)),
-                pltpu.SemaphoreType.DMA((nx,)),
+                pltpu.SemaphoreType.DMA((nx, ny, cores)),
             ],
         ),
         name="project",
-    )(at, acts, weights, scale)
+    )(at, pltpu.with_memory_space_constraint(acts, pltpu.VMEM), weights, scale)
 
 
 def open_kernel(quads, keep_ref, keys_ref, values_ref, message_ref, across_ref, down_ref):

time: 137 us -> 137 us (level)
  no operation moved by 1% of the time
where the time goes in v8:
time: 137 us; the launch traced here: 135 us
  starting transfers between devices  42.5 us (31%)
  waiting for transfers between devices  39.7 us (29%)
  blocking collectives  17.6 us (13%)
  between operations  14.4 us (11%)
  Pallas kernels  10.2 us (7%)
  local copies, waits for them, and re-layouts  6.76 us (5%)
  other arithmetic  2.37 us (2%)
  matrix products  1.77 us (1%)
    all_to_all x1, blocking collectives, per_device(): acts = lax.all_to_all(message, 'y', 0, 0, tiled=True)  17.6 us
    all_to_all x1, starting transfers between devices, per_device(): got = lax.all_to_all(opener, INNER, 0, 0, tiled=True)  15.2 us
    all_to_all x1, waiting for transfers between devices, per_device(): lax.all_to_all(jnp.broadcast_to(total[None], (quads,) + total.shape), 'za...  13.1 us
    all_to_all x1, starting transfers between devices, per_device(): lax.all_to_all(jnp.broadcast_to(total[None], (quads,) + total.shape), 'za...  12 us
    all_to_all x1, waiting for transfers between devices, per_device(): lax.all_to_all(project(acts, gathered, scale, at), 'x', 0, 0, tiled=True)  9.37 us
    pallas_call x1, Pallas kernels, project(): pl.pallas_call(project_kernel, out_shape=pltpu.VMEM((nx, rows, cols), BF1...  7.05 us
    all_to_all x1, waiting for transfers between devices, per_device(): back = lax.all_to_all(states, INNER, 0, 0, tiled=True)  5.73 us
    all_to_all x1, starting transfers between devices, per_device(): back = lax.all_to_all(states, INNER, 0, 0, tiled=True)  5.42 us
  transfers between devices with their start and end apart: 7, of which 6 were waited for; matrix products, arithmetic and copies ran while one was open for 7% of the time, Pallas kernels for 2%

profile of v8, /device:TPU:1, one launch (start us, length us, event | category | flops | bytes accessed | tf_op | source)
XLA Modules:
  0.0 135.3 jit_solution(2612859273005154739)
XLA Ops:
  7.2 1.7 %collective-permute-start = (bf16[192,512]{1,0:T(8,128)(2,1)}, bf16[192,512]{1,0:T(8,128)(2,1)S(1)}, u32[]{:S(2)}, u32[]{:S(2)}) collective-permute-start(bf16[192,512]{1,0:T(8,128)(2,1)} %bitcast.101), channel_id=1, source_target_pairs={{0,0},{1,32},{2,64},{3,480},{16,16},{17,48},{18,464},{19,496},{32,... | collective-permute-start | bytes 589832 | tf_op jit(solution)/shard_map/ppermute | solution.py:198
  8.9 3.2 %open_scan.1 = (bf16[8,72,128]{2,1,0:T(8,128)(2,1)}, f32[4,256]{1,0:T(4,128)}, f32[256,4]{1,0:T(8,128)}) custom-call(f32[4,256]{1,0:T(4,128)} %keep_ref.1, bf16[256,512]{1,0:T(8,128)(2,1)} %keys_ref.1, bf16[256,512]{1,0:T(8,128)(2,1)} %values_ref.1), custom_call_target="tpu_custom_call" | custom-call | tf_op jit(solution)/shard_map/open_scan/pallas_call | solution.py:165
  12.1 0.7 copy-done.3
  12.8 15.2 %all-to-all-start = ((bf16[8,72,128]{2,1,0:T(8,128)(2,1)}), bf16[8,72,128]{2,1,0:T(8,128)(2,1)S(1)}, u32[]{:S(2)}, u32[]{:S(2)}) async-start(bf16[8,72,128]{2,1,0:T(8,128)(2,1)} %get-tuple-element.8), calls=%async_computation | async-start | bytes 294912 | tf_op jit(solution)/shard_map/all_to_all | solution.py:204
  28.1 0.8 constant_dynamic-slice_fusion.1
  28.9 5.2 %all-to-all-done = bf16[8,72,128]{2,1,0:T(8,128)(2,1)S(1)} async-done(((bf16[8,72,128]{2,1,0:T(8,128)(2,1)}), bf16[8,72,128]{2,1,0:T(8,128)(2,1)S(1)}, u32[]{:S(2)}, u32[]{:S(2)}) %all-to-all-start) | async-done | bytes 147488 | tf_op jit(solution)/shard_map/all_to_all | solution.py:204
  34.1 0.1 copy.58
  34.2 0.2 reduce_window_sum.22
  34.4 0.1 concatenate.12
  34.4 0.1 reduce-precision_convert_fusion.1
  34.5 0.1 pad_maximum_fusion.3
  34.6 0.1 copy.77
  34.7 0.5 convolution_bitcast_fusion
  35.2 0.1 fusion.26
  35.3 0.6 broadcast_in_dim.34
  36.0 12.0 %all-to-all-start.1 = ((bf16[4,72,128]{2,1,0:T(8,128)(2,1)}), bf16[4,72,128]{2,1,0:T(8,128)(2,1)S(1)}, u32[]{:S(2)}, u32[]{:S(2)}) async-start(bf16[4,72,128]{2,1,0:T(8,128)(2,1)} %broadcast_in_dim.34), calls=%async_computation.1 | async-start | bytes 147456 | tf_op jit(solution)/shard_map/all_to_all | solution.py:224
  48.0 0.1 slice_exponential_fusion
  48.1 13.1 %all-to-all-done.1 = bf16[4,72,128]{2,1,0:T(8,128)(2,1)S(1)} async-done(((bf16[4,72,128]{2,1,0:T(8,128)(2,1)}), bf16[4,72,128]{2,1,0:T(8,128)(2,1)S(1)}, u32[]{:S(2)}, u32[]{:S(2)}) %all-to-all-start.1) | async-done | bytes 73760 | tf_op jit(solution)/shard_map/all_to_all | solution.py:224
  61.2 0.1 copy.62
  61.3 0.1 copy.64
  61.4 0.1 concatenate.14.clone
  61.5 0.4 fusion
  61.9 0.1 fusion.56
  62.1 0.1 fusion.19
  62.2 0.1 copy.65
  62.3 0.7 reshape.201
  63.0 5.4 %all-to-all-start.2 = ((bf16[8,64,128]{2,1,0:T(8,128)(2,1)}), bf16[8,64,128]{2,1,0:T(8,128)(2,1)S(1)}, u32[]{:S(2)}, u32[]{:S(2)}) async-start(bf16[8,64,128]{2,1,0:T(8,128)(2,1)} %reshape.201), calls=%async_computation.2 | async-start | bytes 262144 | tf_op jit(solution)/shard_map/all_to_all | solution.py:242
  68.4 0.1 copy.75
  68.6 0.1 copy.70
  68.8 0.6 convolution_bitcast_fusion.3
  69.3 5.7 %all-to-all-done.2 = bf16[8,64,128]{2,1,0:T(8,128)(2,1)S(1)} async-done(((bf16[8,64,128]{2,1,0:T(8,128)(2,1)}), bf16[8,64,128]{2,1,0:T(8,128)(2,1)S(1)}, u32[]{:S(2)}, u32[]{:S(2)}) %all-to-all-start.2) | async-done | bytes 131104 | tf_op jit(solution)/shard_map/all_to_all | solution.py:242
  75.1 0.1 copy.66
  75.2 0.3 multiply_reduce_fusion
  75.5 0.2 copy.72
  75.8 0.1 copy-done.5
  76.0 0.1 broadcast_in_dim.40
  76.1 17.6 %all_to_all.30.acts_ref = bf16[4,272,512]{2,1,0:T(8,128)(2,1)S(1)} all-to-all(bf16[4,272,512]{2,1,0:T(8,128)(2,1)S(1)} %broadcast_in_dim.40), channel_id=1, replica_groups=mesh['za'=4,'zb'=4,'core'=2,'x'=4,'y'=4] {'y'}, dimensions={0} | all-to-all | bytes 2228224 | tf_op jit(solution)/shard_map/all_to_all | solution.py:254
  93.9 0.6 broadcast_in_dim.42
  94.5 4.0 %all-to-all-start.4 = ((bf16[4,8,128]{2,1,0:T(8,128)(2,1)}), bf16[4,8,128]{2,1,0:T(8,128)(2,1)S(1)}, u32[]{:S(2)}, u32[]{:S(2)}) async-start(bf16[4,8,128]{2,1,0:T(8,128)(2,1)} %broadcast_in_dim.42), calls=%async_computation.4 | async-start | bytes 16384 | tf_op jit(solution)/shard_map/all_to_all | solution.py:257
  98.5 4.2 %all-to-all-done.4 = bf16[4,8,128]{2,1,0:T(8,128)(2,1)S(1)} async-done(((bf16[4,8,128]{2,1,0:T(8,128)(2,1)}), bf16[4,8,128]{2,1,0:T(8,128)(2,1)S(1)}, u32[]{:S(2)}, u32[]{:S(2)}) %all-to-all-start.4) | async-done | bytes 8224 | tf_op jit(solution)/shard_map/all_to_all | solution.py:257
  102.7 0.8 copy.73.scale_ref
  103.5 2.2 %all-gather.2.cloned.1.call-done = bf16[6144,512]{1,0:T(8,128)(2,1)} async-done(((bf16[192,512]{1,0:T(8,128)(2,1)}), bf16[6144,512]{1,0:T(8,128)(2,1)}) %all-gather.2.cloned.1.call-update) | async-done | bytes 6291472 | tf_op jit(solution)/shard_map/all_gather | solution.py:207
  105.7 7.0 %project.1 = bf16[4,256,384]{2,1,0:T(8,128)(2,1)} custom-call(s32[1]{0:T(128)} %bitcast.25.at_ref, bf16[4,272,512]{2,1,0:T(8,128)(2,1)S(1)} %all_to_all.30.acts_ref, bf16[16,2,192,512]{3,2,1,0:T(8,128)(2,1)} %bitcast.83, f32[256,1]{1,0:T(8,128)} %copy.73.scale_ref), custom_call_target="tpu_custom_call" | custom-call | tf_op jit(solution)/shard_map/project/pallas_call | solution.py:102
  112.8 4.0 %all-to-all-start.5 = ((bf16[4,256,384]{2,1,0:T(8,128)(2,1)}), bf16[4,256,384]{2,1,0:T(8,128)(2,1)S(1)}, u32[]{:S(2)}, u32[]{:S(2)}) async-start(bf16[4,256,384]{2,1,0:T(8,128)(2,1)} %project.1), calls=%async_computation.5 | async-start | bytes 1572864 | tf_op jit(solution)/shard_map/all_to_all | solution.py:261
  116.8 0.6 dynamic-slice_bitcast_fusion
  117.4 0.8 multiply_convert_fusion
  118.2 9.4 %all-to-all-done.5 = bf16[4,256,384]{2,1,0:T(8,128)(2,1)S(1)} async-done(((bf16[4,256,384]{2,1,0:T(8,128)(2,1)}), bf16[4,256,384]{2,1,0:T(8,128)(2,1)S(1)}, u32[]{:S(2)}, u32[]{:S(2)}) %all-to-all-start.5) | async-done | bytes 786464 | tf_op jit(solution)/shard_map/all_to_all | solution.py:261
  127.6 0.8 reduce_sum.48
  (55 shorter events, 0.8 us)
Async XLA Ops:
  7.2 61.6 %copy-start = (bf16[256,512]{1,0:T(8,128)(2,1)S(1)}, bf16[256,512]{1,0:T(8,128)(2,1)}, u32[]{:S(2)}) copy-start(bf16[256,512]{1,0:T(8,128)(2,1)} %param.7) | copy-start | bytes 786436
  7.2 98.5 %all-gather.2.cloned.1.call-start = ((), (), s32[]{:S(2)}) async-start(), calls=%async_computation.6 | async-start | bytes 6488064 | tf_op jit(solution)/shard_map/all_gather | solution.py:207
  7.2 4.9 %collective-permute-start = (bf16[192,512]{1,0:T(8,128)(2,1)}, bf16[192,512]{1,0:T(8,128)(2,1)S(1)}, u32[]{:S(2)}, u32[]{:S(2)}) collective-permute-start(bf16[192,512]{1,0:T(8,128)(2,1)} %bitcast.101), channel_id=1, source_target_pairs={{0,0},{1,32},{2,64},{3,480},{16,16},{17,48},{18,464},{19,496},{32,... | collective-permute-start | bytes 589832 | tf_op jit(solution)/shard_map/ppermute | solution.py:198
  12.1 0.7 copy-start.3
  12.8 21.2 %all-to-all-start = ((bf16[8,72,128]{2,1,0:T(8,128)(2,1)}), bf16[8,72,128]{2,1,0:T(8,128)(2,1)S(1)}, u32[]{:S(2)}, u32[]{:S(2)}) async-start(bf16[8,72,128]{2,1,0:T(8,128)(2,1)} %get-tuple-element.8), calls=%async_computation | async-start | bytes 294912 | tf_op jit(solution)/shard_map/all_to_all | solution.py:204
  36.0 32.4 %copy-start.1 = (bf16[256,512]{1,0:T(8,128)(2,1)S(1)}, bf16[256,512]{1,0:T(8,128)(2,1)}, u32[]{:S(2)}) copy-start(bf16[256,512]{1,0:T(8,128)(2,1)} %values_ref.1) | copy-start | bytes 786436
  36.0 25.2 %all-to-all-start.1 = ((bf16[4,72,128]{2,1,0:T(8,128)(2,1)}), bf16[4,72,128]{2,1,0:T(8,128)(2,1)S(1)}, u32[]{:S(2)}, u32[]{:S(2)}) async-start(bf16[4,72,128]{2,1,0:T(8,128)(2,1)} %broadcast_in_dim.34), calls=%async_computation.1 | async-start | bytes 147456 | tf_op jit(solution)/shard_map/all_to_all | solution.py:224
  61.5 7.1 %copy-start.4 = (f32[256,4]{1,0:T(8,128)S(1)}, f32[256,4]{1,0:T(8,128)}, u32[]{:S(2)}) copy-start(f32[256,4]{1,0:T(8,128)} %get-tuple-element.9) | copy-start | bytes 12292
  62.0 6.7 %copy-start.2 = (bf16[256,512]{1,0:T(8,128)(2,1)S(1)}, bf16[256,512]{1,0:T(8,128)(2,1)}, u32[]{:S(2)}) copy-start(bf16[256,512]{1,0:T(8,128)(2,1)} %keys_ref.1) | copy-start | bytes 786436
  62.0 6.7 %copy-start.6 = (f32[4,256]{1,0:T(4,128)S(1)}, f32[4,256]{1,0:T(4,128)}, u32[]{:S(2)}) copy-start(f32[4,256]{1,0:T(4,128)} %get-tuple-element.7) | copy-start | bytes 12292
  63.0 12.0 %all-to-all-start.2 = ((bf16[8,64,128]{2,1,0:T(8,128)(2,1)}), bf16[8,64,128]{2,1,0:T(8,128)(2,1)S(1)}, u32[]{:S(2)}, u32[]{:S(2)}) async-start(bf16[8,64,128]{2,1,0:T(8,128)(2,1)} %reshape.201), calls=%async_computation.2 | async-start | bytes 262144 | tf_op jit(solution)/shard_map/all_to_all | solution.py:242
  75.2 0.7 copy-start.5
  94.5 8.2 %all-to-all-start.4 = ((bf16[4,8,128]{2,1,0:T(8,128)(2,1)}), bf16[4,8,128]{2,1,0:T(8,128)(2,1)S(1)}, u32[]{:S(2)}, u32[]{:S(2)}) async-start(bf16[4,8,128]{2,1,0:T(8,128)(2,1)} %broadcast_in_dim.42), calls=%async_computation.4 | async-start | bytes 16384 | tf_op jit(solution)/shard_map/all_to_all | solution.py:257
  112.8 14.8 %all-to-all-start.5 = ((bf16[4,256,384]{2,1,0:T(8,128)(2,1)}), bf16[4,256,384]{2,1,0:T(8,128)(2,1)S(1)}, u32[]{:S(2)}, u32[]{:S(2)}) async-start(bf16[4,256,384]{2,1,0:T(8,128)(2,1)} %project.1), calls=%async_computation.5 | async-start | bytes 1572864 | tf_op jit(solution)/shard_map/all_to_all | solution.py:261
Sparse Core Ops, SparseCore 0:
  13.0 92.7 all-gather.1

commit v9 on v8

--- a/solution.py
+++ b/solution.py
@@ -57,7 +57,7 @@
 
 
 def project_kernel(at_ref, acts_ref, weights_ref, scale_ref, out_ref, right, sems):
-    tokens = scale_ref.shape[0]
+    tokens = scale_ref.shape[1]
     ny = acts_ref.shape[0]
     chips, cores, share, _ = weights_ref.shape
     y = at_ref[0]
@@ -73,6 +73,13 @@
     for group in copies[:FLIGHT]:
         for copy in group:
             copy.start()
+    scale = lax.dot_general(
+        scale_ref[...],
+        jnp.ones((1, out_ref.shape[2]), F32),
+        (((0,), (0,)), ((), ())),
+        precision=HIGH,
+        preferred_element_type=F32,
+    )
     m = 0
     for n in range(chips // ny):
         total = None
@@ -90,12 +97,12 @@
                 preferred_element_type=F32,
             )
             total = value if total is None else total + value
-        out_ref[n] = (total * scale_ref[...]).astype(BF16)
+        out_ref[n] = (total * scale).astype(BF16)
 
 
 def project(acts, weights, scale, at):
     ny, _, depth = acts.shape
-    rows = scale.shape[0]
+    rows = scale.shape[1]
     chips, cores, share, _ = weights.shape
     nx, cols = chips // ny, cores * share
     vmem = pl.BlockSpec(memory_space=pltpu.VMEM)
@@ -215,9 +222,10 @@
     weights = (scores * decay).astype(BF16)
     intra = jnp.einsum("hst,thd->shd", weights, v, preferred_element_type=F32)
 
-    incs = got[:, :slab].astype(F32).reshape(inner, heads, -1)
+    shape = (heads, quads * rows, DH)
+    incs = got[:, :slab].reshape((inner,) + shape).astype(F32)
     upto, mixing = mixer(join3(jnp.moveaxis(got[:, slab : slab + 3, :heads], 1, 0)))
-    local = jnp.einsum("cjh,jhn->chn", mixing, incs, precision=HIGH)
+    local = jnp.sum(mixing[:, :, :, None, None] * incs[None], axis=1)
 
     total_log = jnp.pad(split3(upto[inner]), ((0, 5), (0, DH - heads)))
     total = jnp.concatenate([local[inner].reshape(slab, DH).astype(BF16), total_log])
@@ -227,17 +235,20 @@
     after, across = mixer(join3(jnp.moveaxis(totals[:, slab : slab + 3, :heads], 1, 0)))
     first = lax.dynamic_index_in_dim(
         state_in.reshape(heads, quads, inner, rows, DH), lax.axis_index(INNER), 2, keepdims=False
-    ).reshape(heads, -1)
-    bounds = jnp.einsum(
-        "cjh,jhn->chn", across, totals[:, :slab].reshape(quads, heads, -1), precision=HIGH
-    )
-    bounds = bounds + jnp.exp(after)[:, :, None] * first[None]
+    ).reshape(shape)
     quad = lax.axis_index("za")
+    totals = totals[:, :slab].reshape((quads,) + shape)
+
+    def bound(c):
+        weigh = lax.dynamic_index_in_dim(across, c, 0, keepdims=False)[:, :, None, None]
+        carried = jnp.exp(lax.dynamic_index_in_dim(after, c, 0, keepdims=False))[:, None, None]
+        return jnp.sum(weigh * totals, axis=0) + carried * first
+
+    opening = bound(quad)
     final = lax.dynamic_index_in_dim(
-        bounds[quads].reshape(heads, quads, rows, DH), quad, 1, keepdims=False
-    )
-    opening = lax.dynamic_index_in_dim(bounds, quad, 0, keepdims=False)
-    states = local[:inner] + jnp.exp(upto[:inner])[:, :, None] * opening[None]
+        bound(quads).reshape(heads, quads, rows, DH), quad, 1, keepdims=False
+    )
+    states = local[:inner] + jnp.exp(upto[:inner])[:, :, None, None] * opening[None]
     states = states.astype(BF16).reshape(inner, slab, DH)
     back = lax.all_to_all(states, INNER, 0, 0, tiled=True)
     start = back.reshape(inner, heads, quads, rows, DH).transpose(1, 2, 0, 3, 4)
@@ -255,10 +266,10 @@
     squares = rows_of(acts[:, tokens:], tokens)
     mine = tail_of(squares, 8, DH)
     each = lax.all_to_all(jnp.broadcast_to(mine[None], (nx,) + mine.shape), "x", 0, 0, tiled=True)
-    scale = lax.rsqrt(rows_of(each, tokens) / (H * DH) + EPSILON)[:, None]
-    normed = (attended * scale * norm_gain).astype(BF16)
+    scale = lax.rsqrt(rows_of(each, tokens) / (H * DH) + EPSILON)
+    normed = (attended * scale[:, None] * norm_gain).astype(BF16)
     at = lax.axis_index("y").astype(jnp.int32).reshape(1)
-    shares = lax.all_to_all(project(acts, gathered, scale, at), "x", 0, 0, tiled=True)
+    shares = lax.all_to_all(project(acts, gathered, scale[None], at), "x", 0, 0, tiled=True)
     layer_out = jnp.sum(shares.astype(F32), axis=0).astype(BF16)
     return (normed, final, layer_out)
 

time: 137 us -> 139 us (1.015)
  other arithmetic: 2.37 us -> 5.03 us
  Pallas kernels: 10.2 us -> 12.1 us
  local copies, waits for them, and re-layouts: 6.76 us -> 5.09 us
    pallas_call x1, Pallas kernels: 7.05 us -> 8.9 us  [project(): pl.pallas_call(project_kernel, out_shape=pltpu.VMEM((nx, rows, cols), BF1...]
where the time goes in v9:
time: 139 us; the launch traced here: 137 us
  starting transfers between devices  41.8 us (30%)
  waiting for transfers between devices  39.1 us (28%)
  blocking collectives  18.4 us (13%)
  between operations  14.4 us (10%)
  Pallas kernels  12.1 us (9%)
  local copies, waits for them, and re-layouts  5.09 us (4%)
  other arithmetic  5.03 us (4%)
    all_to_all x1, blocking collectives, per_device(): acts = lax.all_to_all(message, 'y', 0, 0, tiled=True)  18.4 us
    all_to_all x1, starting transfers between devices, per_device(): got = lax.all_to_all(opener, INNER, 0, 0, tiled=True)  15.2 us
    all_to_all x1, waiting for transfers between devices, per_device(): lax.all_to_all(jnp.broadcast_to(total[None], (quads,) + total.shape), 'za...  13.4 us
    all_to_all x1, starting transfers between devices, per_device(): lax.all_to_all(jnp.broadcast_to(total[None], (quads,) + total.shape), 'za...  11.9 us
    pallas_call x1, Pallas kernels, project(): pl.pallas_call(project_kernel, out_shape=pltpu.VMEM((nx, rows, cols), BF1...  8.9 us
    all_to_all x1, waiting for transfers between devices, per_device(): lax.all_to_all(project(acts, gathered, scale[None], at), 'x', 0, 0, tiled...  8.62 us
    all_to_all x1, waiting for transfers between devices, per_device(): back = lax.all_to_all(states, INNER, 0, 0, tiled=True)  5.52 us
    all_to_all x1, waiting for transfers between devices, per_device(): got = lax.all_to_all(opener, INNER, 0, 0, tiled=True)  5.19 us
  transfers between devices with their start and end apart: 7, of which 6 were waited for; matrix products, arithmetic and copies ran while one was open for 7% of the time, Pallas kernels for 2%

profile of v9, /device:TPU:1, one launch (start us, length us, event | category | flops | bytes accessed | tf_op | source)
XLA Modules:
  0.0 136.7 jit_solution(3525237726849131350)
XLA Ops:
  7.2 1.7 %collective-permute-start = (bf16[192,512]{1,0:T(8,128)(2,1)}, bf16[192,512]{1,0:T(8,128)(2,1)S(1)}, u32[]{:S(2)}, u32[]{:S(2)}) collective-permute-start(bf16[192,512]{1,0:T(8,128)(2,1)} %bitcast.115), channel_id=1, source_target_pairs={{0,0},{1,32},{2,64},{3,480},{16,16},{17,48},{18,464},{19,496},{32,... | collective-permute-start | bytes 589832 | tf_op jit(solution)/shard_map/ppermute | solution.py:205
  9.0 3.2 %open_scan.1 = (bf16[8,72,128]{2,1,0:T(8,128)(2,1)}, f32[4,256]{1,0:T(4,128)}, f32[256,4]{1,0:T(8,128)}) custom-call(f32[4,256]{1,0:T(4,128)} %keep_ref.1, bf16[256,512]{1,0:T(8,128)(2,1)} %keys_ref.1, bf16[256,512]{1,0:T(8,128)(2,1)} %values_ref.1), custom_call_target="tpu_custom_call" | custom-call | tf_op jit(solution)/shard_map/open_scan/pallas_call | solution.py:172
  12.2 0.7 copy-done.3
  12.9 15.2 %all-to-all-start = ((bf16[8,72,128]{2,1,0:T(8,128)(2,1)}), bf16[8,72,128]{2,1,0:T(8,128)(2,1)S(1)}, u32[]{:S(2)}, u32[]{:S(2)}) async-start(bf16[8,72,128]{2,1,0:T(8,128)(2,1)} %get-tuple-element.8), calls=%async_computation | async-start | bytes 294912 | tf_op jit(solution)/shard_map/all_to_all | solution.py:211
  28.1 0.8 constant_dynamic-slice_fusion
  28.8 5.2 %all-to-all-done = bf16[8,72,128]{2,1,0:T(8,128)(2,1)S(1)} async-done(((bf16[8,72,128]{2,1,0:T(8,128)(2,1)}), bf16[8,72,128]{2,1,0:T(8,128)(2,1)S(1)}, u32[]{:S(2)}, u32[]{:S(2)}) %all-to-all-start) | async-done | bytes 147488 | tf_op jit(solution)/shard_map/all_to_all | solution.py:211
  34.1 0.1 copy.74
  34.1 0.2 reduce_window_sum.22
  34.3 0.1 copy.76
  34.4 0.1 reduce-precision_convert_fusion.1
  34.5 0.1 pad_maximum_fusion.3
  34.6 0.1 copy.90
  34.7 0.1 exponential_select_fusion
  34.8 0.4 multiply_reduce_fusion
  35.2 0.6 broadcast_in_dim.35
  35.8 11.9 %all-to-all-start.1 = ((bf16[4,72,128]{2,1,0:T(8,128)(2,1)}), bf16[4,72,128]{2,1,0:T(8,128)(2,1)S(1)}, u32[]{:S(2)}, u32[]{:S(2)}) async-start(bf16[4,72,128]{2,1,0:T(8,128)(2,1)} %broadcast_in_dim.35), calls=%async_computation.1 | async-start | bytes 147456 | tf_op jit(solution)/shard_map/all_to_all | solution.py:232
  47.7 0.1 slice_exponential_fusion
  47.8 0.1 copy.77
  47.9 13.4 %all-to-all-done.1 = bf16[4,72,128]{2,1,0:T(8,128)(2,1)S(1)} async-done(((bf16[4,72,128]{2,1,0:T(8,128)(2,1)}), bf16[4,72,128]{2,1,0:T(8,128)(2,1)S(1)}, u32[]{:S(2)}, u32[]{:S(2)}) %all-to-all-start.1) | async-done | bytes 73760 | tf_op jit(solution)/shard_map/all_to_all | solution.py:232
  61.3 0.1 exponential_select_fusion.1
  61.4 0.1 mul.141
  61.5 0.1 mul.142
  61.7 0.1 mul.124
  61.7 0.1 multiply_reduce_fusion.2
  61.9 0.1 multiply_add_fusion
  62.0 0.8 fusion.18
  62.8 5.0 %all-to-all-start.2 = ((bf16[8,64,128]{2,1,0:T(8,128)(2,1)}), bf16[8,64,128]{2,1,0:T(8,128)(2,1)S(1)}, u32[]{:S(2)}, u32[]{:S(2)}) async-start(bf16[8,64,128]{2,1,0:T(8,128)(2,1)} %bitcast.13), calls=%async_computation.2 | async-start | bytes 262144 | tf_op jit(solution)/shard_map/all_to_all | solution.py:253
  67.8 0.1 copy.88
  68.0 0.1 copy.84
  68.1 0.6 convolution_bitcast_fusion.1
  68.7 5.5 %all-to-all-done.2 = bf16[8,64,128]{2,1,0:T(8,128)(2,1)S(1)} async-done(((bf16[8,64,128]{2,1,0:T(8,128)(2,1)}), bf16[8,64,128]{2,1,0:T(8,128)(2,1)S(1)}, u32[]{:S(2)}, u32[]{:S(2)}) %all-to-all-start.2) | async-done | bytes 131104 | tf_op jit(solution)/shard_map/all_to_all | solution.py:253
  74.2 0.1 copy.80
  74.4 0.3 multiply_reduce_fusion.1
  74.7 0.2 copy.86
  75.1 0.1 broadcast_in_dim.36
  75.1 18.4 %all_to_all.30.acts_ref = bf16[4,272,512]{2,1,0:T(8,128)(2,1)S(1)} all-to-all(bf16[4,272,512]{2,1,0:T(8,128)(2,1)S(1)} %broadcast_in_dim.36), channel_id=1, replica_groups=mesh['za'=4,'zb'=4,'core'=2,'x'=4,'y'=4] {'y'}, dimensions={0} | all-to-all | bytes 2228224 | tf_op jit(solution)/shard_map/all_to_all | solution.py:265
  93.7 0.6 broadcast_in_dim.42
  94.3 4.3 %all-to-all-start.4 = ((bf16[4,8,128]{2,1,0:T(8,128)(2,1)}), bf16[4,8,128]{2,1,0:T(8,128)(2,1)S(1)}, u32[]{:S(2)}, u32[]{:S(2)}) async-start(bf16[4,8,128]{2,1,0:T(8,128)(2,1)} %broadcast_in_dim.42), calls=%async_computation.4 | async-start | bytes 16384 | tf_op jit(solution)/shard_map/all_to_all | solution.py:268
  98.6 4.2 %all-to-all-done.4 = bf16[4,8,128]{2,1,0:T(8,128)(2,1)S(1)} async-done(((bf16[4,8,128]{2,1,0:T(8,128)(2,1)}), bf16[4,8,128]{2,1,0:T(8,128)(2,1)S(1)}, u32[]{:S(2)}, u32[]{:S(2)}) %all-to-all-start.4) | async-done | bytes 8224 | tf_op jit(solution)/shard_map/all_to_all | solution.py:268
  102.8 0.6 add_rsqrt_fusion
  103.4 2.2 %all-gather.2.cloned.1.call-done = bf16[6144,512]{1,0:T(8,128)(2,1)} async-done(((bf16[192,512]{1,0:T(8,128)(2,1)}), bf16[6144,512]{1,0:T(8,128)(2,1)}) %all-gather.2.cloned.1.call-update) | async-done | bytes 6291472 | tf_op jit(solution)/shard_map/all_gather | solution.py:214
  105.5 8.9 %project.1 = bf16[4,256,384]{2,1,0:T(8,128)(2,1)} custom-call(s32[1]{0:T(128)} %bitcast.33.at_ref, bf16[4,272,512]{2,1,0:T(8,128)(2,1)S(1)} %all_to_all.30.acts_ref, bf16[16,2,192,512]{3,2,1,0:T(8,128)(2,1)} %bitcast.94, f32[1,256]{1,0:T(1,128)} %bitcast.110), custom_call_target="tpu_custom_call" | custom-call | tf_op jit(solution)/shard_map/project/pallas_call | solution.py:109
  114.5 3.7 %all-to-all-start.5 = ((bf16[4,256,384]{2,1,0:T(8,128)(2,1)}), bf16[4,256,384]{2,1,0:T(8,128)(2,1)S(1)}, u32[]{:S(2)}, u32[]{:S(2)}) async-start(bf16[4,256,384]{2,1,0:T(8,128)(2,1)} %project.1), calls=%async_computation.5 | async-start | bytes 1572864 | tf_op jit(solution)/shard_map/all_to_all | solution.py:272
  118.1 0.8 fusion.39
  118.9 0.7 fusion.24
  119.6 0.8 multiply_convert_fusion
  120.4 8.6 %all-to-all-done.5 = bf16[4,256,384]{2,1,0:T(8,128)(2,1)S(1)} async-done(((bf16[4,256,384]{2,1,0:T(8,128)(2,1)}), bf16[4,256,384]{2,1,0:T(8,128)(2,1)S(1)}, u32[]{:S(2)}, u32[]{:S(2)}) %all-to-all-start.5) | async-done | bytes 786464 | tf_op jit(solution)/shard_map/all_to_all | solution.py:272
  129.0 0.8 reduce_sum.84
  (57 shorter events, 0.8 us)
Async XLA Ops:
  7.2 60.9 %copy-start = (bf16[256,512]{1,0:T(8,128)(2,1)S(1)}, bf16[256,512]{1,0:T(8,128)(2,1)}, u32[]{:S(2)}) copy-start(bf16[256,512]{1,0:T(8,128)(2,1)} %param.7) | copy-start | bytes 786436
  7.2 60.6 %copy-start.1 = (bf16[256,512]{1,0:T(8,128)(2,1)S(1)}, bf16[256,512]{1,0:T(8,128)(2,1)}, u32[]{:S(2)}) copy-start(bf16[256,512]{1,0:T(8,128)(2,1)} %values_ref.1) | copy-start | bytes 786436
  7.2 98.4 %all-gather.2.cloned.1.call-start = ((), (), s32[]{:S(2)}) async-start(), calls=%async_computation.6 | async-start | bytes 6488064 | tf_op jit(solution)/shard_map/all_gather | solution.py:214
  7.2 60.8 %copy-start.2 = (bf16[256,512]{1,0:T(8,128)(2,1)S(1)}, bf16[256,512]{1,0:T(8,128)(2,1)}, u32[]{:S(2)}) copy-start(bf16[256,512]{1,0:T(8,128)(2,1)} %keys_ref.1) | copy-start | bytes 786436
  7.2 4.9 %collective-permute-start = (bf16[192,512]{1,0:T(8,128)(2,1)}, bf16[192,512]{1,0:T(8,128)(2,1)S(1)}, u32[]{:S(2)}, u32[]{:S(2)}) collective-permute-start(bf16[192,512]{1,0:T(8,128)(2,1)} %bitcast.115), channel_id=1, source_target_pairs={{0,0},{1,32},{2,64},{3,480},{16,16},{17,48},{18,464},{19,496},{32,... | collective-permute-start | bytes 589832 | tf_op jit(solution)/shard_map/ppermute | solution.py:205
  12.1 55.8 %copy-start.4 = (f32[256,4]{1,0:T(8,128)S(1)}, f32[256,4]{1,0:T(8,128)}, u32[]{:S(2)}) copy-start(f32[256,4]{1,0:T(8,128)} %get-tuple-element.9) | copy-start | bytes 12292
  12.1 55.9 %copy-start.7 = (f32[4,256]{1,0:T(4,128)S(1)}, f32[4,256]{1,0:T(4,128)}, u32[]{:S(2)}) copy-start(f32[4,256]{1,0:T(4,128)} %get-tuple-element.7) | copy-start | bytes 12292
  12.2 0.7 copy-start.3
  12.9 21.2 %all-to-all-start = ((bf16[8,72,128]{2,1,0:T(8,128)(2,1)}), bf16[8,72,128]{2,1,0:T(8,128)(2,1)S(1)}, u32[]{:S(2)}, u32[]{:S(2)}) async-start(bf16[8,72,128]{2,1,0:T(8,128)(2,1)} %get-tuple-element.8), calls=%async_computation | async-start | bytes 294912 | tf_op jit(solution)/shard_map/all_to_all | solution.py:211
  35.8 25.4 %all-to-all-start.1 = ((bf16[4,72,128]{2,1,0:T(8,128)(2,1)}), bf16[4,72,128]{2,1,0:T(8,128)(2,1)S(1)}, u32[]{:S(2)}, u32[]{:S(2)}) async-start(bf16[4,72,128]{2,1,0:T(8,128)(2,1)} %broadcast_in_dim.35), calls=%async_computation.1 | async-start | bytes 147456 | tf_op jit(solution)/shard_map/all_to_all | solution.py:232
  62.8 11.4 %all-to-all-start.2 = ((bf16[8,64,128]{2,1,0:T(8,128)(2,1)}), bf16[8,64,128]{2,1,0:T(8,128)(2,1)S(1)}, u32[]{:S(2)}, u32[]{:S(2)}) async-start(bf16[8,64,128]{2,1,0:T(8,128)(2,1)} %bitcast.13), calls=%async_computation.2 | async-start | bytes 262144 | tf_op jit(solution)/shard_map/all_to_all | solution.py:253
  68.1 6.9 %copy-start.6 = (f32[512]{0:T(512)S(1)}, f32[512]{0:T(512)}, u32[]{:S(2)}) copy-start(f32[512]{0:T(512)} %param.12) | copy-start | bytes 6148
  94.3 8.4 %all-to-all-start.4 = ((bf16[4,8,128]{2,1,0:T(8,128)(2,1)}), bf16[4,8,128]{2,1,0:T(8,128)(2,1)S(1)}, u32[]{:S(2)}, u32[]{:S(2)}) async-start(bf16[4,8,128]{2,1,0:T(8,128)(2,1)} %broadcast_in_dim.42), calls=%async_computation.4 | async-start | bytes 16384 | tf_op jit(solution)/shard_map/all_to_all | solution.py:268
  105.5 14.0 %copy-start.5 = (f32[256]{0:T(256)S(1)}, f32[256]{0:T(256)}, u32[]{:S(2)}) copy-start(f32[256]{0:T(256)} %add_rsqrt_fusion) | copy-start | bytes 3076
  114.5 14.5 %all-to-all-start.5 = ((bf16[4,256,384]{2,1,0:T(8,128)(2,1)}), bf16[4,256,384]{2,1,0:T(8,128)(2,1)S(1)}, u32[]{:S(2)}, u32[]{:S(2)}) async-start(bf16[4,256,384]{2,1,0:T(8,128)(2,1)} %project.1), calls=%async_computation.5 | async-start | bytes 1572864 | tf_op jit(solution)/shard_map/all_to_all | solution.py:272
Sparse Core Ops, SparseCore 0:
  13.0 92.5 all-gather.1

commit v10 on v9

--- a/solution.py
+++ b/solution.py
@@ -57,7 +57,7 @@
 
 
 def project_kernel(at_ref, acts_ref, weights_ref, scale_ref, out_ref, right, sems):
-    tokens = scale_ref.shape[1]
+    tokens = scale_ref.shape[0]
     ny = acts_ref.shape[0]
     chips, cores, share, _ = weights_ref.shape
     y = at_ref[0]
@@ -73,13 +73,6 @@
     for group in copies[:FLIGHT]:
         for copy in group:
             copy.start()
-    scale = lax.dot_general(
-        scale_ref[...],
-        jnp.ones((1, out_ref.shape[2]), F32),
-        (((0,), (0,)), ((), ())),
-        precision=HIGH,
-        preferred_element_type=F32,
-    )
     m = 0
     for n in range(chips // ny):
         total = None
@@ -97,12 +90,12 @@
                 preferred_element_type=F32,
             )
             total = value if total is None else total + value
-        out_ref[n] = (total * scale).astype(BF16)
+        out_ref[n] = (total * scale_ref[...]).astype(BF16)
 
 
 def project(acts, weights, scale, at):
     ny, _, depth = acts.shape
-    rows = scale.shape[1]
+    rows = scale.shape[0]
     chips, cores, share, _ = weights.shape
     nx, cols = chips // ny, cores * share
     vmem = pl.BlockSpec(memory_space=pltpu.VMEM)
@@ -269,7 +262,7 @@
     scale = lax.rsqrt(rows_of(each, tokens) / (H * DH) + EPSILON)
     normed = (attended * scale[:, None] * norm_gain).astype(BF16)
     at = lax.axis_index("y").astype(jnp.int32).reshape(1)
-    shares = lax.all_to_all(project(acts, gathered, scale[None], at), "x", 0, 0, tiled=True)
+    shares = lax.all_to_all(project(acts, gathered, scale[:, None], at), "x", 0, 0, tiled=True)
     layer_out = jnp.sum(shares.astype(F32), axis=0).astype(BF16)
     return (normed, final, layer_out)
 

time: 139 us -> 137 us (0.986)
  the two profiles are of different devices: /device:TPU:1 before, /device:TPU:24 now
where the time goes in v10:
time: 137 us; the launch traced here: 136 us
  waiting for transfers between devices  45.5 us (33%)
  starting transfers between devices  37.5 us (27%)
  blocking collectives  17.4 us (13%)
  between operations  14.4 us (11%)
  Pallas kernels  10.2 us (7%)
  local copies, waits for them, and re-layouts  5.89 us (4%)
  other arithmetic  4.47 us (3%)
    all_to_all x1, blocking collectives, per_device(): acts = lax.all_to_all(message, 'y', 0, 0, tiled=True)  17.4 us
    all_to_all x1, waiting for transfers between devices, per_device(): lax.all_to_all(jnp.broadcast_to(total[None], (quads,) + total.shape), 'za...  13.8 us
    ppermute x1, starting transfers between devices, per_device(): moved = lax.ppermute(out_weight.T, CTX + ('y',), swap)  11.2 us
    all_to_all x1, waiting for transfers between devices, per_device(): lax.all_to_all(project(acts, gathered, scale[:, None], at), 'x', 0, 0, ti...  10.4 us
    all_to_all x1, starting transfers between devices, per_device(): lax.all_to_all(jnp.broadcast_to(total[None], (quads,) + total.shape), 'za...  10.3 us
    pallas_call x1, Pallas kernels, project(): pl.pallas_call(project_kernel, out_shape=pltpu.VMEM((nx, rows, cols), BF1...  7.04 us
    all_to_all x1, waiting for transfers between devices, per_device(): back = lax.all_to_all(states, INNER, 0, 0, tiled=True)  6.99 us
    all_to_all x1, waiting for transfers between devices, per_device(): got = lax.all_to_all(opener, INNER, 0, 0, tiled=True)  6.11 us
  transfers between devices with their start and end apart: 7, of which 6 were waited for; matrix products, arithmetic and copies ran while one was open for 7% of the time, Pallas kernels for 2%

profile of v10, /device:TPU:24, one launch (start us, length us, event | category | flops | bytes accessed | tf_op | source)
XLA Modules:
  0.0 136.3 jit_solution(18292790623250388540)
XLA Ops:
  7.2 11.2 %collective-permute-start = (bf16[192,512]{1,0:T(8,128)(2,1)}, bf16[192,512]{1,0:T(8,128)(2,1)S(1)}, u32[]{:S(2)}, u32[]{:S(2)}) collective-permute-start(bf16[192,512]{1,0:T(8,128)(2,1)} %bitcast.115), channel_id=1, source_target_pairs={{0,0},{1,32},{2,64},{3,480},{16,16},{17,48},{18,464},{19,496},{32,... | collective-permute-start | bytes 589832 | tf_op jit(solution)/shard_map/ppermute | solution.py:198
  18.4 3.2 %open_scan.1 = (bf16[8,72,128]{2,1,0:T(8,128)(2,1)}, f32[4,256]{1,0:T(4,128)}, f32[256,4]{1,0:T(8,128)}) custom-call(f32[4,256]{1,0:T(4,128)} %keep_ref.1, bf16[256,512]{1,0:T(8,128)(2,1)} %keys_ref.1, bf16[256,512]{1,0:T(8,128)(2,1)} %values_ref.1), custom_call_target="tpu_custom_call" | custom-call | tf_op jit(solution)/shard_map/open_scan/pallas_call | solution.py:165
  21.6 2.9 %collective-permute-done = bf16[192,512]{1,0:T(8,128)(2,1)S(1)} collective-permute-done((bf16[192,512]{1,0:T(8,128)(2,1)}, bf16[192,512]{1,0:T(8,128)(2,1)S(1)}, u32[]{:S(2)}, u32[]{:S(2)}) %collective-permute-start) | collective-permute-done | bytes 196640 | tf_op jit(solution)/shard_map/ppermute | solution.py:198
  24.6 0.7 copy-done.3
  25.3 3.4 %all-to-all-start = ((bf16[8,72,128]{2,1,0:T(8,128)(2,1)}), bf16[8,72,128]{2,1,0:T(8,128)(2,1)S(1)}, u32[]{:S(2)}, u32[]{:S(2)}) async-start(bf16[8,72,128]{2,1,0:T(8,128)(2,1)} %get-tuple-element.8), calls=%async_computation | async-start | bytes 294912 | tf_op jit(solution)/shard_map/all_to_all | solution.py:204
  28.7 0.8 constant_dynamic-slice_fusion
  29.4 6.1 %all-to-all-done = bf16[8,72,128]{2,1,0:T(8,128)(2,1)S(1)} async-done(((bf16[8,72,128]{2,1,0:T(8,128)(2,1)}), bf16[8,72,128]{2,1,0:T(8,128)(2,1)S(1)}, u32[]{:S(2)}, u32[]{:S(2)}) %all-to-all-start) | async-done | bytes 147488 | tf_op jit(solution)/shard_map/all_to_all | solution.py:204
  35.6 0.1 copy.77
  35.7 0.2 reduce_window_sum.22
  35.8 0.1 copy.79
  35.9 0.1 reduce-precision_convert_fusion.1
  36.0 0.1 pad_maximum_fusion.3
  36.1 0.1 copy.94
  36.2 0.1 exponential_select_fusion
  36.3 0.4 multiply_reduce_fusion
  36.7 0.6 broadcast_in_dim.35
  37.4 10.3 %all-to-all-start.1 = ((bf16[4,72,128]{2,1,0:T(8,128)(2,1)}), bf16[4,72,128]{2,1,0:T(8,128)(2,1)S(1)}, u32[]{:S(2)}, u32[]{:S(2)}) async-start(bf16[4,72,128]{2,1,0:T(8,128)(2,1)} %broadcast_in_dim.35), calls=%async_computation.1 | async-start | bytes 147456 | tf_op jit(solution)/shard_map/all_to_all | solution.py:225
  47.6 0.1 slice_exponential_fusion
  47.7 0.1 copy.80
  47.8 13.8 %all-to-all-done.1 = bf16[4,72,128]{2,1,0:T(8,128)(2,1)S(1)} async-done(((bf16[4,72,128]{2,1,0:T(8,128)(2,1)}), bf16[4,72,128]{2,1,0:T(8,128)(2,1)S(1)}, u32[]{:S(2)}, u32[]{:S(2)}) %all-to-all-start.1) | async-done | bytes 73760 | tf_op jit(solution)/shard_map/all_to_all | solution.py:225
  61.6 0.1 exponential_select_fusion.1
  61.7 0.1 mul.141
  61.8 0.1 mul.142
  62.0 0.1 mul.124
  62.0 0.1 multiply_reduce_fusion.2
  62.2 0.1 multiply_add_fusion
  62.3 0.8 fusion.18
  63.1 3.4 %all-to-all-start.2 = ((bf16[8,64,128]{2,1,0:T(8,128)(2,1)}), bf16[8,64,128]{2,1,0:T(8,128)(2,1)S(1)}, u32[]{:S(2)}, u32[]{:S(2)}) async-start(bf16[8,64,128]{2,1,0:T(8,128)(2,1)} %bitcast.13), calls=%async_computation.2 | async-start | bytes 262144 | tf_op jit(solution)/shard_map/all_to_all | solution.py:246
  66.5 0.1 copy.92
  66.6 0.1 copy.87
  66.8 0.6 convolution_bitcast_fusion.1
  67.4 7.0 %all-to-all-done.2 = bf16[8,64,128]{2,1,0:T(8,128)(2,1)S(1)} async-done(((bf16[8,64,128]{2,1,0:T(8,128)(2,1)}), bf16[8,64,128]{2,1,0:T(8,128)(2,1)S(1)}, u32[]{:S(2)}, u32[]{:S(2)}) %all-to-all-start.2) | async-done | bytes 131104 | tf_op jit(solution)/shard_map/all_to_all | solution.py:246
  74.3 0.1 copy.83
  74.5 0.3 multiply_reduce_fusion.1
  74.8 0.2 copy.89
  75.2 0.1 broadcast_in_dim.36
  75.3 17.4 %all_to_all.30.acts_ref = bf16[4,272,512]{2,1,0:T(8,128)(2,1)S(1)} all-to-all(bf16[4,272,512]{2,1,0:T(8,128)(2,1)S(1)} %broadcast_in_dim.36), channel_id=1, replica_groups=mesh['za'=4,'zb'=4,'core'=2,'x'=4,'y'=4] {'y'}, dimensions={0} | all-to-all | bytes 2228224 | tf_op jit(solution)/shard_map/all_to_all | solution.py:258
  92.8 0.6 broadcast_in_dim.42
  93.4 4.5 %all-to-all-start.4 = ((bf16[4,8,128]{2,1,0:T(8,128)(2,1)}), bf16[4,8,128]{2,1,0:T(8,128)(2,1)S(1)}, u32[]{:S(2)}, u32[]{:S(2)}) async-start(bf16[4,8,128]{2,1,0:T(8,128)(2,1)} %broadcast_in_dim.42), calls=%async_computation.4 | async-start | bytes 16384 | tf_op jit(solution)/shard_map/all_to_all | solution.py:261
  98.0 5.3 %all-to-all-done.4 = bf16[4,8,128]{2,1,0:T(8,128)(2,1)S(1)} async-done(((bf16[4,8,128]{2,1,0:T(8,128)(2,1)}), bf16[4,8,128]{2,1,0:T(8,128)(2,1)S(1)}, u32[]{:S(2)}, u32[]{:S(2)}) %all-to-all-start.4) | async-done | bytes 8224 | tf_op jit(solution)/shard_map/all_to_all | solution.py:261
  103.4 0.8 copy.90.scale_ref
  104.2 7.0 %project.1 = bf16[4,256,384]{2,1,0:T(8,128)(2,1)} custom-call(s32[1]{0:T(128)} %bitcast.33.at_ref, bf16[4,272,512]{2,1,0:T(8,128)(2,1)S(1)} %all_to_all.30.acts_ref, bf16[16,2,192,512]{3,2,1,0:T(8,128)(2,1)} %bitcast.94, f32[256,1]{1,0:T(8,128)} %copy.90.scale_ref), custom_call_target="tpu_custom_call" | custom-call | tf_op jit(solution)/shard_map/project/pallas_call | solution.py:102
  111.2 4.7 %all-to-all-start.5 = ((bf16[4,256,384]{2,1,0:T(8,128)(2,1)}), bf16[4,256,384]{2,1,0:T(8,128)(2,1)S(1)}, u32[]{:S(2)}, u32[]{:S(2)}) async-start(bf16[4,256,384]{2,1,0:T(8,128)(2,1)} %project.1), calls=%async_computation.5 | async-start | bytes 1572864 | tf_op jit(solution)/shard_map/all_to_all | solution.py:265
  115.9 0.8 fusion.39
  116.7 0.7 fusion.24
  117.4 0.8 multiply_convert_fusion
  118.2 10.4 %all-to-all-done.5 = bf16[4,256,384]{2,1,0:T(8,128)(2,1)S(1)} async-done(((bf16[4,256,384]{2,1,0:T(8,128)(2,1)}), bf16[4,256,384]{2,1,0:T(8,128)(2,1)S(1)}, u32[]{:S(2)}, u32[]{:S(2)}) %all-to-all-start.5) | async-done | bytes 786464 | tf_op jit(solution)/shard_map/all_to_all | solution.py:265
  128.6 0.8 reduce_sum.84
  (56 shorter events, 0.8 us)
Async XLA Ops:
  7.2 59.6 %copy-start = (bf16[256,512]{1,0:T(8,128)(2,1)S(1)}, bf16[256,512]{1,0:T(8,128)(2,1)}, u32[]{:S(2)}) copy-start(bf16[256,512]{1,0:T(8,128)(2,1)} %param.7) | copy-start | bytes 786436
  7.2 59.3 %copy-start.1 = (bf16[256,512]{1,0:T(8,128)(2,1)S(1)}, bf16[256,512]{1,0:T(8,128)(2,1)}, u32[]{:S(2)}) copy-start(bf16[256,512]{1,0:T(8,128)(2,1)} %values_ref.1) | copy-start | bytes 786436
  7.2 97.0 %all-gather.2.cloned.1.call-start = ((), (), s32[]{:S(2)}) async-start(), calls=%async_computation.6 | async-start | bytes 6488064 | tf_op jit(solution)/shard_map/all_gather | solution.py:207
  7.2 59.5 %copy-start.2 = (bf16[256,512]{1,0:T(8,128)(2,1)S(1)}, bf16[256,512]{1,0:T(8,128)(2,1)}, u32[]{:S(2)}) copy-start(bf16[256,512]{1,0:T(8,128)(2,1)} %keys_ref.1) | copy-start | bytes 786436
  7.2 17.3 %collective-permute-start = (bf16[192,512]{1,0:T(8,128)(2,1)}, bf16[192,512]{1,0:T(8,128)(2,1)S(1)}, u32[]{:S(2)}, u32[]{:S(2)}) collective-permute-start(bf16[192,512]{1,0:T(8,128)(2,1)} %bitcast.115), channel_id=1, source_target_pairs={{0,0},{1,32},{2,64},{3,480},{16,16},{17,48},{18,464},{19,496},{32,... | collective-permute-start | bytes 589832 | tf_op jit(solution)/shard_map/ppermute | solution.py:198
  21.6 45.0 %copy-start.4 = (f32[256,4]{1,0:T(8,128)S(1)}, f32[256,4]{1,0:T(8,128)}, u32[]{:S(2)}) copy-start(f32[256,4]{1,0:T(8,128)} %get-tuple-element.9) | copy-start | bytes 12292
  21.6 45.1 %copy-start.6 = (f32[4,256]{1,0:T(4,128)S(1)}, f32[4,256]{1,0:T(4,128)}, u32[]{:S(2)}) copy-start(f32[4,256]{1,0:T(4,128)} %get-tuple-element.7) | copy-start | bytes 12292
  24.6 0.7 copy-start.3
  25.3 10.3 %all-to-all-start = ((bf16[8,72,128]{2,1,0:T(8,128)(2,1)}), bf16[8,72,128]{2,1,0:T(8,128)(2,1)S(1)}, u32[]{:S(2)}, u32[]{:S(2)}) async-start(bf16[8,72,128]{2,1,0:T(8,128)(2,1)} %get-tuple-element.8), calls=%async_computation | async-start | bytes 294912 | tf_op jit(solution)/shard_map/all_to_all | solution.py:204
  37.4 24.2 %all-to-all-start.1 = ((bf16[4,72,128]{2,1,0:T(8,128)(2,1)}), bf16[4,72,128]{2,1,0:T(8,128)(2,1)S(1)}, u32[]{:S(2)}, u32[]{:S(2)}) async-start(bf16[4,72,128]{2,1,0:T(8,128)(2,1)} %broadcast_in_dim.35), calls=%async_computation.1 | async-start | bytes 147456 | tf_op jit(solution)/shard_map/all_to_all | solution.py:225
  63.1 11.3 %all-to-all-start.2 = ((bf16[8,64,128]{2,1,0:T(8,128)(2,1)}), bf16[8,64,128]{2,1,0:T(8,128)(2,1)S(1)}, u32[]{:S(2)}, u32[]{:S(2)}) async-start(bf16[8,64,128]{2,1,0:T(8,128)(2,1)} %bitcast.13), calls=%async_computation.2 | async-start | bytes 262144 | tf_op jit(solution)/shard_map/all_to_all | solution.py:246
  66.8 8.3 %copy-start.5 = (f32[512]{0:T(512)S(1)}, f32[512]{0:T(512)}, u32[]{:S(2)}) copy-start(f32[512]{0:T(512)} %param.12) | copy-start | bytes 6148
  93.4 9.9 %all-to-all-start.4 = ((bf16[4,8,128]{2,1,0:T(8,128)(2,1)}), bf16[4,8,128]{2,1,0:T(8,128)(2,1)S(1)}, u32[]{:S(2)}, u32[]{:S(2)}) async-start(bf16[4,8,128]{2,1,0:T(8,128)(2,1)} %broadcast_in_dim.42), calls=%async_computation.4 | async-start | bytes 16384 | tf_op jit(solution)/shard_map/all_to_all | solution.py:261
  111.2 17.4 %all-to-all-start.5 = ((bf16[4,256,384]{2,1,0:T(8,128)(2,1)}), bf16[4,256,384]{2,1,0:T(8,128)(2,1)S(1)}, u32[]{:S(2)}, u32[]{:S(2)}) async-start(bf16[4,256,384]{2,1,0:T(8,128)(2,1)} %project.1), calls=%async_computation.5 | async-start | bytes 1572864 | tf_op jit(solution)/shard_map/all_to_all | solution.py:265
Sparse Core Ops, SparseCore 0:
  25.4 78.7 all-gather.1
